TPU v7x, 128 devices: a whole 4x4x4 slice. The times are simulated.
128 devices in a mesh: prow: 8 (over y_lo, z), pcol: 16 (over x, y_hi, core).
Axes of the slice: x: 4, y: 4 (y_hi: 2, y_lo: 2; y = y_hi * 2 + y_lo), z: 4, core: 2. Of those that a mesh axis runs over, the one named last changes fastest.
Arguments:
- anc_inverse: float32 [4096, 4096], P('pcol', 'prow')
- pattern_one: int32 [16, 8], replicated, may hold values from 0 to 15, as said below
- parents: int32 [16], replicated, may hold values from 0 to 15, as said below
- low_one: float32 [16, 2048, 256], P('pcol', 'prow'), may hold values from -2 to 2
- pivot_one: float32 [16, 256, 256], P('pcol'), may hold values from -4 to 4
- low_two: float32 [16, 2048, 256], P('pcol', 'prow'), may hold values from -2 to 2
- second_scaled_factor: float32 [16, 256, 256], P('pcol'), may hold values from -2 to 2
- second_pivot_inverse: float32 [16, 256, 256], P('pcol'), may hold values from -4 to 4
Outputs:
- column_one: float32 [16, 4096, 256], P('prow', 'pcol')
- diag_one: float32 [16, 256, 256], P('pcol')
- column_two: float32 [16, 4096, 256], P('prow', 'pcol')
- second_parent_inverse: float32 [16, 256, 256], P('pcol')
- second_diagonal_inverse: float32 [16, 256, 256], P('pcol')
Inputs may be any that keep to these rules, and one draw needn't show every extreme that they name: `pattern_one`: entry r of each row names an ancestor of process row r: it lies in r * 2 to r * 2 + 1; for each r, every ancestor of that range is entry r of exactly 8 rows. `parents`: every first-level supernode is the parent of exactly one second-level supernode.
All inputs are finite; a program needn't handle non-finite values.
Results may differ from a plain program's by a relative error of at most 0.000073.
Values sent between devices are 32-bit elements; how exact they have to be, the bound alone decides.
No kernel may reach another device: no remote copies, remote signals or barrier semaphores. Data moves between devices by JAX's collectives and lax.ppermute only.
A program may use at most 128 MiB of HBM per device.

v0:
```python
import jax
import jax.numpy as jnp
from jax import lax
from jax.sharding import PartitionSpec as P


def in_one_piece(arrays, axis, dim, along):
    widths = [a.shape[along] for a in arrays]
    both = jnp.concatenate(arrays, axis=along)
    result = lax.all_gather(both, axis, axis=dim, tiled=True)
    return tuple(jnp.split(result, [sum(widths[:k]) for k in range(1, len(widths))], axis=along))


def sent_to_all(x, axis):
    copies = jnp.broadcast_to(x, (lax.axis_size(axis), *x.shape))
    return lax.all_to_all(copies, axis, split_axis=0, concat_axis=0, tiled=True)


def over_copies(x, axis):
    return sent_to_all(x, axis).sum(axis=0)


def side_by_side(arrays, axis, dim, along):
    both = jnp.concatenate(arrays, axis=along)
    result, at, outs = (lax.psum_scatter(both, axis, scatter_dimension=dim, tiled=True), 0, [])
    for a in arrays:
        outs.append(lax.slice_in_dim(result, at, at + a.shape[along], axis=along))
        at += a.shape[along]
    return tuple(outs)


def together(arrays, axis):
    line, at, outs = (jnp.concatenate([a.reshape(-1) for a in arrays]), 0, [])
    subtotal = over_copies(line, axis)
    for a in arrays:
        outs.append(subtotal[at : at + a.size].reshape(a.shape))
        at += a.size
    return tuple(outs)


def batched(left, right):
    return jnp.einsum("kab,kbd->kad", left, right, precision=lax.Precision.HIGHEST)


def batched_left_t(left, right):
    return jnp.einsum("kba,kbd->kad", left, right, precision=lax.Precision.HIGHEST)


def pick_rows(hit_mask, count):
    total = hit_mask.shape[0]
    keys = jnp.where(hit_mask, 0, total).astype(jnp.int32) + jnp.arange(total, dtype=jnp.int32)
    chosen_rows = jnp.argsort(keys)[:count]
    valid = jnp.take(hit_mask, chosen_rows, axis=0).astype(jnp.float32)[:, None, None]
    return (chosen_rows, valid)


def body(
    anc_inverse,
    pattern_one,
    parents,
    low_one,
    pivot_one,
    low_two,
    second_scaled_factor,
    second_pivot_inverse,
):
    my_row = lax.axis_index("prow")
    my_col = lax.axis_index("pcol")
    row_count = lax.axis_size("prow")
    col_count = lax.axis_size("pcol")
    per_row_anc = col_count // row_count
    supernode_block_width = pivot_one.shape[1]
    per_col_one = pivot_one.shape[0]
    per_col_two = second_scaled_factor.shape[0]
    owned = anc_inverse.shape[1] // supernode_block_width
    zblocks = anc_inverse.reshape(supernode_block_width, owned, supernode_block_width).transpose(
        1, 0, 2
    )
    lowall = lax.all_gather(low_one, "pcol", axis=0, tiled=True)
    total_one = lowall.shape[0]
    owned_slot_list = lax.dynamic_index_in_dim(pattern_one, my_row, 1, keepdims=False)
    chosen = jnp.take(zblocks, owned_slot_list - my_row * owned, axis=0)
    first_terms = batched(chosen, lowall)
    lowsec, topall = in_one_piece((low_two, second_scaled_factor), "pcol", 0, 1)
    total_two = lowsec.shape[0]
    pattern_two = jnp.take(pattern_one, parents, axis=0)
    my_slots_two = lax.dynamic_index_in_dim(pattern_two, my_row, 1, keepdims=False)
    chosen_two = jnp.take(zblocks, my_slots_two - my_row * owned, axis=0)
    first_full = -lax.psum(first_terms, "prow")
    share = total_two // row_count
    start = my_row * share
    parents_share = lax.dynamic_slice_in_dim(parents, start, share, 0)
    tops_share = lax.dynamic_slice_in_dim(topall, start, share, 0)
    carried = batched(jnp.take(first_full, parents_share, axis=0), tops_share)
    base_terms = batched(chosen_two, lowsec)
    updated = lax.dynamic_slice_in_dim(base_terms, start, share, 0) + carried
    second_terms = lax.dynamic_update_slice_in_dim(base_terms, updated, start, 0)
    second_full = -lax.psum(second_terms, "prow")
    rows_one, valid_one = pick_rows(owned_slot_list == my_col, total_one // per_row_anc)
    pivot_small = valid_one * batched_left_t(
        jnp.take(lowall, rows_one, axis=0), jnp.take(first_full, rows_one, axis=0)
    )
    pivot_terms = jnp.zeros_like(first_full).at[rows_one].add(pivot_small)
    pivot_part = lax.psum_scatter(pivot_terms, "pcol", scatter_dimension=0, tiled=True)
    pivot_sum = over_copies(pivot_part, "prow")
    diag_one = pivot_one - pivot_sum
    count_one = first_full.shape[0] // row_count
    column_one = lax.dynamic_slice_in_dim(first_full, my_row * count_one, count_one, 0)
    second_level_count = second_full.shape[0] // row_count
    column_two = lax.dynamic_slice_in_dim(
        second_full, my_row * second_level_count, second_level_count, 0
    )
    rows_two, valid_two = pick_rows(my_slots_two == my_col, total_two // per_row_anc)
    lows_picked = jnp.take(lowsec, rows_two, axis=0)
    parent_picked = jnp.take(first_full, jnp.take(parents, rows_two, axis=0), axis=0)
    cross_small = valid_two * batched_left_t(parent_picked, lows_picked)
    diag_small = valid_two * batched_left_t(lows_picked, jnp.take(second_full, rows_two, axis=0))
    local_parent = parents - my_col * per_col_one
    own_parent = (local_parent >= 0) & (local_parent < per_col_one)
    rows_own, valid_own = pick_rows(own_parent, per_col_two)
    valid_own = valid_own * (my_row == 0).astype(jnp.float32)
    local_picked = jnp.clip(jnp.take(local_parent, rows_own, axis=0), 0, per_col_one - 1)
    picked = jnp.take(diag_one, local_picked, axis=0)
    own_small = valid_own * batched(picked, jnp.take(topall, rows_own, axis=0))
    cross_terms = (
        jnp.zeros_like(second_full).at[rows_two].add(cross_small).at[rows_own].add(own_small)
    )
    diag_terms = jnp.zeros_like(second_full).at[rows_two].add(diag_small)
    part_cross, part_diag = side_by_side((cross_terms, diag_terms), "pcol", 0, 1)
    sum_cross, sum_diag = together((part_cross, part_diag), "prow")
    second_parent_inverse = -sum_cross
    second_diagonal_inverse = (
        second_pivot_inverse
        - batched_left_t(second_scaled_factor, second_parent_inverse)
        - sum_diag
    )
    return (column_one, diag_one, column_two, second_parent_inverse, second_diagonal_inverse)


def solution(mesh):
    placed = (
        P("pcol", "prow"),
        P(),
        P(),
        P("pcol", "prow", None),
        P("pcol", None, None),
        P("pcol", "prow", None),
        P("pcol", None, None),
        P("pcol", None, None),
    )
    return jax.shard_map(
        body,
        mesh=mesh,
        in_specs=placed,
        out_specs=(
            P("prow", "pcol", None),
            P("pcol", None, None),
            P("prow", "pcol", None),
            P("pcol", None, None),
            P("pcol", None, None),
        ),
        check_vma=False,
    )
```

profile of v0, /device:TPU:1, one launch (start us, length us, event | category | flops | bytes accessed | tf_op | source)
XLA Modules:
  0.0 674.0 jit_solution(4868192869001686954)
XLA Ops:
  13.8 56.2 %all-gather.3.cloned.1.call-done = f32[16,256,256]{2,1,0:T(8,128)} async-done(((f32[1,256,256]{2,1,0:T(8,128)}), f32[16,256,256]{2,1,0:T(8,128)}) %all-gather.3.cloned.1.call-update) | async-done | bytes 4194320 | tf_op jit(solution)/shard_map/all_gather | solution.py:79
  70.0 9.7 %fusion.2 = f32[16,256,256]{2,1,0:T(8,128)} fusion(f32[16,256,256]{2,1,0:T(8,128)} %all-gather.3.cloned.1.call-done, f32[16,256,256]{2,1,0:T(8,128)} %gather_fusion.3, pred[16]{0:T(512)(128)(4,1)S(1)} %compare_and_fusion.4), kind=kOutput, calls=%fused_computation.18 | convolution fusion | flops 3222274048 | bytes 12582928 | tf_op jit(solution)/shard_map/kab,kbd->kad/dot_general | solution.py:42
  88.0 95.9 %all-reduce.3.cloned.1.call-done = f32[16,256,256]{2,1,0:T(8,128)} async-done(((f32[16,256,256]{2,1,0:T(8,128)}), f32[16,256,256]{2,1,0:T(8,128)}) %all-reduce.3.cloned.1.call-update) | async-done | bytes 4194320 | tf_op jit(solution)/shard_map/psum | solution.py:89
  183.9 4.5 neg.15
  188.4 4.2 gather_fusion.6
  192.6 6.1 fusion.17
  201.1 4.4 scatter_fusion
  212.4 46.3 %all-gather.5.cloned.1.call-done = f32[16,512,256]{2,1,0:T(8,128)} async-done(((f32[1,512,256]{2,1,0:T(8,128)}), f32[16,512,256]{2,1,0:T(8,128)}) %all-gather.5.cloned.1.call-update) | async-done | bytes 8388624 | tf_op jit(solution)/shard_map/all_gather | solution.py:10
  258.7 6.4 fusion.67
  267.3 5.6 fusion
  275.4 63.5 %reduce-scatter.3.cloned.1.call-done = f32[1,256,256]{2,1,0:T(8,128)} async-done(((f32[16,256,256]{2,1,0:T(8,128)}), f32[1,256,256]{2,1,0:T(8,128)}) %reduce-scatter.3.cloned.1.call-update) | async-done | bytes 262160 | tf_op jit(solution)/shard_map/reduce_scatter | solution.py:104
  341.5 4.4 all-to-all-start
  360.1 6.7 %fusion.22 = f32[8,256,256]{2,1,0:T(8,128)} fusion(f32[8,256,256]{2,1,0:T(8,128)S(1)} %gather_fusion.10, f32[8,256,256]{2,1,0:T(8,128)} %gather_fusion.9, f32[8]{0:T(128)S(1)} %get-tuple-element.106, pred[8]{0:T(512)(128)(4,1)S(1)} %get-tuple-element.93, pred[8]{0:T(512)(128)(4,1)S(1)} %get-tuple-element.91), kind=kOutput, calls=%fused_computation.34 | convolution fusion | flops 1612185600 | bytes 6291504 | tf_op jit(solution)/shard_map/kba,kbd->kad/dot_general | solution.py:46
  369.3 5.4 scatter_fusion.1
  374.6 90.6 %all-reduce.5.cloned.1.call-done = f32[16,256,256]{2,1,0:T(8,128)} async-done(((f32[16,256,256]{2,1,0:T(8,128)}), f32[16,256,256]{2,1,0:T(8,128)}) %all-reduce.5.cloned.1.call-update) | async-done | bytes 4194320 | tf_op jit(solution)/shard_map/psum | solution.py:98
  465.3 4.5 neg.16
  469.7 4.2 gather_fusion.11
  474.0 6.7 fusion.27
  483.0 4.4 scatter_fusion.2
  492.0 7.4 %pad_maximum_fusion = f32[16,512,256]{2,1,0:T(8,128)} fusion(f32[16,256,256]{2,1,0:T(8,128)} %scatter_fusion.2, f32[16,256,256]{2,1,0:T(8,128)} %fusion.36), kind=kLoop, calls=%fused_computation.15 | loop fusion | flops 2097152 | bytes 16777216 | tf_op jit(solution)/shard_map/concatenate | solution.py:24
  499.4 100.4 %reduce-scatter.5.cloned.1.call-done = f32[1,512,256]{2,1,0:T(8,128)} async-done(((f32[16,512,256]{2,1,0:T(8,128)}), f32[1,512,256]{2,1,0:T(8,128)}) %reduce-scatter.5.cloned.1.call-update) | async-done | bytes 524304 | tf_op jit(solution)/shard_map/reduce_scatter | solution.py:25
  605.3 4.9 all-to-all-start.1
  614.2 44.8 %all-to-all-done.1 = f32[8,1,131072]{2,1,0:T(1,128)} async-done(((f32[8,1,131072]{2,1,0:T(1,128)}), f32[8,1,131072]{2,1,0:T(1,128)}, u32[]{:S(2)}, u32[]{:S(2)}) %all-to-all-start.1) | async-done | bytes 4194336 | tf_op jit(solution)/shard_map/all_to_all | solution.py:16
  658.9 5.2 reduce_sum.22
  (104 shorter events, 65.3 us)
Async XLA Ops:
  7.2 62.9 %all-gather.3.cloned.1.call-start = ((), (), s32[]{:S(2)}) async-start(), calls=%async_computation.4 | async-start | bytes 4456448 | tf_op jit(solution)/shard_map/all_gather | solution.py:79
  7.9 176.0 %all-reduce.3.cloned.1.call-start = ((), (), s32[]{:S(2)}) async-start(), calls=%async_computation.5 | async-start | bytes 8388608 | tf_op jit(solution)/shard_map/psum | solution.py:89
  79.7 0.9 copy-start.6
  79.7 1.0 copy-start.9
  79.8 179.0 %all-gather.5.cloned.1.call-start = ((), (), s32[]{:S(2)}) async-start(), calls=%async_computation.7 | async-start | bytes 8912896 | tf_op jit(solution)/shard_map/all_gather | solution.py:10
  81.6 257.4 %reduce-scatter.3.cloned.1.call-start = ((), (), s32[]{:S(2)}) async-start(), calls=%async_computation.6 | async-start | bytes 4456448 | tf_op jit(solution)/shard_map/reduce_scatter | solution.py:104
  201.1 4.7 copy-start
  205.6 259.7 %all-reduce.5.cloned.1.call-start = ((), (), s32[]{:S(2)}) async-start(), calls=%async_computation.8 | async-start | bytes 8388608 | tf_op jit(solution)/shard_map/psum | solution.py:98
  258.7 7.2 %copy-start.1 = (f32[16,512,256]{2,1,0:T(8,128)S(1)}, f32[16,512,256]{2,1,0:T(8,128)}, u32[]{:S(2)}) copy-start(f32[16,512,256]{2,1,0:T(8,128)} %all-gather.5.cloned.1.call-done) | copy-start | bytes 25165828
  258.7 8.5 %copy-start.2 = (f32[16,256,256]{2,1,0:T(8,128)S(1)}, f32[16,256,256]{2,1,0:T(8,128)}, u32[]{:S(2)}) copy-start(f32[16,256,256]{2,1,0:T(8,128)} %gather_fusion.7) | copy-start | bytes 12582916
  267.2 5.6 copy-start.4
  275.4 76.9 %copy-start.10 = (s32[3]{0:T(128)S(1)}, s32[3]{0:T(128)}, u32[]{:S(2)}) copy-start(s32[3]{0:T(128)} %constant.173.clone.1) | copy-start | bytes 40
  341.5 145.9 %all-to-all-start = ((f32[8,1,256,256]{3,2,1,0:T(8,128)}), f32[8,1,256,256]{3,2,1,0:T(8,128)}, u32[]{:S(2)}, u32[]{:S(2)}) async-start(f32[8,1,256,256]{3,2,1,0:T(8,128)} %broadcast_in_dim.110), calls=%async_computation.1 | async-start | bytes 4194304 | tf_op jit(solution)/shard_map/all_to_all | solution.py:16
  345.9 253.9 %reduce-scatter.5.cloned.1.call-start = ((), (), s32[]{:S(2)}) async-start(), calls=%async_computation.9 | async-start | bytes 8912896 | tf_op jit(solution)/shard_map/reduce_scatter | solution.py:25
  480.7 2.4 copy-start.3
  483.0 6.1 copy-start.7
  489.2 10.2 %copy-start.5 = (f32[1,256,256]{2,1,0:T(8,128)}, f32[1,256,256]{2,1,0:T(8,128)S(1)}, u32[]{:S(2)}) copy-start(f32[1,256,256]{2,1,0:T(8,128)S(1)} %bitcast_subtract_fusion) | copy-start | bytes 786436
  605.3 4.9 copy-start.8
  605.3 53.6 %all-to-all-start.1 = ((f32[8,1,131072]{2,1,0:T(1,128)}), f32[8,1,131072]{2,1,0:T(1,128)}, u32[]{:S(2)}, u32[]{:S(2)}) async-start(f32[8,1,131072]{2,1,0:T(1,128)} %broadcast_in_dim.125), calls=%async_computation.3 | async-start | bytes 8388608 | tf_op jit(solution)/shard_map/all_to_all | solution.py:16
Sparse Core Ops, SparseCore 0:
  10.4 59.5 all-gather.2
  79.9 103.9 all-reduce.2
  186.9 71.8 all-gather.4
  262.6 76.3 reduce-scatter.2
  341.5 123.7 all-reduce.4
  499.6 100.1 reduce-scatter.4
where the time goes:
time: 683 us; the launch traced here: 674 us
  waiting for transfers between devices  498 us (73%)
  local copies, waits for them, and re-layouts  64.3 us (9%)
  other arithmetic  44.5 us (7%)
  matrix products  40.7 us (6%)
  between operations  16.2 us (2%)
  starting transfers between devices  9.71 us (1%)
    reduce_scatter x1, waiting for transfers between devices, side_by_side(): lax.psum_scatter(both, axis, scatter_dimension=dim, tiled=True)  100 us
    psum x1, waiting for transfers between devices, body(): first_full = -lax.psum(first_terms, 'prow')  95.9 us
    psum x1, waiting for transfers between devices, body(): second_full = -lax.psum(second_terms, 'prow')  90.6 us
    reduce_scatter x1, waiting for transfers between devices, body(): lax.psum_scatter(pivot_terms, 'pcol', scatter_dimension=0, tiled=True)  63.5 us
    all_gather x1, waiting for transfers between devices, body(): lowall = lax.all_gather(low_one, 'pcol', axis=0, tiled=True)  56.2 us
    all_gather x1, waiting for transfers between devices, in_one_piece(): result = lax.all_gather(both, axis, axis=dim, tiled=True)  46.3 us
    all_to_all x2, waiting for transfers between devices, sent_to_all(): return lax.all_to_all(copies, axis, split_axis=0, concat_axis=0, tiled=True)  44.8 us
    dot_general x4, matrix products, batched(): jnp.einsum('kab,kbd->kad', left, right, precision=lax.Precision.HIGHEST)  20.6 us
  transfers between devices with their start and end apart: 8, of which 7 were waited for; matrix products, arithmetic and copies ran while one was open for 17% of the time, Pallas kernels for 0%

commit v1 on v0

v1 whole, which is shorter than its diff:
```python
import functools

import jax
import jax.numpy as jnp
from jax import lax
from jax.experimental import pallas as pl
from jax.experimental.pallas import tpu as pltpu
from jax.sharding import Mesh, PartitionSpec as P

ROWS, CHIPS, CORES = "prow", "chip", "core"


def split(x):
    high = x.astype(jnp.bfloat16)
    return high, (x - high.astype(jnp.float32)).astype(jnp.bfloat16)


def product(a, b, a_dim=1, b_dim=0):
    dims = (((a_dim,), (b_dim,)), ((), ()))
    dot = functools.partial(lax.dot_general, dimension_numbers=dims, preferred_element_type=jnp.float32)
    (ah, al), (bh, bl) = split(a), split(b)
    return dot(ah, bh) + (dot(ah, bl) + dot(al, bh))


def kernel(info, own, other, low, low_here, factor, pivot, keep, give, parts, total):
    r = pl.program_id(0)
    width = own.shape[-1]

    @pl.when(r == 0)
    def _():
        total[...] = jnp.zeros_like(total)

    def blocks(ref):
        piece = ref.shape[1] // 2
        one = ref[:, :piece, :].reshape(width, width)
        return one, ref[:, piece:, :].reshape(width, width)

    left = jnp.concatenate([own[0], other[0]], axis=0)
    right = jnp.concatenate(blocks(low), axis=1)
    total[...] += product(left, right)

    @pl.when(r == pl.num_programs(0) - 1)
    def _():
        upper = factor[...].reshape(width, width)
        one = total[:, :width]
        two = product(one, upper) - total[:, width:]
        keep[0] = -one[:width]
        give[0] = -one[width:]
        keep[1] = two[:width]
        give[1] = two[width:]
        second = info[8] > 0
        slot_one = jnp.where(second, give[0], keep[0])
        slot_two = jnp.where(second, give[1], keep[1])
        low_one, low_two = blocks(low_here)
        here = jnp.where(info[9] > 0, pivot[0], jnp.zeros_like(slot_one))
        diag = here - product(low_one, slot_one, 0, 0)
        cross = product(diag, upper) + product(slot_one, low_two, 0, 0)
        last = product(upper, cross, 0, 0) - product(low_two, slot_two, 0, 0)
        pieces, tall = parts.shape[0], parts.shape[1] // 3
        for n, term in enumerate((diag, cross, last)):
            parts[:, n * tall : (n + 1) * tall, :] = term.reshape(pieces, tall, width)


def level_blocks(info, gathered, other, low, pivot, rows):
    width = pivot.shape[-1]
    slots = other.shape[0]
    cols, piece = low.shape[0], width // low.shape[0]
    pieces = slots
    f32 = jnp.float32
    grid_spec = pltpu.PrefetchScalarGridSpec(
        num_scalar_prefetch=1,
        grid=(slots,),
        in_specs=[
            pl.BlockSpec((1, width, width), lambda r, s: (r, 0, s[r])),
            pl.BlockSpec((1, width, width), lambda r, s: (r, 0, 0)),
            pl.BlockSpec((cols, 2 * piece, width), lambda r, s: (0, r, 0)),
            pl.BlockSpec((cols, 2 * piece, width), lambda r, s: (0, s[10], 0)),
            pl.BlockSpec((cols, piece, width), lambda r, s: (0, 2 * slots, 0)),
            pl.BlockSpec((1, width, width), lambda r, s: (0, 0, 0)),
        ],
        out_specs=[
            pl.BlockSpec((2, width, width), lambda r, s: (0, 0, 0)),
            pl.BlockSpec((2, width, width), lambda r, s: (0, 0, 0)),
            pl.BlockSpec((pieces, 3 * width // pieces, width), lambda r, s: (0, 0, 0)),
        ],
        scratch_shapes=[pltpu.VMEM((2 * width, 2 * width), f32)],
    )
    return pl.pallas_call(
        kernel,
        grid_spec=grid_spec,
        out_shape=[
            jax.ShapeDtypeStruct((2, width, width), f32),
            jax.ShapeDtypeStruct((2, width, width), f32),
            jax.ShapeDtypeStruct((pieces, 3 * width // pieces, width), f32),
        ],
        compiler_params=pltpu.CompilerParams(vmem_limit_bytes=40 << 20),
        cost_estimate=pl.CostEstimate(flops=10_000_000_000, bytes_accessed=12_000_000, transcendentals=0),
    )(info, gathered, other, low, low, low, pivot)


def exchange(x, axis):
    return lax.all_to_all(x, axis, split_axis=0, concat_axis=0, tiled=True)


def swap(x):
    return lax.ppermute(x, CORES, [(0, 1), (1, 0)])


def body(anc, pattern, parents, low_one, pivot_one, low_two, factor, pivot_two):
    row, chip, core = (lax.axis_index(a) for a in (ROWS, CHIPS, CORES))
    rows, chips, cores = (lax.axis_size(a) for a in (ROWS, CHIPS, CORES))
    cols = chips * cores
    width = pivot_one.shape[-1]
    piece = width // cols
    col = chip * cores + core
    kind = jnp.arange(cols, dtype=jnp.int32)
    children = jnp.sum(jnp.where(parents[None, :] == kind[:, None], kind[None, :], 0), axis=1)

    gathered = lax.all_gather(anc, ROWS, axis=0, tiled=False)

    flat = [x.reshape(cols, piece, width) for x in (low_one, low_two, factor)]
    pieces = exchange(jnp.concatenate(flat, axis=1), (CHIPS, CORES)).reshape(3 * cols, piece, width)
    order = jnp.stack([3 * kind, 3 * children + 1], axis=1).reshape(-1)
    routed = jnp.take(pieces, order, axis=0).reshape(rows, cores * 2 * piece, width)
    uppers = jnp.take(pieces, 3 * lax.dynamic_slice_in_dim(children, row * cores, cores) + 2, axis=0)
    mine = exchange(routed, ROWS).reshape(rows, cores, 2 * piece, width)
    mine = mine.transpose(1, 0, 2, 3).reshape(cores, rows * 2 * piece, width)
    mine = jnp.concatenate([mine, uppers], axis=1)
    send = jnp.broadcast_to(mine[None], (chips, *mine.shape)).reshape(cols, *mine.shape[1:])
    low = exchange(send, (CHIPS, CORES))

    base = jnp.arange(rows, dtype=jnp.int32) * 2
    here = jnp.take(pattern, row * cores + core, axis=0)
    there = jnp.take(pattern, row * cores + 1 - core, axis=0)
    pick = (there - base)[:, None, None] > 0
    other = swap(jnp.where(pick, gathered[:, :, width:], gathered[:, :, :width]))
    on_slot = jnp.take(here, chip) != col
    info = jnp.concatenate(
        [here - base, jnp.stack([on_slot.astype(jnp.int32), (chip == row).astype(jnp.int32), chip])]
    )
    keep, give, parts = level_blocks(info, gathered, other, low, pivot_one, rows)
    taken = swap(give)

    summed = jnp.sum(exchange(parts, CHIPS), axis=0)
    halves = summed.reshape(3, cores, piece, width).transpose(1, 0, 2, 3).reshape(cores, 3 * piece, width)
    halves = jnp.broadcast_to(halves[None], (rows, *halves.shape)).reshape(cols, 3 * piece, width)
    known = exchange(halves, (ROWS, CORES)).reshape(3 * cols, piece, width)
    order = jnp.stack([3 * kind, 3 * parents + 1, 3 * parents + 2], axis=1).reshape(-1)
    final = exchange(jnp.take(known, order, axis=0).reshape(cols, 3 * piece, width), (CHIPS, CORES))
    final = final.reshape(cols, 3, piece, width)
    diag_one, cross, last = (final[:, n].reshape(1, width, width) for n in range(3))

    first = core == 0
    column_one = jnp.where(first, jnp.stack([keep[0], taken[0]]), jnp.stack([taken[0], keep[0]]))
    pair = jnp.stack([keep[1], taken[1]])
    every = lax.all_gather(pair, ROWS, axis=0, tiled=True)
    wanted = lax.dynamic_slice_in_dim(parents, row * cores, cores)
    column_two = jnp.take(every, 2 * (wanted // 2) + jnp.bitwise_xor(wanted % 2, core), axis=0)
    return column_one, diag_one, column_two, -cross, pivot_two + last


def solution(mesh):
    rows, cols = mesh.devices.shape
    cut = Mesh(mesh.devices.reshape(rows, cols // 2, 2), (ROWS, CHIPS, CORES))
    side = (CHIPS, CORES)
    return jax.shard_map(
        body,
        mesh=cut,
        in_specs=(
            P(side, ROWS),
            P(),
            P(),
            P(side, ROWS, None),
            P(side, None, None),
            P(side, ROWS, None),
            P(side, None, None),
            P(side, None, None),
        ),
        out_specs=(
            P(ROWS, side, None),
            P(side, None, None),
            P(ROWS, side, None),
            P(side, None, None),
            P(side, None, None),
        ),
        check_vma=False,
    )
```

time: 683 us -> 239 us (0.35)
  the two profiles are of different devices: /device:TPU:1 before, /device:TPU:104 now
where the time goes in v1:
time: 239 us; the launch traced here: 238 us
  waiting for transfers between devices  118 us (49%)
  starting transfers between devices  42.9 us (18%)
  blocking collectives  26.5 us (11%)
  between operations  14.9 us (6%)
  other arithmetic  13.6 us (6%)
  local copies, waits for them, and re-layouts  11.8 us (5%)
  Pallas kernels  9.9 us (4%)
    all_to_all x5, waiting for transfers between devices, exchange(): return lax.all_to_all(x, axis, split_axis=0, concat_axis=0, tiled=True)  62.6 us
    all_gather x1, waiting for transfers between devices, body(): gathered = lax.all_gather(anc, ROWS, axis=0, tiled=False)  53.4 us
    all_to_all x5, starting transfers between devices, exchange(): return lax.all_to_all(x, axis, split_axis=0, concat_axis=0, tiled=True)  42.6 us
    all_to_all x1, blocking collectives, exchange(): return lax.all_to_all(x, axis, split_axis=0, concat_axis=0, tiled=True)  26.5 us
    pallas_call x1, Pallas kernels, level_blocks(): pl.pallas_call(kernel, grid_spec=grid_spec, out_shape=[jax.ShapeDtypeStru...  9.9 us
  transfers between devices with their start and end apart: 9, of which 7 were waited for; matrix products, arithmetic and copies ran while one was open for 8% of the time, Pallas kernels for 0%

profile of v1, /device:TPU:104, one launch (start us, length us, event | category | flops | bytes accessed | tf_op | source)
XLA Modules:
  0.0 237.9 jit_solution(14942777777183422102)
XLA Ops:
  7.9 2.1 pad_maximum_fusion
  10.0 6.1 %all-to-all-start = ((f32[16,48,256]{2,1,0:T(8,128)}), f32[16,48,256]{2,1,0:T(8,128)S(1)}, u32[]{:S(2)}, u32[]{:S(2)}) async-start(f32[16,48,256]{2,1,0:T(8,128)} %pad_maximum_fusion), calls=%async_computation | async-start | bytes 1572864 | tf_op jit(solution)/shard_map/all_to_all | solution.py:102
  17.4 13.9 %all-to-all-done = f32[16,48,256]{2,1,0:T(8,128)S(1)} async-done(((f32[16,48,256]{2,1,0:T(8,128)}), f32[16,48,256]{2,1,0:T(8,128)S(1)}, u32[]{:S(2)}, u32[]{:S(2)}) %all-to-all-start) | async-done | bytes 786464 | tf_op jit(solution)/shard_map/all_to_all | solution.py:102
  31.9 0.9 bitcast_select_fusion.1
  32.8 5.4 %all-to-all-start.1 = ((f32[8,64,256]{2,1,0:T(8,128)}), f32[8,64,256]{2,1,0:T(8,128)S(1)}, u32[]{:S(2)}, u32[]{:S(2)}) async-start(f32[8,64,256]{2,1,0:T(8,128)} %bitcast_select_fusion.1), calls=%async_computation.1 | async-start | bytes 1048576 | tf_op jit(solution)/shard_map/all_to_all | solution.py:102
  38.9 12.4 %all-to-all-done.1 = f32[8,64,256]{2,1,0:T(8,128)S(1)} async-done(((f32[8,64,256]{2,1,0:T(8,128)}), f32[8,64,256]{2,1,0:T(8,128)S(1)}, u32[]{:S(2)}, u32[]{:S(2)}) %all-to-all-start.1) | async-done | bytes 524320 | tf_op jit(solution)/shard_map/all_to_all | solution.py:102
  51.4 2.5 %broadcast_in_dim.110 = f32[8,2,272,256]{3,2,1,0:T(8,128)} broadcast(f32[2,272,256]{2,1,0:T(8,128)S(1)} %pad_maximum_fusion.1), dimensions={1,2,3} | broadcast | bytes 5013504 | tf_op jit(solution)/shard_map/broadcast_in_dim | solution.py:129
  53.9 4.7 %all-to-all-start.2 = ((f32[16,272,256]{2,1,0:T(8,128)}), f32[16,272,256]{2,1,0:T(8,128)}, u32[]{:S(2)}, u32[]{:S(2)}) async-start(f32[16,272,256]{2,1,0:T(8,128)} %bitcast.43), calls=%async_computation.2 | async-start | bytes 8912896 | tf_op jit(solution)/shard_map/all_to_all | solution.py:102
  58.9 53.4 %all-gather.6.cloned.1.call-done = f32[2048,512]{1,0:T(8,128)} async-done(((f32[256,512]{1,0:T(8,128)}), f32[2048,512]{1,0:T(8,128)}) %all-gather.6.cloned.1.call-update) | async-done | bytes 4194320 | tf_op jit(solution)/shard_map/all_gather | solution.py:119
  112.3 3.9 %slice_select_fusion = f32[8,256,256]{2,1,0:T(8,128)} fusion(f32[8,256,512]{2,1,0:T(8,128)} %bitcast.41, pred[8]{0:T(512)(128)(4,1)S(1)} %subtract_compare_fusion), kind=kLoop, calls=%fused_computation.4 | loop fusion | flops 524288 | bytes 6291464 | tf_op jit(solution)/shard_map/jit(_where)/select_n | solution.py:136
  117.5 4.3 %all-to-all-done.2.low.low_here.factor = f32[16,272,256]{2,1,0:T(8,128)} async-done(((f32[16,272,256]{2,1,0:T(8,128)}), f32[16,272,256]{2,1,0:T(8,128)}, u32[]{:S(2)}, u32[]{:S(2)}) %all-to-all-start.2) | async-done | bytes 4456480 | tf_op jit(solution)/shard_map/all_to_all | solution.py:102
  121.8 2.2 copy-done
  124.0 9.9 %shard_map.119 = (f32[2,256,256]{2,1,0:T(8,128)S(1)}, f32[2,256,256]{2,1,0:T(8,128)S(1)}, f32[8,96,256]{2,1,0:T(8,128)S(1)}) custom-call(s32[11]{0:T(128)S(1)} %pad_add_fusion.2.info, f32[8,256,512]{2,1,0:T(8,128)S(1)} %bitcast.42, f32[8,256,256]{2,1,0:T(8,128)S(1)} %collective-permute-done.other, f32[16,272,256]{2,1,0:T(8,128)} %all-to-all-done.2.low.low_here.factor, ...), custom_call_target="tpu_custom_call" | custom-call | flops 10000000000 | bytes 12000000 | tf_op jit(solution)/shard_map/pallas_call | solution.py:88
  134.2 1.8 collective-permute-done.1
  136.8 26.5 %all_to_all.30 = f32[8,96,256]{2,1,0:T(8,128)S(1)} all-to-all(f32[8,96,256]{2,1,0:T(8,128)S(1)} %get-tuple-element.11), channel_id=1, replica_groups=mesh['prow'=8,'chip'=8,'core'=2] {'chip'}, dimensions={0} | all-to-all | bytes 1572864 | tf_op jit(solution)/shard_map/all_to_all | solution.py:102
  163.4 1.0 broadcast_in_dim.115
  164.4 8.2 %all-to-all-start.4 = ((f32[16,48,256]{2,1,0:T(8,128)}), f32[16,48,256]{2,1,0:T(8,128)S(1)}, u32[]{:S(2)}, u32[]{:S(2)}) async-start(f32[16,48,256]{2,1,0:T(8,128)} %bitcast.22), calls=%async_computation.4 | async-start | bytes 1572864 | tf_op jit(solution)/shard_map/all_to_all | solution.py:102
  173.1 17.7 %all-to-all-done.4 = f32[16,48,256]{2,1,0:T(8,128)S(1)} async-done(((f32[16,48,256]{2,1,0:T(8,128)}), f32[16,48,256]{2,1,0:T(8,128)S(1)}, u32[]{:S(2)}, u32[]{:S(2)}) %all-to-all-start.4) | async-done | bytes 786464 | tf_op jit(solution)/shard_map/all_to_all | solution.py:102
  191.5 1.1 bitcast_select_fusion
  192.5 18.1 %all-to-all-start.5 = ((f32[16,48,256]{2,1,0:T(8,128)}), f32[16,48,256]{2,1,0:T(8,128)S(1)}, u32[]{:S(2)}, u32[]{:S(2)}) async-start(f32[16,48,256]{2,1,0:T(8,128)} %bitcast_select_fusion), calls=%async_computation.5 | async-start | bytes 1572864 | tf_op jit(solution)/shard_map/all_to_all | solution.py:102
  211.6 14.2 %all-to-all-done.5 = f32[16,48,256]{2,1,0:T(8,128)S(1)} async-done(((f32[16,48,256]{2,1,0:T(8,128)}), f32[16,48,256]{2,1,0:T(8,128)S(1)}, u32[]{:S(2)}, u32[]{:S(2)}) %all-to-all-start.5) | async-done | bytes 786464 | tf_op jit(solution)/shard_map/all_to_all | solution.py:102
  225.8 0.8 fusion.5
  227.4 2.8 %gather_fusion.3 = f32[2,256,256]{2,1,0:T(8,128)S(1)} fusion(f32[16,256,256]{2,1,0:T(8,128)} %all-gather.4.cloned.1.call-done, s32[1024]{0:T(1024)S(1)} %pad_clamp_fusion), kind=kCustom, calls=%fused_computation.3 | custom fusion | bytes 1048584 | tf_op jit(solution)/shard_map/jit(_take)/gather | solution.py:158
  230.2 0.9 broadcast_select_fusion
  (61 shorter events, 8.2 us)
Async XLA Ops:
  7.2 105.2 %all-gather.6.cloned.1.call-start = ((), (), s32[]{:S(2)}) async-start(), calls=%async_computation.7 | async-start | bytes 4718592 | tf_op jit(solution)/shard_map/all_gather | solution.py:119
  10.0 21.3 %all-to-all-start = ((f32[16,48,256]{2,1,0:T(8,128)}), f32[16,48,256]{2,1,0:T(8,128)S(1)}, u32[]{:S(2)}, u32[]{:S(2)}) async-start(f32[16,48,256]{2,1,0:T(8,128)} %pad_maximum_fusion), calls=%async_computation | async-start | bytes 1572864 | tf_op jit(solution)/shard_map/all_to_all | solution.py:102
  32.8 18.5 %all-to-all-start.1 = ((f32[8,64,256]{2,1,0:T(8,128)}), f32[8,64,256]{2,1,0:T(8,128)S(1)}, u32[]{:S(2)}, u32[]{:S(2)}) async-start(f32[8,64,256]{2,1,0:T(8,128)} %bitcast_select_fusion.1), calls=%async_computation.1 | async-start | bytes 1048576 | tf_op jit(solution)/shard_map/all_to_all | solution.py:102
  53.9 4.8 %copy-start.3 = (s32[16,8]{0,1:T(8,128)S(1)}, s32[16,8]{0,1:T(8,128)}, u32[]{:S(2)}) copy-start(s32[16,8]{0,1:T(8,128)} %param.11) | copy-start | bytes 1540
  53.9 67.9 %all-to-all-start.2 = ((f32[16,272,256]{2,1,0:T(8,128)}), f32[16,272,256]{2,1,0:T(8,128)}, u32[]{:S(2)}, u32[]{:S(2)}) async-start(f32[16,272,256]{2,1,0:T(8,128)} %bitcast.43), calls=%async_computation.2 | async-start | bytes 8912896 | tf_op jit(solution)/shard_map/all_to_all | solution.py:102
  58.6 63.2 %copy-start.1 = (f32[1,256,256]{2,1,0:T(8,128)S(1)}, f32[1,256,256]{2,1,0:T(8,128)}, u32[]{:S(2)}) copy-start(f32[1,256,256]{2,1,0:T(8,128)} %pivot.1) | copy-start | bytes 786436
  58.6 168.8 %all-gather.4.cloned.1.call-start = ((), (), s32[]{:S(2)}) async-start(), calls=%async_computation.6 | async-start | bytes 4718592 | tf_op jit(solution)/shard_map/all_gather | solution.py:156
  116.2 5.7 %collective-permute-start = (f32[8,256,256]{2,1,0:T(8,128)}, f32[8,256,256]{2,1,0:T(8,128)S(1)}, u32[]{:S(2)}, u32[]{:S(2)}) collective-permute-start(f32[8,256,256]{2,1,0:T(8,128)} %slice_select_fusion), channel_id=1, source_target_pairs={{0,1},{1,0},{2,3},{3,2},{4,5},{5,4},{6,7},{7,6},{8,9},{9,8},{10,11... | collective-permute-start | bytes 6291464 | tf_op jit(solution)/shard_map/ppermute | solution.py:106
  121.8 2.2 copy-start
  133.9 2.0 collective-permute-start.1
  134.1 38.5 %copy-start.4 = (s32[16]{0:T(128)S(1)}, s32[16]{0:T(128)}, u32[]{:S(2)}) copy-start(s32[16]{0:T(128)} %param.12) | copy-start | bytes 196
  164.4 62.3 %copy-start.2 = (f32[1,256,256]{2,1,0:T(8,128)S(1)}, f32[1,256,256]{2,1,0:T(8,128)}, u32[]{:S(2)}) copy-start(f32[1,256,256]{2,1,0:T(8,128)} %param.17) | copy-start | bytes 786436
  164.4 26.5 %all-to-all-start.4 = ((f32[16,48,256]{2,1,0:T(8,128)}), f32[16,48,256]{2,1,0:T(8,128)S(1)}, u32[]{:S(2)}, u32[]{:S(2)}) async-start(f32[16,48,256]{2,1,0:T(8,128)} %bitcast.22), calls=%async_computation.4 | async-start | bytes 1572864 | tf_op jit(solution)/shard_map/all_to_all | solution.py:102
  192.5 33.3 %all-to-all-start.5 = ((f32[16,48,256]{2,1,0:T(8,128)}), f32[16,48,256]{2,1,0:T(8,128)S(1)}, u32[]{:S(2)}, u32[]{:S(2)}) async-start(f32[16,48,256]{2,1,0:T(8,128)} %bitcast_select_fusion), calls=%async_computation.5 | async-start | bytes 1572864 | tf_op jit(solution)/shard_map/all_to_all | solution.py:102
Sparse Core Ops, SparseCore 0:
  9.6 102.6 all-gather.5
  136.9 82.0 all-gather.3

commit v2 on v1

v2 whole, which is shorter than its diff:
```python
import functools

import jax
import jax.numpy as jnp
from jax import lax
from jax.experimental import pallas as pl
from jax.experimental.pallas import tpu as pltpu
from jax.sharding import Mesh, PartitionSpec as P

NEXT, RING, LINE, ACROSS, CORES = "next", "ring", "x", "across", "core"
ROWS = (NEXT, RING)
CHIPS = (LINE, ACROSS)
SIDE = (*CHIPS, CORES)


def split(x):
    high = x.astype(jnp.bfloat16)
    return high, (x - high.astype(jnp.float32)).astype(jnp.bfloat16)


def product(a, b, a_dim=1, b_dim=0):
    dims = (((a_dim,), (b_dim,)), ((), ()))
    dot = functools.partial(lax.dot_general, dimension_numbers=dims, preferred_element_type=jnp.float32)
    (ah, al), (bh, bl) = split(a), split(b)
    return dot(ah, bh) + (dot(ah, bl) + dot(al, bh))


ROUTE = (
    ((0, 0, 0), (0, 0, 1)),
    ((-1, 0, 0), (-1, 0, 1)),
    ((1, 0, 0), (1, 0, 1)),
    ((0, 1, 0), (0, 1, 1)),
    ((-1, 1, 0), (-1, 1, 1), (2, 0, 0)),
    ((1, 1, 0), (1, 1, 1), (2, 0, 1)),
    ((2, 1, 0),),
    ((2, 1, 1),),
)
PLACES = ((0, 0), (-1, 0), (1, 0), (2, 0), (0, 1), (-1, 1), (1, 1), (2, 1))


def kernel(info, own, other, *refs):
    lows, (pivot, keep, give, second, parts, total, wide) = refs[: len(ROUTE)], refs[len(ROUTE) :]
    step = pl.program_id(0)
    slots = pl.num_programs(0)
    width = own.shape[-1]
    piece = 16

    @pl.when(step == 0)
    def _():
        total[...] = jnp.zeros_like(total)

    def collect(row, levels):
        for ref, entries in zip(lows, ROUTE):
            for n, (along, beside, part) in enumerate(entries):
                chip = info[20 + PLACES.index((along, beside))]
                to = pl.ds(pl.multiple_of((2 * chip + part) * piece, piece), piece)
                for level in range(levels):
                    at = pl.ds(pl.multiple_of(row + level * piece, piece), piece)
                    wide[to, level * width : (level + 1) * width] = ref[n, at, :]

    left = jnp.concatenate([own[0], other[0]], axis=0)
    collect(2 * piece * info[12 + step], 2)
    total[...] += product(left, wide[...])

    @pl.when(step == slots - 1)
    def _():
        collect(2 * piece * slots, 1)
        upper = wide[:, :width]
        one = total[:, :width]
        two = product(one, upper) - total[:, width:]
        keep[0] = -one[:width]
        give[0] = -one[width:]
        core = info[11]
        tiles = (second.shape[0], second.shape[2], width)
        second[:, core] = two[:width].reshape(tiles)
        second[:, 1 - core] = two[width:].reshape(tiles)
        away = info[8] > 0
        slot_one = jnp.where(away, -one[width:], -one[:width])
        slot_two = jnp.where(away, two[width:], two[:width])
        collect(2 * piece * info[10], 2)
        low_one, low_two = wide[:, :width], wide[:, width:]
        here = jnp.where(info[9] > 0, pivot[0], jnp.zeros_like(slot_one))
        diag = here - product(low_one, slot_one, 0, 0)
        cross = product(diag, upper) + product(slot_one, low_two, 0, 0)
        last = product(upper, cross, 0, 0) - product(low_two, slot_two, 0, 0)
        pieces, tall = parts.shape[0], parts.shape[1] // 3
        for n, term in enumerate((diag, cross, last)):
            parts[:, n * tall : (n + 1) * tall, :] = term.reshape(pieces, tall, width)


def level_blocks(info, gathered, other, lows, pivot):
    width = pivot.shape[-1]
    slots = other.shape[0]
    pieces = slots
    f32 = jnp.float32
    grid_spec = pltpu.PrefetchScalarGridSpec(
        num_scalar_prefetch=1,
        grid=(slots,),
        in_specs=[
            pl.BlockSpec((1, width, width), lambda r, s: (r, 0, s[r])),
            pl.BlockSpec((1, width, width), lambda r, s: (r, 0, 0)),
            *[pl.BlockSpec(x.shape, lambda r, s: (0, 0, 0), pipeline_mode=pl.Buffered(1)) for x in lows],
            pl.BlockSpec((1, width, width), lambda r, s: (0, 0, 0)),
        ],
        out_specs=[
            pl.BlockSpec((1, width, width), lambda r, s: (0, 0, 0)),
            pl.BlockSpec((1, width, width), lambda r, s: (0, 0, 0)),
            pl.BlockSpec((slots, 2, width // slots, width), lambda r, s: (0, 0, 0, 0)),
            pl.BlockSpec((pieces, 3 * width // pieces, width), lambda r, s: (0, 0, 0)),
        ],
        scratch_shapes=[pltpu.VMEM((2 * width, 2 * width), f32), pltpu.VMEM((width, 2 * width), f32)],
    )
    return pl.pallas_call(
        kernel,
        grid_spec=grid_spec,
        out_shape=[
            jax.ShapeDtypeStruct((1, width, width), f32),
            jax.ShapeDtypeStruct((1, width, width), f32),
            jax.ShapeDtypeStruct((slots, 2, width // slots, width), f32),
            jax.ShapeDtypeStruct((pieces, 3 * width // pieces, width), f32),
        ],
        compiler_params=pltpu.CompilerParams(vmem_limit_bytes=60 << 20),
        cost_estimate=pl.CostEstimate(flops=10_000_000_000, bytes_accessed=12_000_000, transcendentals=0),
    )(info, gathered, other, *lows, pivot)


def exchange(x, axis):
    return lax.all_to_all(x, axis, split_axis=0, concat_axis=0, tiled=True)


def swap(x, axis=CORES):
    return lax.ppermute(x, axis, [(0, 1), (1, 0)])


def shift(x, axis, by):
    n = lax.axis_size(axis)
    return lax.ppermute(x, axis, [(i, (i + by) % n) for i in range(n)])


def go_round(*ways):
    hold = lax.optimization_barrier
    owns = hold(tuple(own for own, _, _ in ways))
    near = []
    for own, (_, line, neighbour) in zip(owns, ways):
        near.append((shift(own, line, 1), shift(own, line, -1), swap(own, neighbour)))
    near = hold(near)
    far = []
    for (below, above, beside), (_, line, _) in zip(near, ways):
        half = below.shape[0] // 2
        up = shift(jnp.concatenate([beside, below[:half]]), line, 1)
        down = shift(jnp.concatenate([beside, above[half:]]), line, -1)
        far.append((up, down))
    far = hold(far)
    ends = []
    for (up, down), (own, line, _) in zip(far, ways):
        half = own.shape[0] // 2
        ends.append((shift(up[:half], line, 1), shift(down[half : 2 * half], line, -1)))
    return [(own, *n, *f, *e) for own, n, f, e in zip(owns, near, far, ends)]


def body(anc, pattern, parents, low_one, pivot_one, low_two, factor, pivot_two):
    row, line, across, core = (lax.axis_index(a) for a in (ROWS, LINE, ACROSS, CORES))
    half = lax.axis_index(NEXT)
    rows, lines, pair, cores = (lax.axis_size(a) for a in (ROWS, LINE, ACROSS, CORES))
    chips = lines * pair
    cols = chips * cores
    width = pivot_one.shape[-1]
    piece = width // cols
    chip = line * pair + across
    col = chip * cores + core
    kind = jnp.arange(cols, dtype=jnp.int32)
    children = jnp.sum(jnp.where(parents[None, :] == kind[:, None], kind[None, :], 0), axis=1)

    flat = [x.reshape(cols, piece, width) for x in (low_one, low_two, factor)]
    pieces = exchange(jnp.concatenate(flat, axis=1), SIDE).reshape(3 * cols, piece, width)
    order = jnp.stack([3 * kind, 3 * children + 1], axis=1).reshape(-1)
    routed = jnp.take(pieces, order, axis=0).reshape(rows, cores * 2 * piece, width)
    own_children = lax.dynamic_slice_in_dim(children, row * cores, cores)
    uppers = jnp.take(pieces, 3 * own_children + 2, axis=0)
    mine = exchange(routed, ROWS).reshape(rows, cores, 2 * piece, width)

    kept, sent = (
        jnp.concatenate(
            [
                lax.dynamic_index_in_dim(mine, n, 1, keepdims=False).reshape(rows * 2 * piece, width),
                lax.dynamic_index_in_dim(uppers, n, 0, keepdims=False),
            ]
        )
        for n in (core, 1 - core)
    )
    got = swap(sent)
    both = jnp.where(core == 0, jnp.stack([kept, got]), jnp.stack([got, kept]))

    inverse, lows = go_round((anc, RING, NEXT), (both, LINE, ACROSS))
    own, below, above, beside, up, down, low_far, high_far = inverse
    across_far = jnp.concatenate([up[width:], down[width:]])
    last_far = jnp.concatenate([low_far, high_far])
    gathered = jnp.stack([own, below, above, across_far, beside, up[:width], down[:width], last_far])

    ring = lax.axis_index(RING)
    lengths = lax.axis_size(RING)
    slot = jnp.stack([(half ^ n) * lengths + (ring + m) % lengths for m, n in PLACES])
    places = jnp.stack([(line + m) % lines * pair + (across ^ n) for m, n in PLACES])
    here = jnp.take(pattern, row * cores + core, axis=0)
    there = jnp.take(pattern, row * cores + 1 - core, axis=0)
    pick = jnp.take(there, slot)[:, None, None] % 2 > 0
    other = swap(jnp.where(pick, gathered[:, :, width:], gathered[:, :, :width]))
    away = jnp.take(here, chip) != col
    flags = jnp.stack([away.astype(jnp.int32), (chip == row).astype(jnp.int32), chip, core])
    info = jnp.concatenate([jnp.take(here, slot) % 2, flags, slot, places])
    keep, give, second, parts = level_blocks(info, gathered, other, lows, pivot_one)
    taken = swap(give)
    column_one = jnp.where(core == 0, jnp.concatenate([keep, taken]), jnp.concatenate([taken, keep]))

    summed = jnp.sum(exchange(parts, CHIPS), axis=0)
    halves = summed.reshape(3, cores, piece, width).transpose(1, 0, 2, 3).reshape(1, cores, 3 * piece, width)
    halves = jnp.broadcast_to(halves, (rows, *halves.shape[1:]))
    send = jnp.concatenate([halves, second], axis=2).reshape(cols, -1, width)
    known = exchange(send, (*ROWS, CORES))
    column_two = jnp.take(known[:, 3 * piece :], parents, axis=0)
    column_two = exchange(column_two.reshape(rows, -1, width), ROWS)
    column_two = column_two.reshape(rows, cores, -1, width).transpose(1, 0, 2, 3)
    known = known.reshape(cols, -1, piece, width)
    blocks = [known[:, 0], jnp.take(known[:, 1:3], parents, axis=0).reshape(cols, -1, width)]
    final = exchange(jnp.concatenate(blocks, axis=1), SIDE)
    final = final.reshape(cols, 3, piece, width)
    diag_one, cross, last = (final[:, n].reshape(1, width, width) for n in range(3))
    return column_one, diag_one, column_two.reshape(cores, width, width), -cross, pivot_two + last


def solution(mesh):
    rows, cols = mesh.devices.shape
    cut = Mesh(mesh.devices.reshape(2, rows // 2, cols // 4, 2, 2), (*ROWS, *SIDE))
    flat, wide = P(SIDE, None, None), P(SIDE, ROWS, None)
    return jax.shard_map(
        body,
        mesh=cut,
        in_specs=(P(SIDE, ROWS), P(), P(), wide, flat, wide, flat, flat),
        out_specs=(P(ROWS, SIDE, None), flat, P(ROWS, SIDE, None), flat, flat),
        check_vma=False,
    )
```

time: 239 us -> 215 us (0.90)
  the two profiles are of different devices: /device:TPU:104 before, /device:TPU:1 now
where the time goes in v2:
time: 215 us; the launch traced here: 214 us
  waiting for transfers between devices  102 us (47%)
  starting transfers between devices  54.8 us (25%)
  blocking collectives  18.3 us (9%)
  local copies, waits for them, and re-layouts  12.7 us (6%)
  Pallas kernels  12.6 us (6%)
  other arithmetic  11.7 us (5%)
    all_to_all x5, waiting for transfers between devices, exchange(): return lax.all_to_all(x, axis, split_axis=0, concat_axis=0, tiled=True)  55.4 us
    ppermute x12, waiting for transfers between devices, shift(): return lax.ppermute(x, axis, [(i, (i + by) % n) for i in range(n)])  33 us
    all_to_all x5, starting transfers between devices, exchange(): return lax.all_to_all(x, axis, split_axis=0, concat_axis=0, tiled=True)  29.3 us
    all_to_all x1, blocking collectives, exchange(): return lax.all_to_all(x, axis, split_axis=0, concat_axis=0, tiled=True)  18.3 us
    ppermute x12, starting transfers between devices, shift(): return lax.ppermute(x, axis, [(i, (i + by) % n) for i in range(n)])  15 us
    ppermute x5, waiting for transfers between devices, swap(): return lax.ppermute(x, axis, [(0, 1), (1, 0)])  14.1 us
    pallas_call x1, Pallas kernels, level_blocks(): pl.pallas_call(kernel, grid_spec=grid_spec, out_shape=[jax.ShapeDtypeStru...  12.6 us
    ppermute x5, starting transfers between devices, swap(): return lax.ppermute(x, axis, [(0, 1), (1, 0)])  10.5 us
  transfers between devices with their start and end apart: 22, of which 15 were waited for; matrix products, arithmetic and copies ran while one was open for 6% of the time, Pallas kernels for 0%

profile of v2, /device:TPU:1, one launch (start us, length us, event | category | flops | bytes accessed | tf_op | source)
XLA Modules:
  0.0 214.2 jit_solution(16026437414227250975)
XLA Ops:
  2.7 8.6 %all-to-all-start = ((f32[16,48,256]{2,1,0:T(8,128)}), f32[16,48,256]{2,1,0:T(8,128)S(1)}, u32[]{:S(2)}, u32[]{:S(2)}) async-start(f32[16,48,256]{2,1,0:T(8,128)} %pad_maximum_fusion.5), calls=%async_computation | async-start | bytes 1572864 | tf_op jit(solution)/shard_map/all_to_all | solution.py:128
  12.6 12.8 %all-to-all-done = f32[16,48,256]{2,1,0:T(8,128)S(1)} async-done(((f32[16,48,256]{2,1,0:T(8,128)}), f32[16,48,256]{2,1,0:T(8,128)S(1)}, u32[]{:S(2)}, u32[]{:S(2)}) %all-to-all-start) | async-done | bytes 786464 | tf_op jit(solution)/shard_map/all_to_all | solution.py:128
  27.0 5.1 %all-to-all-start.1 = ((f32[8,64,256]{2,1,0:T(8,128)}), f32[8,64,256]{2,1,0:T(8,128)S(1)}, u32[]{:S(2)}, u32[]{:S(2)}) async-start(f32[8,64,256]{2,1,0:T(8,128)} %bitcast_select_fusion.2), calls=%async_computation.1 | async-start | bytes 1048576 | tf_op jit(solution)/shard_map/all_to_all | solution.py:128
  32.7 6.8 %all-to-all-done.1 = f32[8,64,256]{2,1,0:T(8,128)S(1)} async-done(((f32[8,64,256]{2,1,0:T(8,128)}), f32[8,64,256]{2,1,0:T(8,128)S(1)}, u32[]{:S(2)}, u32[]{:S(2)}) %all-to-all-start.1) | async-done | bytes 524320 | tf_op jit(solution)/shard_map/all_to_all | solution.py:128
  39.6 3.3 %collective-permute-start = (f32[272,256]{1,0:T(8,128)S(1)}, f32[272,256]{1,0:T(8,128)S(1)}, u32[]{:S(2)}, u32[]{:S(2)}) collective-permute-start(f32[272,256]{1,0:T(8,128)S(1)} %pad_maximum_fusion.7), channel_id=1, source_target_pairs={{0,1},{1,0},{2,3},{3,2},{4,5},{5,4},{6,7},{7,6},{8,9},{9,8},{10,11... | collective-permute-start | bytes 835592 | tf_op jit(solution)/shard_map/ppermute | solution.py:132
  44.3 2.7 %collective-permute-start.5 = (f32[2,272,256]{2,1,0:T(8,128)S(1)}, f32[2,272,256]{2,1,0:T(8,128)}, u32[]{:S(2)}, u32[]{:S(2)}) collective-permute-start(f32[2,272,256]{2,1,0:T(8,128)S(1)} %maximum_select_fusion.refs_0_), channel_id=1, source_target_pairs={{0,12},{4,0},{8,4},{12,8},{1,13},{5,1},{9,5},{13,9},{2,14},{6,2},{... | collective-permute-start | bytes 1671176 | tf_op jit(solution)/shard_map/ppermute | solution.py:137
  51.0 7.9 %collective-permute-done.1 = f32[256,512]{1,0:T(8,128)S(1)} collective-permute-done((f32[256,512]{1,0:T(8,128)}, f32[256,512]{1,0:T(8,128)S(1)}, u32[]{:S(2)}, u32[]{:S(2)}) %collective-permute-start.1) | collective-permute-done | bytes 524320 | tf_op jit(solution)/shard_map/ppermute | solution.py:137
  61.0 11.6 %collective-permute-done.3 = f32[256,512]{1,0:T(8,128)S(1)} collective-permute-done((f32[256,512]{1,0:T(8,128)}, f32[256,512]{1,0:T(8,128)S(1)}, u32[]{:S(2)}, u32[]{:S(2)}) %collective-permute-start.3) | collective-permute-done | bytes 524320 | tf_op jit(solution)/shard_map/ppermute | solution.py:132
  72.9 2.7 %collective-permute-start.8 = (f32[384,512]{1,0:T(8,128)S(1)}, f32[384,512]{1,0:T(8,128)S(1)}, u32[]{:S(2)}, u32[]{:S(2)}) collective-permute-start(f32[384,512]{1,0:T(8,128)S(1)} %get-tuple-element.74), channel_id=1, source_target_pairs={{0,48},{16,0},{32,16},{48,32},{1,49},{17,1},{33,17},{49,33},{2,50}... | collective-permute-start | bytes 2359304 | tf_op jit(solution)/shard_map/ppermute | solution.py:137
  77.8 2.7 %collective-permute-start.10 = (f32[3,272,256]{2,1,0:T(8,128)S(1)}, f32[3,272,256]{2,1,0:T(8,128)S(1)}, u32[]{:S(2)}, u32[]{:S(2)}) collective-permute-start(f32[3,272,256]{2,1,0:T(8,128)S(1)} %get-tuple-element.72), channel_id=1, source_target_pairs={{0,12},{4,0},{8,4},{12,8},{1,13},{5,1},{9,5},{13,9},{2,14},{6,2},{... | collective-permute-start | bytes 2506760 | tf_op jit(solution)/shard_map/ppermute | solution.py:137
  81.6 10.1 %collective-permute-done.7 = f32[384,512]{1,0:T(8,128)S(1)} collective-permute-done((f32[384,512]{1,0:T(8,128)S(1)}, f32[384,512]{1,0:T(8,128)S(1)}, u32[]{:S(2)}, u32[]{:S(2)}) %collective-permute-start.7) | collective-permute-done | bytes 786464 | tf_op jit(solution)/shard_map/ppermute | solution.py:137
  91.7 5.3 %collective-permute-done.9.refs_4_ = f32[3,272,256]{2,1,0:T(8,128)S(1)} collective-permute-done((f32[3,272,256]{2,1,0:T(8,128)S(1)}, f32[3,272,256]{2,1,0:T(8,128)S(1)}, u32[]{:S(2)}, u32[]{:S(2)}) %collective-permute-start.9) | collective-permute-done | bytes 835616 | tf_op jit(solution)/shard_map/ppermute | solution.py:137
  98.9 3.7 %collective-permute-done.12 = f32[128,512]{1,0:T(8,128)S(1)} collective-permute-done((f32[128,512]{1,0:T(8,128)S(1)}, f32[128,512]{1,0:T(8,128)S(1)}, u32[]{:S(2)}, u32[]{:S(2)}) %collective-permute-start.12) | collective-permute-done | bytes 262176 | tf_op jit(solution)/shard_map/ppermute | solution.py:137
  106.2 4.5 %collective-permute-start.13 = (f32[8,256,256]{2,1,0:T(8,128)S(1)}, f32[8,256,256]{2,1,0:T(8,128)}, u32[]{:S(2)}, u32[]{:S(2)}) collective-permute-start(f32[8,256,256]{2,1,0:T(8,128)S(1)} %slice_select_fusion), channel_id=1, source_target_pairs={{0,1},{1,0},{2,3},{3,2},{4,5},{5,4},{6,7},{7,6},{8,9},{9,8},{10,11... | collective-permute-start | bytes 6291464 | tf_op jit(solution)/shard_map/ppermute | solution.py:132
  110.8 2.7 %collective-permute-start.15 = (f32[1,272,256]{2,1,0:T(8,128)S(1)}, f32[1,272,256]{2,1,0:T(8,128)S(1)}, u32[]{:S(2)}, u32[]{:S(2)}) collective-permute-start(f32[1,272,256]{2,1,0:T(8,128)S(1)} %slice.73), channel_id=1, source_target_pairs={{0,12},{4,0},{8,4},{12,8},{1,13},{5,1},{9,5},{13,9},{2,14},{6,2},{... | collective-permute-start | bytes 835592 | tf_op jit(solution)/shard_map/ppermute | solution.py:137
  116.0 4.2 %collective-permute-done.14.refs_6_ = f32[1,272,256]{2,1,0:T(8,128)S(1)} collective-permute-done((f32[1,272,256]{2,1,0:T(8,128)S(1)}, f32[1,272,256]{2,1,0:T(8,128)S(1)}, u32[]{:S(2)}, u32[]{:S(2)}) %collective-permute-start.14) | collective-permute-done | bytes 278560 | tf_op jit(solution)/shard_map/ppermute | solution.py:137
  121.1 12.6 %shard_map.119 = (f32[1,256,256]{2,1,0:T(8,128)}, f32[1,256,256]{2,1,0:T(8,128)}, f32[8,2,32,256]{3,2,1,0:T(8,128)}, f32[8,96,256]{2,1,0:T(8,128)}) custom-call(s32[28]{0:T(128)} %concatenate.43.info, f32[8,256,512]{2,1,0:T(8,128)} %copy-done, f32[8,256,256]{2,1,0:T(8,128)} %collective-permute-done.13.other, f32[2,272,256]{2,1,0:T(8,128)} %copy-done.2, ...), custom_call_target="tpu_custom_call" | custom-call | flops 10000000000 | bytes 12000000 | tf_op jit(solution)/shard_map/pallas_call | solution.py:113
  133.7 18.3 %all_to_all.30 = f32[8,96,256]{2,1,0:T(8,128)S(1)} all-to-all(f32[8,96,256]{2,1,0:T(8,128)} %get-tuple-element.37), channel_id=1, replica_groups=mesh['next'=2,'ring'=4,'x'=4,'across'=2,'core'=2] {'x','across'}, dimensions={0} | all-to-all | bytes 1572864 | tf_op jit(solution)/shard_map/all_to_all | solution.py:128
  154.3 6.2 %all-to-all-start.3 = ((f32[16,80,256]{2,1,0:T(8,128)}), f32[16,80,256]{2,1,0:T(8,128)S(1)}, u32[]{:S(2)}, u32[]{:S(2)}) async-start(f32[16,80,256]{2,1,0:T(8,128)} %bitcast.47), calls=%async_computation.3 | async-start | bytes 2621440 | tf_op jit(solution)/shard_map/all_to_all | solution.py:128
  160.9 18.5 %all-to-all-done.3 = f32[16,80,256]{2,1,0:T(8,128)S(1)} async-done(((f32[16,80,256]{2,1,0:T(8,128)}), f32[16,80,256]{2,1,0:T(8,128)S(1)}, u32[]{:S(2)}, u32[]{:S(2)}) %all-to-all-start.3) | async-done | bytes 1310752 | tf_op jit(solution)/shard_map/all_to_all | solution.py:128
  180.9 3.7 %all-to-all-start.5 = ((f32[8,64,256]{2,1,0:T(8,128)}), f32[8,64,256]{2,1,0:T(8,128)S(1)}, u32[]{:S(2)}, u32[]{:S(2)}) async-start(f32[8,64,256]{2,1,0:T(8,128)} %bitcast_select_fusion), calls=%async_computation.5 | async-start | bytes 1048576 | tf_op jit(solution)/shard_map/all_to_all | solution.py:128
  186.3 6.4 %all-to-all-done.5 = f32[8,64,256]{2,1,0:T(8,128)S(1)} async-done(((f32[8,64,256]{2,1,0:T(8,128)}), f32[8,64,256]{2,1,0:T(8,128)S(1)}, u32[]{:S(2)}, u32[]{:S(2)}) %all-to-all-start.5) | async-done | bytes 524320 | tf_op jit(solution)/shard_map/all_to_all | solution.py:128
  192.7 5.7 %all-to-all-start.4 = ((f32[16,48,256]{2,1,0:T(8,128)}), f32[16,48,256]{2,1,0:T(8,128)S(1)}, u32[]{:S(2)}, u32[]{:S(2)}) async-start(f32[16,48,256]{2,1,0:T(8,128)} %pad_maximum_fusion.6), calls=%async_computation.4 | async-start | bytes 1572864 | tf_op jit(solution)/shard_map/all_to_all | solution.py:128
  201.7 11.0 %all-to-all-done.4 = f32[16,48,256]{2,1,0:T(8,128)S(1)} async-done(((f32[16,48,256]{2,1,0:T(8,128)}), f32[16,48,256]{2,1,0:T(8,128)S(1)}, u32[]{:S(2)}, u32[]{:S(2)}) %all-to-all-start.4) | async-done | bytes 786464 | tf_op jit(solution)/shard_map/all_to_all | solution.py:128
  (120 shorter events, 35.6 us)
Async XLA Ops:
  2.7 56.9 %copy-start.7 = (s32[16,8]{0,1:T(8,128)S(1)}, s32[16,8]{0,1:T(8,128)}, u32[]{:S(2)}) copy-start(s32[16,8]{0,1:T(8,128)} %param.13) | copy-start | bytes 1540
  2.7 22.7 %all-to-all-start = ((f32[16,48,256]{2,1,0:T(8,128)}), f32[16,48,256]{2,1,0:T(8,128)S(1)}, u32[]{:S(2)}, u32[]{:S(2)}) async-start(f32[16,48,256]{2,1,0:T(8,128)} %pad_maximum_fusion.5), calls=%async_computation | async-start | bytes 1572864 | tf_op jit(solution)/shard_map/all_to_all | solution.py:128
  27.0 12.6 %all-to-all-start.1 = ((f32[8,64,256]{2,1,0:T(8,128)}), f32[8,64,256]{2,1,0:T(8,128)S(1)}, u32[]{:S(2)}, u32[]{:S(2)}) async-start(f32[8,64,256]{2,1,0:T(8,128)} %bitcast_select_fusion.2), calls=%async_computation.1 | async-start | bytes 1048576 | tf_op jit(solution)/shard_map/all_to_all | solution.py:128
  39.6 4.5 %collective-permute-start = (f32[272,256]{1,0:T(8,128)S(1)}, f32[272,256]{1,0:T(8,128)S(1)}, u32[]{:S(2)}, u32[]{:S(2)}) collective-permute-start(f32[272,256]{1,0:T(8,128)S(1)} %pad_maximum_fusion.7), channel_id=1, source_target_pairs={{0,1},{1,0},{2,3},{3,2},{4,5},{5,4},{6,7},{7,6},{8,9},{9,8},{10,11... | collective-permute-start | bytes 835592 | tf_op jit(solution)/shard_map/ppermute | solution.py:132
  44.1 37.4 %copy-start.2 = (f32[2,272,256]{2,1,0:T(8,128)}, f32[2,272,256]{2,1,0:T(8,128)S(1)}, u32[]{:S(2)}) copy-start(f32[2,272,256]{2,1,0:T(8,128)S(1)} %maximum_select_fusion.refs_0_) | copy-start | bytes 1671172
  44.1 14.7 %collective-permute-start.1 = (f32[256,512]{1,0:T(8,128)}, f32[256,512]{1,0:T(8,128)S(1)}, u32[]{:S(2)}, u32[]{:S(2)}) collective-permute-start(f32[256,512]{1,0:T(8,128)} %param.12), channel_id=1, source_target_pairs={{0,16},{16,32},{32,48},{48,0},{1,17},{17,33},{33,49},{49,1},{2,18}... | collective-permute-start | bytes 1572872 | tf_op jit(solution)/shard_map/ppermute | solution.py:137
  44.3 28.3 %collective-permute-start.4 = (f32[2,272,256]{2,1,0:T(8,128)S(1)}, f32[2,272,256]{2,1,0:T(8,128)}, u32[]{:S(2)}, u32[]{:S(2)}) collective-permute-start(f32[2,272,256]{2,1,0:T(8,128)S(1)} %maximum_select_fusion.refs_0_), channel_id=1, source_target_pairs={{0,4},{4,8},{8,12},{12,0},{1,5},{5,9},{9,13},{13,1},{2,6},{6,10},{... | collective-permute-start | bytes 1671176 | tf_op jit(solution)/shard_map/ppermute | solution.py:137
  44.3 28.3 %collective-permute-start.5 = (f32[2,272,256]{2,1,0:T(8,128)S(1)}, f32[2,272,256]{2,1,0:T(8,128)}, u32[]{:S(2)}, u32[]{:S(2)}) collective-permute-start(f32[2,272,256]{2,1,0:T(8,128)S(1)} %maximum_select_fusion.refs_0_), channel_id=1, source_target_pairs={{0,12},{4,0},{8,4},{12,8},{1,13},{5,1},{9,5},{13,9},{2,14},{6,2},{... | collective-permute-start | bytes 1671176 | tf_op jit(solution)/shard_map/ppermute | solution.py:137
  47.0 25.6 %collective-permute-start.6 = (f32[2,272,256]{2,1,0:T(8,128)S(1)}, f32[2,272,256]{2,1,0:T(8,128)S(1)}, u32[]{:S(2)}, u32[]{:S(2)}) collective-permute-start(f32[2,272,256]{2,1,0:T(8,128)S(1)} %maximum_select_fusion.refs_0_), channel_id=1, source_target_pairs={{0,2},{2,0},{1,3},{3,1},{4,6},{6,4},{5,7},{7,5},{8,10},{10,8},{9,1... | collective-permute-start | bytes 1671176 | tf_op jit(solution)/shard_map/ppermute | solution.py:132
  48.6 12.4 %collective-permute-start.2 = (f32[256,512]{1,0:T(8,128)}, f32[256,512]{1,0:T(8,128)S(1)}, u32[]{:S(2)}, u32[]{:S(2)}) collective-permute-start(f32[256,512]{1,0:T(8,128)} %param.12), channel_id=1, source_target_pairs={{0,48},{16,0},{32,16},{48,32},{1,49},{17,1},{33,17},{49,33},{2,50}... | collective-permute-start | bytes 1572872 | tf_op jit(solution)/shard_map/ppermute | solution.py:137
  58.9 13.7 %collective-permute-start.3 = (f32[256,512]{1,0:T(8,128)}, f32[256,512]{1,0:T(8,128)S(1)}, u32[]{:S(2)}, u32[]{:S(2)}) collective-permute-start(f32[256,512]{1,0:T(8,128)} %param.12), channel_id=1, source_target_pairs={{0,64},{64,0},{1,65},{65,1},{2,66},{66,2},{3,67},{67,3},{4,68},{68... | collective-permute-start | bytes 1572872 | tf_op jit(solution)/shard_map/ppermute | solution.py:132
  72.8 18.9 %collective-permute-start.7 = (f32[384,512]{1,0:T(8,128)S(1)}, f32[384,512]{1,0:T(8,128)S(1)}, u32[]{:S(2)}, u32[]{:S(2)}) collective-permute-start(f32[384,512]{1,0:T(8,128)S(1)} %get-tuple-element.75), channel_id=1, source_target_pairs={{0,16},{16,32},{32,48},{48,0},{1,17},{17,33},{33,49},{49,1},{2,18}... | collective-permute-start | bytes 2359304 | tf_op jit(solution)/shard_map/ppermute | solution.py:137
  72.9 18.8 %collective-permute-start.8 = (f32[384,512]{1,0:T(8,128)S(1)}, f32[384,512]{1,0:T(8,128)S(1)}, u32[]{:S(2)}, u32[]{:S(2)}) collective-permute-start(f32[384,512]{1,0:T(8,128)S(1)} %get-tuple-element.74), channel_id=1, source_target_pairs={{0,48},{16,0},{32,16},{48,32},{1,49},{17,1},{33,17},{49,33},{2,50}... | collective-permute-start | bytes 2359304 | tf_op jit(solution)/shard_map/ppermute | solution.py:137
  77.7 19.4 %collective-permute-start.9 = (f32[3,272,256]{2,1,0:T(8,128)S(1)}, f32[3,272,256]{2,1,0:T(8,128)S(1)}, u32[]{:S(2)}, u32[]{:S(2)}) collective-permute-start(f32[3,272,256]{2,1,0:T(8,128)S(1)} %get-tuple-element.73), channel_id=1, source_target_pairs={{0,4},{4,8},{8,12},{12,0},{1,5},{5,9},{9,13},{13,1},{2,6},{6,10},{... | collective-permute-start | bytes 2506760 | tf_op jit(solution)/shard_map/ppermute | solution.py:137
  77.8 19.3 %collective-permute-start.10 = (f32[3,272,256]{2,1,0:T(8,128)S(1)}, f32[3,272,256]{2,1,0:T(8,128)S(1)}, u32[]{:S(2)}, u32[]{:S(2)}) collective-permute-start(f32[3,272,256]{2,1,0:T(8,128)S(1)} %get-tuple-element.72), channel_id=1, source_target_pairs={{0,12},{4,0},{8,4},{12,8},{1,13},{5,1},{9,5},{13,9},{2,14},{6,2},{... | collective-permute-start | bytes 2506760 | tf_op jit(solution)/shard_map/ppermute | solution.py:137
  97.2 5.3 %collective-permute-start.12 = (f32[128,512]{1,0:T(8,128)S(1)}, f32[128,512]{1,0:T(8,128)S(1)}, u32[]{:S(2)}, u32[]{:S(2)}) collective-permute-start(f32[128,512]{1,0:T(8,128)S(1)} %get-tuple-element.70), channel_id=1, source_target_pairs={{0,48},{16,0},{32,16},{48,32},{1,49},{17,1},{33,17},{49,33},{2,50}... | collective-permute-start | bytes 786440 | tf_op jit(solution)/shard_map/ppermute | solution.py:137
  97.3 6.5 %collective-permute-start.11 = (f32[128,512]{1,0:T(8,128)S(1)}, f32[128,512]{1,0:T(8,128)S(1)}, u32[]{:S(2)}, u32[]{:S(2)}) collective-permute-start(f32[128,512]{1,0:T(8,128)S(1)} %get-tuple-element.68), channel_id=1, source_target_pairs={{0,16},{16,32},{32,48},{48,0},{1,17},{17,33},{33,49},{49,1},{2,18}... | collective-permute-start | bytes 786440 | tf_op jit(solution)/shard_map/ppermute | solution.py:137
  106.2 14.1 %collective-permute-start.13 = (f32[8,256,256]{2,1,0:T(8,128)S(1)}, f32[8,256,256]{2,1,0:T(8,128)}, u32[]{:S(2)}, u32[]{:S(2)}) collective-permute-start(f32[8,256,256]{2,1,0:T(8,128)S(1)} %slice_select_fusion), channel_id=1, source_target_pairs={{0,1},{1,0},{2,3},{3,2},{4,5},{5,4},{6,7},{7,6},{8,9},{9,8},{10,11... | collective-permute-start | bytes 6291464 | tf_op jit(solution)/shard_map/ppermute | solution.py:132
  110.7 9.5 %collective-permute-start.14 = (f32[1,272,256]{2,1,0:T(8,128)S(1)}, f32[1,272,256]{2,1,0:T(8,128)S(1)}, u32[]{:S(2)}, u32[]{:S(2)}) collective-permute-start(f32[1,272,256]{2,1,0:T(8,128)S(1)} %slice.72), channel_id=1, source_target_pairs={{0,4},{4,8},{8,12},{12,0},{1,5},{5,9},{9,13},{13,1},{2,6},{6,10},{... | collective-permute-start | bytes 835592 | tf_op jit(solution)/shard_map/ppermute | solution.py:137
  110.8 9.4 %collective-permute-start.15 = (f32[1,272,256]{2,1,0:T(8,128)S(1)}, f32[1,272,256]{2,1,0:T(8,128)S(1)}, u32[]{:S(2)}, u32[]{:S(2)}) collective-permute-start(f32[1,272,256]{2,1,0:T(8,128)S(1)} %slice.73), channel_id=1, source_target_pairs={{0,12},{4,0},{8,4},{12,8},{1,13},{5,1},{9,5},{13,9},{2,14},{6,2},{... | collective-permute-start | bytes 835592 | tf_op jit(solution)/shard_map/ppermute | solution.py:137
  154.3 25.0 %all-to-all-start.3 = ((f32[16,80,256]{2,1,0:T(8,128)}), f32[16,80,256]{2,1,0:T(8,128)S(1)}, u32[]{:S(2)}, u32[]{:S(2)}) async-start(f32[16,80,256]{2,1,0:T(8,128)} %bitcast.47), calls=%async_computation.3 | async-start | bytes 2621440 | tf_op jit(solution)/shard_map/all_to_all | solution.py:128
  180.9 11.8 %all-to-all-start.5 = ((f32[8,64,256]{2,1,0:T(8,128)}), f32[8,64,256]{2,1,0:T(8,128)S(1)}, u32[]{:S(2)}, u32[]{:S(2)}) async-start(f32[8,64,256]{2,1,0:T(8,128)} %bitcast_select_fusion), calls=%async_computation.5 | async-start | bytes 1048576 | tf_op jit(solution)/shard_map/all_to_all | solution.py:128
  192.7 19.9 %all-to-all-start.4 = ((f32[16,48,256]{2,1,0:T(8,128)}), f32[16,48,256]{2,1,0:T(8,128)S(1)}, u32[]{:S(2)}, u32[]{:S(2)}) async-start(f32[16,48,256]{2,1,0:T(8,128)} %pad_maximum_fusion.6), calls=%async_computation.4 | async-start | bytes 1572864 | tf_op jit(solution)/shard_map/all_to_all | solution.py:128
  198.4 1.6 collective-permute-start.16
  (10 other events, 131.6 us)

commit v3 on v2

v3 whole, which is shorter than its diff:
```python
import functools

import jax
import jax.numpy as jnp
from jax import lax
from jax.experimental import pallas as pl
from jax.experimental.pallas import tpu as pltpu
from jax.sharding import Mesh, PartitionSpec as P

NEXT, RING, LINE, ACROSS, CORES = "next", "ring", "x", "across", "core"
ROWS = (NEXT, RING)
CHIPS = (LINE, ACROSS)
SIDE = (*CHIPS, CORES)


def split(x):
    high = x.astype(jnp.bfloat16)
    return high, (x - high.astype(jnp.float32)).astype(jnp.bfloat16)


def product(a, b, a_dim=1, b_dim=0):
    (ah, al), (bh, bl) = split(a), split(b)
    left = jnp.concatenate([ah, ah, al], axis=a_dim)
    right = jnp.concatenate([bh, bl, bh], axis=b_dim)
    dims = (((a_dim,), (b_dim,)), ((), ()))
    return lax.dot_general(left, right, dims, preferred_element_type=jnp.float32)


ROUTE = (
    ((0, 0, 0), (0, 0, 1)),
    ((-1, 0, 0), (-1, 0, 1)),
    ((1, 0, 0), (1, 0, 1)),
    ((0, 1, 0), (0, 1, 1)),
    ((-1, 1, 0), (-1, 1, 1), (2, 0, 0)),
    ((1, 1, 0), (1, 1, 1), (2, 0, 1)),
    ((2, 1, 0),),
    ((2, 1, 1),),
)
PLACES = ((0, 0), (-1, 0), (1, 0), (0, 1), (-1, 1), (1, 1), (2, 0), (2, 1))


def kernel(info, *refs):
    arrivals, refs = refs[: len(ROUTE)], refs[len(ROUTE) :]
    given, refs = refs[:3], refs[3:]
    lows, refs = refs[: len(ROUTE)], refs[len(ROUTE) :]
    pivot, keep, give, second, parts, total, left, right, low_done, left_done = refs
    slots, width = left.shape[0], left.shape[-1]

    low_copies = []
    for ref, entries in zip(lows, ROUTE):
        for n, (along, beside, part) in enumerate(entries):
            col = 2 * info[20 + PLACES.index((along, beside))] + part
            done = low_done.at[len(low_copies)]
            low_copies.append(pltpu.make_async_copy(ref.at[n], right.at[:, col], done))
    left_copies = [[] for _ in range(slots)]
    parts_of = width // 2
    for which, (ref, entries) in enumerate(zip(arrivals, ROUTE)):
        for n, (along, beside, part) in enumerate(entries):
            t = PLACES.index((along, beside))
            half = pl.ds(pl.multiple_of(info[t] * width, width), width)
            source = ref.at[pl.ds(n * parts_of, parts_of), half]
            target = left.at[t, pl.ds(part * parts_of, parts_of)]
            left_copies[t].append(pltpu.make_async_copy(source, target, left_done.at[t, part]))
    for t in range(slots):
        group = 0 if t < 4 else 1 if t < 7 else 2
        source = given[group].at[t - (0, 4, 7)[group]]
        left_copies[t].append(pltpu.make_async_copy(source, left.at[t, pl.ds(width, width)], left_done.at[t, 2]))
    for copy in low_copies:
        copy.start()
    for copies in left_copies:
        for copy in copies:
            copy.start()
    for copy in low_copies:
        copy.wait()

    def low(row):
        return [right[2 * row + n].reshape(width, width) for n in range(2)]

    for t in range(slots):
        for copy in left_copies[t]:
            copy.wait()
        term = product(left[t], jnp.concatenate(low(info[12 + t]), axis=1))
        if t == 0:
            total[...] = term
        else:
            total[...] += term

    upper = right[2 * slots].reshape(width, width)
    one = total[:, :width]
    two = product(one, upper) - total[:, width:]
    keep[0] = -one[:width]
    give[0] = -one[width:]
    core = info[11]
    tiles = (second.shape[0], second.shape[2], width)
    second[:, core] = two[:width].reshape(tiles)
    second[:, 1 - core] = two[width:].reshape(tiles)
    away = info[8] > 0
    slot_one = jnp.where(away, -one[width:], -one[:width])
    slot_two = jnp.where(away, two[width:], two[:width])
    low_one, low_two = low(info[10])
    here = jnp.where(info[9] > 0, pivot[0], jnp.zeros_like(slot_one))
    diag = here - product(low_one, slot_one, 0, 0)
    cross = product(diag, upper) + product(slot_one, low_two, 0, 0)
    last = product(upper, cross, 0, 0) - product(low_two, slot_two, 0, 0)
    pieces, tall = parts.shape[0], parts.shape[1] // 3
    for n, term in enumerate((diag, cross, last)):
        parts[:, n * tall : (n + 1) * tall, :] = term.reshape(pieces, tall, width)


def level_blocks(info, arrivals, given, lows, pivot):
    width = pivot.shape[-1]
    slots = len(PLACES)
    pieces = slots
    cols = 2 * slots
    f32 = jnp.float32
    whole = lambda *shape: pl.BlockSpec(shape, lambda i, s: (0,) * len(shape))
    grid_spec = pltpu.PrefetchScalarGridSpec(
        num_scalar_prefetch=1,
        grid=(1,),
        in_specs=[pl.BlockSpec(memory_space=pl.ANY)] * (2 * len(ROUTE) + 3) + [whole(1, width, width)],
        out_specs=[
            whole(1, width, width),
            whole(1, width, width),
            whole(slots, 2, width // slots, width),
            whole(pieces, 3 * width // pieces, width),
        ],
        scratch_shapes=[
            pltpu.VMEM((2 * width, 2 * width), f32),
            pltpu.VMEM((slots, 2 * width, width), f32),
            pltpu.VMEM((2 * slots + 1, cols, width // cols, width), f32),
            pltpu.SemaphoreType.DMA((cols,)),
            pltpu.SemaphoreType.DMA((slots, 3)),
        ],
    )
    return pl.pallas_call(
        kernel,
        grid_spec=grid_spec,
        out_shape=[
            jax.ShapeDtypeStruct((1, width, width), f32),
            jax.ShapeDtypeStruct((1, width, width), f32),
            jax.ShapeDtypeStruct((slots, 2, width // slots, width), f32),
            jax.ShapeDtypeStruct((pieces, 3 * width // pieces, width), f32),
        ],
        compiler_params=pltpu.CompilerParams(vmem_limit_bytes=60 << 20),
        cost_estimate=pl.CostEstimate(flops=10_000_000_000, bytes_accessed=12_000_000, transcendentals=0),
    )(info, *arrivals, *given, *lows, pivot)


def exchange(x, axis):
    return lax.all_to_all(x, axis, split_axis=0, concat_axis=0, tiled=True)


def swap(x, axis=CORES):
    return lax.ppermute(x, axis, [(0, 1), (1, 0)])


def shift(x, axis, by):
    n = lax.axis_size(axis)
    return lax.ppermute(x, axis, [(i, (i + by) % n) for i in range(n)])


def go_round(*ways):
    hold = lax.optimization_barrier
    owns = hold(tuple(own for own, _, _ in ways))
    near = []
    for own, (_, line, neighbour) in zip(owns, ways):
        near.append((shift(own, line, 1), shift(own, line, -1), swap(own, neighbour)))
    near = hold(near)
    far = []
    for (below, above, beside), (_, line, _) in zip(near, ways):
        half = below.shape[0] // 2
        up = shift(jnp.concatenate([beside, below[:half]]), line, 1)
        down = shift(jnp.concatenate([beside, above[half:]]), line, -1)
        far.append((up, down))
    far = hold(far)
    ends = []
    for (up, down), (own, line, _) in zip(far, ways):
        half = own.shape[0] // 2
        ends.append((shift(up[:half], line, 1), shift(down[half : 2 * half], line, -1)))
    return [(own, *n, *f, *e) for own, n, f, e in zip(owns, near, far, ends)]


def body(anc, pattern, parents, low_one, pivot_one, low_two, factor, pivot_two):
    row, line, across, core = (lax.axis_index(a) for a in (ROWS, LINE, ACROSS, CORES))
    half = lax.axis_index(NEXT)
    rows, lines, pair, cores = (lax.axis_size(a) for a in (ROWS, LINE, ACROSS, CORES))
    chips = lines * pair
    cols = chips * cores
    width = pivot_one.shape[-1]
    piece = width // cols
    chip = line * pair + across
    col = chip * cores + core
    kind = jnp.arange(cols, dtype=jnp.int32)
    children = jnp.sum(jnp.where(parents[None, :] == kind[:, None], kind[None, :], 0), axis=1)

    flat = [x.reshape(cols, piece, width) for x in (low_one, low_two, factor)]
    pieces = exchange(jnp.concatenate(flat, axis=1), SIDE).reshape(3 * cols, piece, width)
    order = jnp.stack([3 * kind, 3 * children + 1], axis=1).reshape(-1)
    routed = jnp.take(pieces, order, axis=0).reshape(rows, cores * 2 * piece, width)
    own_children = lax.dynamic_slice_in_dim(children, row * cores, cores)
    uppers = jnp.take(pieces, 3 * own_children + 2, axis=0)
    upper = swap(lax.dynamic_index_in_dim(uppers, 1 - core, 0))
    kept = lax.dynamic_index_in_dim(uppers, core, 0)
    uppers = jnp.where(core == 0, jnp.stack([kept, upper]), jnp.stack([upper, kept]))
    mine = exchange(routed.reshape(cols, 2 * piece, width), (*ROWS, CORES))
    mine = mine.reshape(rows, cores, 2, piece, width).transpose(1, 0, 2, 3, 4)
    both = jnp.concatenate([mine.reshape(cores, rows * 2, piece, width), uppers], axis=1)

    inverse, lows = go_round((anc, RING, NEXT), (both, LINE, ACROSS))
    ring = lax.axis_index(RING)
    lengths = lax.axis_size(RING)
    slot = jnp.stack([(half ^ n) * lengths + (ring + m) % lengths for m, n in PLACES])
    places = jnp.stack([(line + m) % lines * pair + (across ^ n) for m, n in PLACES])
    here = jnp.take(pattern, row * cores + core, axis=0)
    there = jnp.take(pattern, row * cores + 1 - core, axis=0)
    picks = jnp.take(there, slot) % 2 > 0

    def handed(first, *blocks):
        picked = [jnp.where(picks[first + n], x[:, width:], x[:, :width]) for n, x in enumerate(blocks)]
        return swap(jnp.stack(picked))

    own, below, above, beside, up, down, low_far, high_far = inverse
    given = (
        handed(0, own, below, above, beside),
        handed(4, up[:width], down[:width], jnp.concatenate([up[width:], down[width:]])),
        handed(7, jnp.concatenate([low_far, high_far])),
    )
    away = jnp.take(here, chip) != col
    flags = jnp.stack([away.astype(jnp.int32), (chip == row).astype(jnp.int32), chip, core])
    info = jnp.concatenate([jnp.take(here, slot) % 2, flags, slot, places])
    keep, give, second, parts = level_blocks(info, inverse, given, lows, pivot_one)
    taken = swap(give)
    column_one = jnp.where(core == 0, jnp.concatenate([keep, taken]), jnp.concatenate([taken, keep]))

    summed = jnp.sum(exchange(parts, CHIPS), axis=0)
    halves = summed.reshape(3, cores, piece, width).transpose(1, 0, 2, 3).reshape(1, cores, 3 * piece, width)
    halves = jnp.broadcast_to(halves, (rows, *halves.shape[1:]))
    send = jnp.concatenate([halves, second], axis=2).reshape(cols, -1, width)
    known = exchange(send, (*ROWS, CORES))
    column_two = jnp.take(known[:, 3 * piece :], parents, axis=0)
    column_two = exchange(column_two.reshape(rows, -1, width), ROWS)
    column_two = column_two.reshape(rows, cores, -1, width).transpose(1, 0, 2, 3)
    known = known.reshape(cols, -1, piece, width)
    blocks = [known[:, 0], jnp.take(known[:, 1:3], parents, axis=0).reshape(cols, -1, width)]
    final = exchange(jnp.concatenate(blocks, axis=1), SIDE)
    final = final.reshape(cols, 3, piece, width)
    diag_one, cross, last = (final[:, n].reshape(1, width, width) for n in range(3))
    return column_one, diag_one, column_two.reshape(cores, width, width), -cross, pivot_two + last


def solution(mesh):
    rows, cols = mesh.devices.shape
    cut = Mesh(mesh.devices.reshape(2, rows // 2, cols // 4, 2, 2), (*ROWS, *SIDE))
    flat, wide = P(SIDE, None, None), P(SIDE, ROWS, None)
    return jax.shard_map(
        body,
        mesh=cut,
        in_specs=(P(SIDE, ROWS), P(), P(), wide, flat, wide, flat, flat),
        out_specs=(P(ROWS, SIDE, None), flat, P(ROWS, SIDE, None), flat, flat),
        check_vma=False,
    )
```

time: 215 us -> 204 us (0.949)
  waiting for transfers between devices: 102 us -> 89.4 us
  other arithmetic: 11.7 us -> 16.3 us
  local copies, waits for them, and re-layouts: 12.7 us -> 10.2 us
    ppermute x12, waiting for transfers between devices: 33 us -> 19.2 us  [shift(): return lax.ppermute(x, axis, [(i, (i + by) % n) for i in range(n)])]
    another operation x2 -> x10, other arithmetic: 0.05 us -> 6.6 us  [handed(): return swap(jnp.stack(picked))]
    ppermute x5 -> x7, waiting for transfers between devices: 14.1 us -> 12.9 us  [swap(): return lax.ppermute(x, axis, [(0, 1), (1, 0)])]
    ppermute x5 -> x7, starting transfers between devices: 10.5 us -> 10.1 us  [swap(): return lax.ppermute(x, axis, [(0, 1), (1, 0)])]
  transfers between devices with their start and end apart: 22 -> 24, of which waited for: 15 -> 11; matrix products, arithmetic and copies ran while one was open for 6% -> 8% of each run, Pallas kernels for 0% -> 0%
where the time goes in v3:
time: 204 us; the launch traced here: 203 us
  waiting for transfers between devices  89.4 us (44%)
  starting transfers between devices  56.5 us (28%)
  blocking collectives  17 us (8%)
  other arithmetic  16.3 us (8%)
  Pallas kernels  11.5 us (6%)
  local copies, waits for them, and re-layouts  10.2 us (5%)
    all_to_all x5, waiting for transfers between devices, exchange(): return lax.all_to_all(x, axis, split_axis=0, concat_axis=0, tiled=True)  57.3 us
    all_to_all x5, starting transfers between devices, exchange(): return lax.all_to_all(x, axis, split_axis=0, concat_axis=0, tiled=True)  31.1 us
    ppermute x12, waiting for transfers between devices, shift(): return lax.ppermute(x, axis, [(i, (i + by) % n) for i in range(n)])  19.2 us
    all_to_all x1, blocking collectives, exchange(): return lax.all_to_all(x, axis, split_axis=0, concat_axis=0, tiled=True)  17 us
    ppermute x12, starting transfers between devices, shift(): return lax.ppermute(x, axis, [(i, (i + by) % n) for i in range(n)])  15.3 us
    ppermute x7, waiting for transfers between devices, swap(): return lax.ppermute(x, axis, [(0, 1), (1, 0)])  12.9 us
    pallas_call x1, Pallas kernels, level_blocks(): pl.pallas_call(kernel, grid_spec=grid_spec, out_shape=[jax.ShapeDtypeStru...  11.5 us
    ppermute x7, starting transfers between devices, swap(): return lax.ppermute(x, axis, [(0, 1), (1, 0)])  10.1 us
  transfers between devices with their start and end apart: 24, of which 11 were waited for; matrix products, arithmetic and copies ran while one was open for 8% of the time, Pallas kernels for 0%

profile of v3, /device:TPU:1, one launch (start us, length us, event | category | flops | bytes accessed | tf_op | source)
XLA Modules:
  0.0 202.8 jit_solution(7381550303464745785)
XLA Ops:
  0.6 2.1 %pad_maximum_fusion.6 = f32[16,48,256]{2,1,0:T(8,128)} fusion(f32[16,16,256]{2,1,0:T(8,128)} %bitcast.102, f32[16,16,256]{2,1,0:T(8,128)} %bitcast.103, f32[16,16,256]{2,1,0:T(8,128)} %bitcast.104), kind=kLoop, calls=%fused_computation.12 | loop fusion | flops 393216 | bytes 1572864 | tf_op jit(solution)/shard_map/concatenate | solution.py:197
  2.7 8.4 %all-to-all-start = ((f32[16,48,256]{2,1,0:T(8,128)}), f32[16,48,256]{2,1,0:T(8,128)S(1)}, u32[]{:S(2)}, u32[]{:S(2)}) async-start(f32[16,48,256]{2,1,0:T(8,128)} %pad_maximum_fusion.6), calls=%async_computation | async-start | bytes 1572864 | tf_op jit(solution)/shard_map/all_to_all | solution.py:150
  11.7 13.6 %all-to-all-done = f32[16,48,256]{2,1,0:T(8,128)S(1)} async-done(((f32[16,48,256]{2,1,0:T(8,128)}), f32[16,48,256]{2,1,0:T(8,128)S(1)}, u32[]{:S(2)}, u32[]{:S(2)}) %all-to-all-start) | async-done | bytes 786464 | tf_op jit(solution)/shard_map/all_to_all | solution.py:150
  26.8 6.6 %all-to-all-start.1 = ((f32[16,32,256]{2,1,0:T(8,128)}), f32[16,32,256]{2,1,0:T(8,128)S(1)}, u32[]{:S(2)}, u32[]{:S(2)}) async-start(f32[16,32,256]{2,1,0:T(8,128)} %bitcast_select_fusion.2), calls=%async_computation.1 | async-start | bytes 1048576 | tf_op jit(solution)/shard_map/all_to_all | solution.py:150
  35.3 7.9 %all-to-all-done.1 = f32[16,32,256]{2,1,0:T(8,128)S(1)} async-done(((f32[16,32,256]{2,1,0:T(8,128)}), f32[16,32,256]{2,1,0:T(8,128)S(1)}, u32[]{:S(2)}, u32[]{:S(2)}) %all-to-all-start.1) | async-done | bytes 524320 | tf_op jit(solution)/shard_map/all_to_all | solution.py:150
  44.5 2.7 %collective-permute-start.5 = (f32[2,17,16,256]{3,2,1,0:T(8,128)S(1)}, f32[2,17,16,256]{3,2,1,0:T(8,128)S(1)}, u32[]{:S(2)}, u32[]{:S(2)}) collective-permute-start(f32[2,17,16,256]{3,2,1,0:T(8,128)S(1)} %pad_maximum_fusion.9.refs_11_), channel_id=1, source_target_pairs={{0,12},{4,0},{8,4},{12,8},{1,13},{5,1},{9,5},{13,9},{2,14},{6,2},{... | collective-permute-start | bytes 1671176 | tf_op jit(solution)/shard_map/ppermute | solution.py:159
  47.9 2.6 %collective-permute-start.2 = (f32[256,512]{1,0:T(8,128)}, f32[256,512]{1,0:T(8,128)S(1)}, u32[]{:S(2)}, u32[]{:S(2)}) collective-permute-start(f32[256,512]{1,0:T(8,128)} %refs_0_), channel_id=1, source_target_pairs={{0,48},{16,0},{32,16},{48,32},{1,49},{17,1},{33,17},{49,33},{2,50}... | collective-permute-start | bytes 1572872 | tf_op jit(solution)/shard_map/ppermute | solution.py:159
  50.5 6.5 %collective-permute-done.1.refs_1_ = f32[256,512]{1,0:T(8,128)S(1)} collective-permute-done((f32[256,512]{1,0:T(8,128)}, f32[256,512]{1,0:T(8,128)S(1)}, u32[]{:S(2)}, u32[]{:S(2)}) %collective-permute-start.1) | collective-permute-done | bytes 524320 | tf_op jit(solution)/shard_map/ppermute | solution.py:159
  60.7 10.5 %collective-permute-done.3.refs_3_ = f32[256,512]{1,0:T(8,128)S(1)} collective-permute-done((f32[256,512]{1,0:T(8,128)}, f32[256,512]{1,0:T(8,128)S(1)}, u32[]{:S(2)}, u32[]{:S(2)}) %collective-permute-start.3) | collective-permute-done | bytes 524320 | tf_op jit(solution)/shard_map/ppermute | solution.py:154
  75.0 2.2 %collective-permute-start.8 = (f32[384,512]{1,0:T(8,128)S(1)}, f32[384,512]{1,0:T(8,128)S(1)}, u32[]{:S(2)}, u32[]{:S(2)}) collective-permute-start(f32[384,512]{1,0:T(8,128)S(1)} %get-tuple-element.74), channel_id=1, source_target_pairs={{0,48},{16,0},{32,16},{48,32},{1,49},{17,1},{33,17},{49,33},{2,50}... | collective-permute-start | bytes 2359304 | tf_op jit(solution)/shard_map/ppermute | solution.py:159
  79.4 2.8 %collective-permute-start.13 = (f32[4,256,256]{2,1,0:T(8,128)S(1)}, f32[4,256,256]{2,1,0:T(8,128)}, u32[]{:S(2)}, u32[]{:S(2)}) collective-permute-start(f32[4,256,256]{2,1,0:T(8,128)S(1)} %pad_maximum_fusion.1), channel_id=1, source_target_pairs={{0,1},{1,0},{2,3},{3,2},{4,5},{5,4},{6,7},{7,6},{8,9},{9,8},{10,11... | collective-permute-start | bytes 3145736 | tf_op jit(solution)/shard_map/ppermute | solution.py:154
  82.2 10.3 %collective-permute-done.7.refs_4_ = f32[384,512]{1,0:T(8,128)S(1)} collective-permute-done((f32[384,512]{1,0:T(8,128)S(1)}, f32[384,512]{1,0:T(8,128)S(1)}, u32[]{:S(2)}, u32[]{:S(2)}) %collective-permute-start.7) | collective-permute-done | bytes 786464 | tf_op jit(solution)/shard_map/ppermute | solution.py:159
  92.8 2.7 %collective-permute-start.12 = (f32[128,512]{1,0:T(8,128)S(1)}, f32[128,512]{1,0:T(8,128)S(1)}, u32[]{:S(2)}, u32[]{:S(2)}) collective-permute-start(f32[128,512]{1,0:T(8,128)S(1)} %get-tuple-element.69), channel_id=1, source_target_pairs={{0,48},{16,0},{32,16},{48,32},{1,49},{17,1},{33,17},{49,33},{2,50}... | collective-permute-start | bytes 786440 | tf_op jit(solution)/shard_map/ppermute | solution.py:159
  97.6 3.8 %collective-permute-start.14 = (f32[3,256,256]{2,1,0:T(8,128)S(1)}, f32[3,256,256]{2,1,0:T(8,128)}, u32[]{:S(2)}, u32[]{:S(2)}) collective-permute-start(f32[3,256,256]{2,1,0:T(8,128)S(1)} %pad_maximum_fusion.7), channel_id=1, source_target_pairs={{0,1},{1,0},{2,3},{3,2},{4,5},{5,4},{6,7},{7,6},{8,9},{9,8},{10,11... | collective-permute-start | bytes 2359304 | tf_op jit(solution)/shard_map/ppermute | solution.py:154
  101.5 2.7 %collective-permute-start.17 = (f32[1,17,16,256]{3,2,1,0:T(8,128)S(1)}, f32[1,17,16,256]{3,2,1,0:T(8,128)}, u32[]{:S(2)}, u32[]{:S(2)}) collective-permute-start(f32[1,17,16,256]{3,2,1,0:T(8,128)S(1)} %slice.159), channel_id=1, source_target_pairs={{0,12},{4,0},{8,4},{12,8},{1,13},{5,1},{9,5},{13,9},{2,14},{6,2},{... | collective-permute-start | bytes 835592 | tf_op jit(solution)/shard_map/ppermute | solution.py:159
  108.6 2.3 %collective-permute-done.16.refs_17_ = f32[1,17,16,256]{3,2,1,0:T(8,128)S(1)} collective-permute-done((f32[1,17,16,256]{3,2,1,0:T(8,128)S(1)}, f32[1,17,16,256]{3,2,1,0:T(8,128)S(1)}, u32[]{:S(2)}, u32[]{:S(2)}) %collective-permute-start.16) | collective-permute-done | bytes 278560 | tf_op jit(solution)/shard_map/ppermute | solution.py:159
  111.7 11.5 %shard_map.119 = (f32[1,256,256]{2,1,0:T(8,128)}, f32[1,256,256]{2,1,0:T(8,128)}, f32[8,2,32,256]{3,2,1,0:T(8,128)}, f32[8,96,256]{2,1,0:T(8,128)}) custom-call(s32[28]{0:T(128)} %concatenate.56.info, f32[256,512]{1,0:T(8,128)} %refs_0_, f32[256,512]{1,0:T(8,128)} %copy-done.3, f32[256,512]{1,0:T(8,128)} %copy-done.4, f32[256,512]{1,0:T(8,128)} %copy-done, ...), custom_call_target="tpu_custom_call" | custom-call | flops 10000000000 | bytes 12000000 | tf_op jit(solution)/shard_map/pallas_call | solution.py:135
  123.1 17.0 %all_to_all.30 = f32[8,96,256]{2,1,0:T(8,128)S(1)} all-to-all(f32[8,96,256]{2,1,0:T(8,128)} %get-tuple-element.37), channel_id=1, replica_groups=mesh['next'=2,'ring'=4,'x'=4,'across'=2,'core'=2] {'x','across'}, dimensions={0} | all-to-all | bytes 1572864 | tf_op jit(solution)/shard_map/all_to_all | solution.py:150
  142.4 6.9 %all-to-all-start.3 = ((f32[16,80,256]{2,1,0:T(8,128)}), f32[16,80,256]{2,1,0:T(8,128)S(1)}, u32[]{:S(2)}, u32[]{:S(2)}) async-start(f32[16,80,256]{2,1,0:T(8,128)} %bitcast.54), calls=%async_computation.3 | async-start | bytes 2621440 | tf_op jit(solution)/shard_map/all_to_all | solution.py:150
  149.6 18.5 %all-to-all-done.3 = f32[16,80,256]{2,1,0:T(8,128)S(1)} async-done(((f32[16,80,256]{2,1,0:T(8,128)}), f32[16,80,256]{2,1,0:T(8,128)S(1)}, u32[]{:S(2)}, u32[]{:S(2)}) %all-to-all-start.3) | async-done | bytes 1310752 | tf_op jit(solution)/shard_map/all_to_all | solution.py:150
  169.6 3.6 %all-to-all-start.5 = ((f32[8,64,256]{2,1,0:T(8,128)}), f32[8,64,256]{2,1,0:T(8,128)S(1)}, u32[]{:S(2)}, u32[]{:S(2)}) async-start(f32[8,64,256]{2,1,0:T(8,128)} %bitcast_select_fusion), calls=%async_computation.5 | async-start | bytes 1048576 | tf_op jit(solution)/shard_map/all_to_all | solution.py:150
  175.0 6.4 %all-to-all-done.5 = f32[8,64,256]{2,1,0:T(8,128)S(1)} async-done(((f32[8,64,256]{2,1,0:T(8,128)}), f32[8,64,256]{2,1,0:T(8,128)S(1)}, u32[]{:S(2)}, u32[]{:S(2)}) %all-to-all-start.5) | async-done | bytes 524320 | tf_op jit(solution)/shard_map/all_to_all | solution.py:150
  181.3 5.7 %all-to-all-start.4 = ((f32[16,48,256]{2,1,0:T(8,128)}), f32[16,48,256]{2,1,0:T(8,128)S(1)}, u32[]{:S(2)}, u32[]{:S(2)}) async-start(f32[16,48,256]{2,1,0:T(8,128)} %pad_maximum_fusion.8), calls=%async_computation.4 | async-start | bytes 1572864 | tf_op jit(solution)/shard_map/all_to_all | solution.py:150
  190.3 11.0 %all-to-all-done.4 = f32[16,48,256]{2,1,0:T(8,128)S(1)} async-done(((f32[16,48,256]{2,1,0:T(8,128)}), f32[16,48,256]{2,1,0:T(8,128)S(1)}, u32[]{:S(2)}, u32[]{:S(2)}) %all-to-all-start.4) | async-done | bytes 786464 | tf_op jit(solution)/shard_map/all_to_all | solution.py:150
  (142 shorter events, 32.7 us)
Async XLA Ops:
  2.7 22.6 %all-to-all-start = ((f32[16,48,256]{2,1,0:T(8,128)}), f32[16,48,256]{2,1,0:T(8,128)S(1)}, u32[]{:S(2)}, u32[]{:S(2)}) async-start(f32[16,48,256]{2,1,0:T(8,128)} %pad_maximum_fusion.6), calls=%async_computation | async-start | bytes 1572864 | tf_op jit(solution)/shard_map/all_to_all | solution.py:150
  26.8 16.4 %all-to-all-start.1 = ((f32[16,32,256]{2,1,0:T(8,128)}), f32[16,32,256]{2,1,0:T(8,128)S(1)}, u32[]{:S(2)}, u32[]{:S(2)}) async-start(f32[16,32,256]{2,1,0:T(8,128)} %bitcast_select_fusion.2), calls=%async_computation.1 | async-start | bytes 1048576 | tf_op jit(solution)/shard_map/all_to_all | solution.py:150
  34.1 1.2 collective-permute-start
  43.3 13.7 %collective-permute-start.1 = (f32[256,512]{1,0:T(8,128)}, f32[256,512]{1,0:T(8,128)S(1)}, u32[]{:S(2)}, u32[]{:S(2)}) collective-permute-start(f32[256,512]{1,0:T(8,128)} %refs_0_), channel_id=1, source_target_pairs={{0,16},{16,32},{32,48},{48,0},{1,17},{17,33},{33,49},{49,1},{2,18}... | collective-permute-start | bytes 1572872 | tf_op jit(solution)/shard_map/ppermute | solution.py:159
  44.4 26.8 %collective-permute-start.4 = (f32[2,17,16,256]{3,2,1,0:T(8,128)S(1)}, f32[2,17,16,256]{3,2,1,0:T(8,128)S(1)}, u32[]{:S(2)}, u32[]{:S(2)}) collective-permute-start(f32[2,17,16,256]{3,2,1,0:T(8,128)S(1)} %pad_maximum_fusion.9.refs_11_), channel_id=1, source_target_pairs={{0,4},{4,8},{8,12},{12,0},{1,5},{5,9},{9,13},{13,1},{2,6},{6,10},{... | collective-permute-start | bytes 1671176 | tf_op jit(solution)/shard_map/ppermute | solution.py:159
  44.5 26.8 %collective-permute-start.5 = (f32[2,17,16,256]{3,2,1,0:T(8,128)S(1)}, f32[2,17,16,256]{3,2,1,0:T(8,128)S(1)}, u32[]{:S(2)}, u32[]{:S(2)}) collective-permute-start(f32[2,17,16,256]{3,2,1,0:T(8,128)S(1)} %pad_maximum_fusion.9.refs_11_), channel_id=1, source_target_pairs={{0,12},{4,0},{8,4},{12,8},{1,13},{5,1},{9,5},{13,9},{2,14},{6,2},{... | collective-permute-start | bytes 1671176 | tf_op jit(solution)/shard_map/ppermute | solution.py:159
  47.2 24.1 %collective-permute-start.6 = (f32[2,17,16,256]{3,2,1,0:T(8,128)S(1)}, f32[2,17,16,256]{3,2,1,0:T(8,128)S(1)}, u32[]{:S(2)}, u32[]{:S(2)}) collective-permute-start(f32[2,17,16,256]{3,2,1,0:T(8,128)S(1)} %pad_maximum_fusion.9.refs_11_), channel_id=1, source_target_pairs={{0,2},{2,0},{1,3},{3,1},{4,6},{6,4},{5,7},{7,5},{8,10},{10,8},{9,1... | collective-permute-start | bytes 1671176 | tf_op jit(solution)/shard_map/ppermute | solution.py:154
  47.9 12.8 %collective-permute-start.2 = (f32[256,512]{1,0:T(8,128)}, f32[256,512]{1,0:T(8,128)S(1)}, u32[]{:S(2)}, u32[]{:S(2)}) collective-permute-start(f32[256,512]{1,0:T(8,128)} %refs_0_), channel_id=1, source_target_pairs={{0,48},{16,0},{32,16},{48,32},{1,49},{17,1},{33,17},{49,33},{2,50}... | collective-permute-start | bytes 1572872 | tf_op jit(solution)/shard_map/ppermute | solution.py:159
  57.0 14.2 %collective-permute-start.3 = (f32[256,512]{1,0:T(8,128)}, f32[256,512]{1,0:T(8,128)S(1)}, u32[]{:S(2)}, u32[]{:S(2)}) collective-permute-start(f32[256,512]{1,0:T(8,128)} %refs_0_), channel_id=1, source_target_pairs={{0,64},{64,0},{1,65},{65,1},{2,66},{66,2},{3,67},{67,3},{4,68},{68... | collective-permute-start | bytes 1572872 | tf_op jit(solution)/shard_map/ppermute | solution.py:154
  72.7 19.9 %collective-permute-start.10 = (f32[3,17,16,256]{3,2,1,0:T(8,128)S(1)}, f32[3,17,16,256]{3,2,1,0:T(8,128)S(1)}, u32[]{:S(2)}, u32[]{:S(2)}) collective-permute-start(f32[3,17,16,256]{3,2,1,0:T(8,128)S(1)} %get-tuple-element.72), channel_id=1, source_target_pairs={{0,12},{4,0},{8,4},{12,8},{1,13},{5,1},{9,5},{13,9},{2,14},{6,2},{... | collective-permute-start | bytes 2506760 | tf_op jit(solution)/shard_map/ppermute | solution.py:159
  72.8 19.8 %collective-permute-start.9 = (f32[3,17,16,256]{3,2,1,0:T(8,128)S(1)}, f32[3,17,16,256]{3,2,1,0:T(8,128)S(1)}, u32[]{:S(2)}, u32[]{:S(2)}) collective-permute-start(f32[3,17,16,256]{3,2,1,0:T(8,128)S(1)} %get-tuple-element.73), channel_id=1, source_target_pairs={{0,4},{4,8},{8,12},{12,0},{1,5},{5,9},{9,13},{13,1},{2,6},{6,10},{... | collective-permute-start | bytes 2506760 | tf_op jit(solution)/shard_map/ppermute | solution.py:159
  74.4 18.1 %collective-permute-start.7 = (f32[384,512]{1,0:T(8,128)S(1)}, f32[384,512]{1,0:T(8,128)S(1)}, u32[]{:S(2)}, u32[]{:S(2)}) collective-permute-start(f32[384,512]{1,0:T(8,128)S(1)} %get-tuple-element.75), channel_id=1, source_target_pairs={{0,16},{16,32},{32,48},{48,0},{1,17},{17,33},{33,49},{49,1},{2,18}... | collective-permute-start | bytes 2359304 | tf_op jit(solution)/shard_map/ppermute | solution.py:159
  75.0 17.6 %collective-permute-start.8 = (f32[384,512]{1,0:T(8,128)S(1)}, f32[384,512]{1,0:T(8,128)S(1)}, u32[]{:S(2)}, u32[]{:S(2)}) collective-permute-start(f32[384,512]{1,0:T(8,128)S(1)} %get-tuple-element.74), channel_id=1, source_target_pairs={{0,48},{16,0},{32,16},{48,32},{1,49},{17,1},{33,17},{49,33},{2,50}... | collective-permute-start | bytes 2359304 | tf_op jit(solution)/shard_map/ppermute | solution.py:159
  79.4 29.2 %collective-permute-start.13 = (f32[4,256,256]{2,1,0:T(8,128)S(1)}, f32[4,256,256]{2,1,0:T(8,128)}, u32[]{:S(2)}, u32[]{:S(2)}) collective-permute-start(f32[4,256,256]{2,1,0:T(8,128)S(1)} %pad_maximum_fusion.1), channel_id=1, source_target_pairs={{0,1},{1,0},{2,3},{3,2},{4,5},{5,4},{6,7},{7,6},{8,9},{9,8},{10,11... | collective-permute-start | bytes 3145736 | tf_op jit(solution)/shard_map/ppermute | solution.py:154
  92.6 8.9 %collective-permute-start.11 = (f32[128,512]{1,0:T(8,128)S(1)}, f32[128,512]{1,0:T(8,128)S(1)}, u32[]{:S(2)}, u32[]{:S(2)}) collective-permute-start(f32[128,512]{1,0:T(8,128)S(1)} %get-tuple-element.71), channel_id=1, source_target_pairs={{0,16},{16,32},{32,48},{48,0},{1,17},{17,33},{33,49},{49,1},{2,18}... | collective-permute-start | bytes 786440 | tf_op jit(solution)/shard_map/ppermute | solution.py:159
  92.8 11.5 %collective-permute-start.12 = (f32[128,512]{1,0:T(8,128)S(1)}, f32[128,512]{1,0:T(8,128)S(1)}, u32[]{:S(2)}, u32[]{:S(2)}) collective-permute-start(f32[128,512]{1,0:T(8,128)S(1)} %get-tuple-element.69), channel_id=1, source_target_pairs={{0,48},{16,0},{32,16},{48,32},{1,49},{17,1},{33,17},{49,33},{2,50}... | collective-permute-start | bytes 786440 | tf_op jit(solution)/shard_map/ppermute | solution.py:159
  97.6 13.4 %collective-permute-start.14 = (f32[3,256,256]{2,1,0:T(8,128)S(1)}, f32[3,256,256]{2,1,0:T(8,128)}, u32[]{:S(2)}, u32[]{:S(2)}) collective-permute-start(f32[3,256,256]{2,1,0:T(8,128)S(1)} %pad_maximum_fusion.7), channel_id=1, source_target_pairs={{0,1},{1,0},{2,3},{3,2},{4,5},{5,4},{6,7},{7,6},{8,9},{9,8},{10,11... | collective-permute-start | bytes 2359304 | tf_op jit(solution)/shard_map/ppermute | solution.py:154
  101.4 9.5 %collective-permute-start.16 = (f32[1,17,16,256]{3,2,1,0:T(8,128)S(1)}, f32[1,17,16,256]{3,2,1,0:T(8,128)S(1)}, u32[]{:S(2)}, u32[]{:S(2)}) collective-permute-start(f32[1,17,16,256]{3,2,1,0:T(8,128)S(1)} %slice.158), channel_id=1, source_target_pairs={{0,4},{4,8},{8,12},{12,0},{1,5},{5,9},{9,13},{13,1},{2,6},{6,10},{... | collective-permute-start | bytes 835592 | tf_op jit(solution)/shard_map/ppermute | solution.py:159
  101.5 9.4 %collective-permute-start.17 = (f32[1,17,16,256]{3,2,1,0:T(8,128)S(1)}, f32[1,17,16,256]{3,2,1,0:T(8,128)}, u32[]{:S(2)}, u32[]{:S(2)}) collective-permute-start(f32[1,17,16,256]{3,2,1,0:T(8,128)S(1)} %slice.159), channel_id=1, source_target_pairs={{0,12},{4,0},{8,4},{12,8},{1,13},{5,1},{9,5},{13,9},{2,14},{6,2},{... | collective-permute-start | bytes 835592 | tf_op jit(solution)/shard_map/ppermute | solution.py:159
  105.0 5.9 %collective-permute-start.15 = (f32[1,256,256]{2,1,0:T(8,128)S(1)}, f32[1,256,256]{2,1,0:T(8,128)}, u32[]{:S(2)}, u32[]{:S(2)}) collective-permute-start(f32[1,256,256]{2,1,0:T(8,128)S(1)} %fusion.3), channel_id=1, source_target_pairs={{0,1},{1,0},{2,3},{3,2},{4,5},{5,4},{6,7},{7,6},{8,9},{9,8},{10,11... | collective-permute-start | bytes 786440 | tf_op jit(solution)/shard_map/ppermute | solution.py:154
  142.4 25.6 %all-to-all-start.3 = ((f32[16,80,256]{2,1,0:T(8,128)}), f32[16,80,256]{2,1,0:T(8,128)S(1)}, u32[]{:S(2)}, u32[]{:S(2)}) async-start(f32[16,80,256]{2,1,0:T(8,128)} %bitcast.54), calls=%async_computation.3 | async-start | bytes 2621440 | tf_op jit(solution)/shard_map/all_to_all | solution.py:150
  169.6 11.7 %all-to-all-start.5 = ((f32[8,64,256]{2,1,0:T(8,128)}), f32[8,64,256]{2,1,0:T(8,128)S(1)}, u32[]{:S(2)}, u32[]{:S(2)}) async-start(f32[8,64,256]{2,1,0:T(8,128)} %bitcast_select_fusion), calls=%async_computation.5 | async-start | bytes 1048576 | tf_op jit(solution)/shard_map/all_to_all | solution.py:150
  181.3 19.9 %all-to-all-start.4 = ((f32[16,48,256]{2,1,0:T(8,128)}), f32[16,48,256]{2,1,0:T(8,128)S(1)}, u32[]{:S(2)}, u32[]{:S(2)}) async-start(f32[16,48,256]{2,1,0:T(8,128)} %pad_maximum_fusion.8), calls=%async_computation.4 | async-start | bytes 1572864 | tf_op jit(solution)/shard_map/all_to_all | solution.py:150
  187.0 1.6 collective-permute-start.18
  (20 other events, 174.1 us)

commit v4 on v3

--- a/solution.py
+++ b/solution.py
@@ -76,10 +76,11 @@
     def low(row):
         return [right[2 * row + n].reshape(width, width) for n in range(2)]
 
-    for t in range(slots):
-        for copy in left_copies[t]:
+    for t in range(0, slots, 2):
+        for copy in left_copies[t] + left_copies[t + 1]:
             copy.wait()
-        term = product(left[t], jnp.concatenate(low(info[12 + t]), axis=1))
+        block = jnp.concatenate([jnp.concatenate(low(info[12 + t + n]), axis=1) for n in range(2)], axis=0)
+        term = product(jnp.concatenate([left[t], left[t + 1]], axis=1), block)
         if t == 0:
             total[...] = term
         else:
@@ -141,13 +142,17 @@
             jax.ShapeDtypeStruct((slots, 2, width // slots, width), f32),
             jax.ShapeDtypeStruct((pieces, 3 * width // pieces, width), f32),
         ],
-        compiler_params=pltpu.CompilerParams(vmem_limit_bytes=60 << 20),
+        compiler_params=pltpu.CompilerParams(vmem_limit_bytes=28 << 20),
         cost_estimate=pl.CostEstimate(flops=10_000_000_000, bytes_accessed=12_000_000, transcendentals=0),
     )(info, *arrivals, *given, *lows, pivot)
 
 
 def exchange(x, axis):
     return lax.all_to_all(x, axis, split_axis=0, concat_axis=0, tiled=True)
+
+
+def pick(x, index):
+    return x.at[index].get(mode="promise_in_bounds")
 
 
 def swap(x, axis=CORES):
@@ -196,9 +201,9 @@
     flat = [x.reshape(cols, piece, width) for x in (low_one, low_two, factor)]
     pieces = exchange(jnp.concatenate(flat, axis=1), SIDE).reshape(3 * cols, piece, width)
     order = jnp.stack([3 * kind, 3 * children + 1], axis=1).reshape(-1)
-    routed = jnp.take(pieces, order, axis=0).reshape(rows, cores * 2 * piece, width)
+    routed = pick(pieces, order).reshape(rows, cores * 2 * piece, width)
     own_children = lax.dynamic_slice_in_dim(children, row * cores, cores)
-    uppers = jnp.take(pieces, 3 * own_children + 2, axis=0)
+    uppers = pick(pieces, 3 * own_children + 2)
     upper = swap(lax.dynamic_index_in_dim(uppers, 1 - core, 0))
     kept = lax.dynamic_index_in_dim(uppers, core, 0)
     uppers = jnp.where(core == 0, jnp.stack([kept, upper]), jnp.stack([upper, kept]))
@@ -206,14 +211,18 @@
     mine = mine.reshape(rows, cores, 2, piece, width).transpose(1, 0, 2, 3, 4)
     both = jnp.concatenate([mine.reshape(cores, rows * 2, piece, width), uppers], axis=1)
 
-    inverse, lows = go_round((anc, RING, NEXT), (both, LINE, ACROSS))
     ring = lax.axis_index(RING)
     lengths = lax.axis_size(RING)
     slot = jnp.stack([(half ^ n) * lengths + (ring + m) % lengths for m, n in PLACES])
     places = jnp.stack([(line + m) % lines * pair + (across ^ n) for m, n in PLACES])
-    here = jnp.take(pattern, row * cores + core, axis=0)
-    there = jnp.take(pattern, row * cores + 1 - core, axis=0)
-    picks = jnp.take(there, slot) % 2 > 0
+    here = pick(pattern, row * cores + core)
+    picks = pick(pick(pattern, row * cores + 1 - core), slot) % 2 > 0
+    away = pick(here, chip) != col
+    flags = jnp.stack([away.astype(jnp.int32), (chip == row).astype(jnp.int32), chip, core])
+    info = jnp.concatenate([pick(here, slot) % 2, flags, slot, places])
+    info, picks, anc, both = lax.optimization_barrier((info, picks, anc, both))
+
+    inverse, lows = go_round((anc, RING, NEXT), (both, LINE, ACROSS))
 
     def handed(first, *blocks):
         picked = [jnp.where(picks[first + n], x[:, width:], x[:, :width]) for n, x in enumerate(blocks)]
@@ -225,9 +234,6 @@
         handed(4, up[:width], down[:width], jnp.concatenate([up[width:], down[width:]])),
         handed(7, jnp.concatenate([low_far, high_far])),
     )
-    away = jnp.take(here, chip) != col
-    flags = jnp.stack([away.astype(jnp.int32), (chip == row).astype(jnp.int32), chip, core])
-    info = jnp.concatenate([jnp.take(here, slot) % 2, flags, slot, places])
     keep, give, second, parts = level_blocks(info, inverse, given, lows, pivot_one)
     taken = swap(give)
     column_one = jnp.where(core == 0, jnp.concatenate([keep, taken]), jnp.concatenate([taken, keep]))
@@ -237,11 +243,11 @@
     halves = jnp.broadcast_to(halves, (rows, *halves.shape[1:]))
     send = jnp.concatenate([halves, second], axis=2).reshape(cols, -1, width)
     known = exchange(send, (*ROWS, CORES))
-    column_two = jnp.take(known[:, 3 * piece :], parents, axis=0)
+    column_two = pick(known[:, 3 * piece :], parents)
     column_two = exchange(column_two.reshape(rows, -1, width), ROWS)
     column_two = column_two.reshape(rows, cores, -1, width).transpose(1, 0, 2, 3)
     known = known.reshape(cols, -1, piece, width)
-    blocks = [known[:, 0], jnp.take(known[:, 1:3], parents, axis=0).reshape(cols, -1, width)]
+    blocks = [known[:, 0], pick(known[:, 1:3], parents).reshape(cols, -1, width)]
     final = exchange(jnp.concatenate(blocks, axis=1), SIDE)
     final = final.reshape(cols, 3, piece, width)
     diag_one, cross, last = (final[:, n].reshape(1, width, width) for n in range(3))

time: 204 us -> 195 us (0.956)
  Pallas kernels: 11.5 us -> 6.76 us
  other arithmetic: 16.3 us -> 12.8 us
    pallas_call x1, Pallas kernels: 11.5 us -> 6.76 us  [level_blocks(): pl.pallas_call(kernel, grid_spec=grid_spec, out_shape=[jax.ShapeDtypeStru...]
    unnamed x41 -> x11, local copies, waits for them, and re-layouts: 2.78 us -> 0.04 us
    select_n x9 -> x5, other arithmetic: 2.28 us -> 0.1 us  [the longest x4 0.09 us: pick(): return x.at[index].get(mode='promise_in_bounds')]
  transfers between devices with their start and end apart: 24 -> 24, of which waited for: 11 -> 10; matrix products, arithmetic and copies ran while one was open for 8% -> 7% of each run, Pallas kernels for 0% -> 0%
where the time goes in v4:
time: 195 us; the launch traced here: 194 us
  waiting for transfers between devices  88.5 us (45%)
  starting transfers between devices  58.3 us (30%)
  blocking collectives  17.8 us (9%)
  other arithmetic  12.8 us (7%)
  local copies, waits for them, and re-layouts  8.35 us (4%)
  Pallas kernels  6.76 us (3%)
    all_to_all x5, waiting for transfers between devices, exchange(): return lax.all_to_all(x, axis, split_axis=0, concat_axis=0, tiled=True)  55.9 us
    all_to_all x5, starting transfers between devices, exchange(): return lax.all_to_all(x, axis, split_axis=0, concat_axis=0, tiled=True)  31.2 us
    ppermute x12, waiting for transfers between devices, shift(): return lax.ppermute(x, axis, [(i, (i + by) % n) for i in range(n)])  21.2 us
    all_to_all x1, blocking collectives, exchange(): return lax.all_to_all(x, axis, split_axis=0, concat_axis=0, tiled=True)  17.8 us
    ppermute x12, starting transfers between devices, shift(): return lax.ppermute(x, axis, [(i, (i + by) % n) for i in range(n)])  16.4 us
    ppermute x7, waiting for transfers between devices, swap(): return lax.ppermute(x, axis, [(0, 1), (1, 0)])  11.4 us
    ppermute x7, starting transfers between devices, swap(): return lax.ppermute(x, axis, [(0, 1), (1, 0)])  10.8 us
    pallas_call x1, Pallas kernels, level_blocks(): pl.pallas_call(kernel, grid_spec=grid_spec, out_shape=[jax.ShapeDtypeStru...  6.76 us
  transfers between devices with their start and end apart: 24, of which 10 were waited for; matrix products, arithmetic and copies ran while one was open for 7% of the time, Pallas kernels for 0%

profile of v4, /device:TPU:1, one launch (start us, length us, event | category | flops | bytes accessed | tf_op | source)
XLA Modules:
  0.0 194.3 jit_solution(10532024374589793023)
XLA Ops:
  0.7 2.1 %pad_maximum_fusion.6 = f32[16,48,256]{2,1,0:T(8,128)} fusion(f32[16,16,256]{2,1,0:T(8,128)} %bitcast.103, f32[16,16,256]{2,1,0:T(8,128)} %bitcast.104, f32[16,16,256]{2,1,0:T(8,128)} %bitcast.105), kind=kLoop, calls=%fused_computation.12 | loop fusion | flops 393216 | bytes 1572864 | tf_op jit(solution)/shard_map/concatenate | solution.py:202
  2.7 8.4 %all-to-all-start = ((f32[16,48,256]{2,1,0:T(8,128)}), f32[16,48,256]{2,1,0:T(8,128)S(1)}, u32[]{:S(2)}, u32[]{:S(2)}) async-start(f32[16,48,256]{2,1,0:T(8,128)} %pad_maximum_fusion.6), calls=%async_computation | async-start | bytes 1572864 | tf_op jit(solution)/shard_map/all_to_all | solution.py:151
  12.6 12.7 %all-to-all-done = f32[16,48,256]{2,1,0:T(8,128)S(1)} async-done(((f32[16,48,256]{2,1,0:T(8,128)}), f32[16,48,256]{2,1,0:T(8,128)S(1)}, u32[]{:S(2)}, u32[]{:S(2)}) %all-to-all-start) | async-done | bytes 786464 | tf_op jit(solution)/shard_map/all_to_all | solution.py:151
  26.7 6.6 %all-to-all-start.1 = ((f32[16,32,256]{2,1,0:T(8,128)}), f32[16,32,256]{2,1,0:T(8,128)S(1)}, u32[]{:S(2)}, u32[]{:S(2)}) async-start(f32[16,32,256]{2,1,0:T(8,128)} %bitcast.36), calls=%async_computation.1 | async-start | bytes 1048576 | tf_op jit(solution)/shard_map/all_to_all | solution.py:151
  36.2 6.9 %all-to-all-done.1 = f32[16,32,256]{2,1,0:T(8,128)S(1)} async-done(((f32[16,32,256]{2,1,0:T(8,128)}), f32[16,32,256]{2,1,0:T(8,128)S(1)}, u32[]{:S(2)}, u32[]{:S(2)}) %all-to-all-start.1) | async-done | bytes 524320 | tf_op jit(solution)/shard_map/all_to_all | solution.py:151
  43.3 2.7 %collective-permute-start.5 = (f32[2,17,16,256]{3,2,1,0:T(8,128)S(1)}, f32[2,17,16,256]{3,2,1,0:T(8,128)S(1)}, u32[]{:S(2)}, u32[]{:S(2)}) collective-permute-start(f32[2,17,16,256]{3,2,1,0:T(8,128)S(1)} %pad_maximum_fusion.9.refs_11_), channel_id=1, source_target_pairs={{0,12},{4,0},{8,4},{12,8},{1,13},{5,1},{9,5},{13,9},{2,14},{6,2},{... | collective-permute-start | bytes 1671176 | tf_op jit(solution)/shard_map/ppermute | solution.py:164
  46.7 2.6 %collective-permute-start.2 = (f32[256,512]{1,0:T(8,128)S(1)}, f32[256,512]{1,0:T(8,128)S(1)}, u32[]{:S(2)}, u32[]{:S(2)}) collective-permute-start(f32[256,512]{1,0:T(8,128)S(1)} %copy-done), channel_id=1, source_target_pairs={{0,48},{16,0},{32,16},{48,32},{1,49},{17,1},{33,17},{49,33},{2,50}... | collective-permute-start | bytes 1572872 | tf_op jit(solution)/shard_map/ppermute | solution.py:164
  49.3 7.4 %collective-permute-done.1.refs_1_ = f32[256,512]{1,0:T(8,128)S(1)} collective-permute-done((f32[256,512]{1,0:T(8,128)S(1)}, f32[256,512]{1,0:T(8,128)S(1)}, u32[]{:S(2)}, u32[]{:S(2)}) %collective-permute-start.1) | collective-permute-done | bytes 524320 | tf_op jit(solution)/shard_map/ppermute | solution.py:164
  59.3 10.1 %collective-permute-done.3.refs_3_ = f32[256,512]{1,0:T(8,128)S(1)} collective-permute-done((f32[256,512]{1,0:T(8,128)S(1)}, f32[256,512]{1,0:T(8,128)S(1)}, u32[]{:S(2)}, u32[]{:S(2)}) %collective-permute-start.3) | collective-permute-done | bytes 524320 | tf_op jit(solution)/shard_map/ppermute | solution.py:159
  72.7 1.7 collective-permute-start.8
  76.5 3.3 %collective-permute-start.13 = (f32[4,256,256]{2,1,0:T(8,128)S(1)}, f32[4,256,256]{2,1,0:T(8,128)S(1)}, u32[]{:S(2)}, u32[]{:S(2)}) collective-permute-start(f32[4,256,256]{2,1,0:T(8,128)S(1)} %pad_maximum_fusion.1), channel_id=1, source_target_pairs={{0,1},{1,0},{2,3},{3,2},{4,5},{5,4},{6,7},{7,6},{8,9},{9,8},{10,11... | collective-permute-start | bytes 3145736 | tf_op jit(solution)/shard_map/ppermute | solution.py:159
  79.8 9.4 %collective-permute-done.7.refs_4_ = f32[384,512]{1,0:T(8,128)S(1)} collective-permute-done((f32[384,512]{1,0:T(8,128)S(1)}, f32[384,512]{1,0:T(8,128)S(1)}, u32[]{:S(2)}, u32[]{:S(2)}) %collective-permute-start.7) | collective-permute-done | bytes 786464 | tf_op jit(solution)/shard_map/ppermute | solution.py:164
  90.5 2.5 %collective-permute-start.12 = (f32[128,512]{1,0:T(8,128)S(1)}, f32[128,512]{1,0:T(8,128)S(1)}, u32[]{:S(2)}, u32[]{:S(2)}) collective-permute-start(f32[128,512]{1,0:T(8,128)S(1)} %get-tuple-element.51), channel_id=1, source_target_pairs={{0,48},{16,0},{32,16},{48,32},{1,49},{17,1},{33,17},{49,33},{2,50}... | collective-permute-start | bytes 786440 | tf_op jit(solution)/shard_map/ppermute | solution.py:164
  95.1 3.4 %collective-permute-start.14 = (f32[3,256,256]{2,1,0:T(8,128)S(1)}, f32[3,256,256]{2,1,0:T(8,128)S(1)}, u32[]{:S(2)}, u32[]{:S(2)}) collective-permute-start(f32[3,256,256]{2,1,0:T(8,128)S(1)} %pad_maximum_fusion.7), channel_id=1, source_target_pairs={{0,1},{1,0},{2,3},{3,2},{4,5},{5,4},{6,7},{7,6},{8,9},{9,8},{10,11... | collective-permute-start | bytes 2359304 | tf_op jit(solution)/shard_map/ppermute | solution.py:159
  98.6 2.7 %collective-permute-start.17 = (f32[1,17,16,256]{3,2,1,0:T(8,128)S(1)}, f32[1,17,16,256]{3,2,1,0:T(8,128)S(1)}, u32[]{:S(2)}, u32[]{:S(2)}) collective-permute-start(f32[1,17,16,256]{3,2,1,0:T(8,128)S(1)} %slice.159), channel_id=1, source_target_pairs={{0,12},{4,0},{8,4},{12,8},{1,13},{5,1},{9,5},{13,9},{2,14},{6,2},{... | collective-permute-start | bytes 835592 | tf_op jit(solution)/shard_map/ppermute | solution.py:164
  103.7 4.4 %collective-permute-done.16.refs_17_ = f32[1,17,16,256]{3,2,1,0:T(8,128)S(1)} collective-permute-done((f32[1,17,16,256]{3,2,1,0:T(8,128)S(1)}, f32[1,17,16,256]{3,2,1,0:T(8,128)S(1)}, u32[]{:S(2)}, u32[]{:S(2)}) %collective-permute-start.16) | collective-permute-done | bytes 278560 | tf_op jit(solution)/shard_map/ppermute | solution.py:164
  108.1 6.8 %shard_map.119 = (f32[1,256,256]{2,1,0:T(8,128)S(1)}, f32[1,256,256]{2,1,0:T(8,128)S(1)}, f32[8,2,32,256]{3,2,1,0:T(8,128)S(1)}, f32[8,96,256]{2,1,0:T(8,128)S(1)}) custom-call(s32[28]{0:T(128)S(1)} %concatenate.75.info, f32[256,512]{1,0:T(8,128)S(1)} %copy-done, f32[256,512]{1,0:T(8,128)S(1)} %collective-permute-done.1.refs_1_, ...), custom_call_target="tpu_custom_call" | custom-call | flops 10000000000 | bytes 12000000 | tf_op jit(solution)/shard_map/pallas_call | solution.py:136
  114.9 17.8 %all_to_all.30 = f32[8,96,256]{2,1,0:T(8,128)S(1)} all-to-all(f32[8,96,256]{2,1,0:T(8,128)S(1)} %get-tuple-element.43), channel_id=1, replica_groups=mesh['next'=2,'ring'=4,'x'=4,'across'=2,'core'=2] {'x','across'}, dimensions={0} | all-to-all | bytes 1572864 | tf_op jit(solution)/shard_map/all_to_all | solution.py:151
  134.0 6.9 %all-to-all-start.3 = ((f32[16,80,256]{2,1,0:T(8,128)}), f32[16,80,256]{2,1,0:T(8,128)S(1)}, u32[]{:S(2)}, u32[]{:S(2)}) async-start(f32[16,80,256]{2,1,0:T(8,128)} %bitcast.91), calls=%async_computation.3 | async-start | bytes 2621440 | tf_op jit(solution)/shard_map/all_to_all | solution.py:151
  141.0 18.7 %all-to-all-done.3 = f32[16,80,256]{2,1,0:T(8,128)S(1)} async-done(((f32[16,80,256]{2,1,0:T(8,128)}), f32[16,80,256]{2,1,0:T(8,128)S(1)}, u32[]{:S(2)}, u32[]{:S(2)}) %all-to-all-start.3) | async-done | bytes 1310752 | tf_op jit(solution)/shard_map/all_to_all | solution.py:151
  161.1 3.6 %all-to-all-start.5 = ((f32[8,64,256]{2,1,0:T(8,128)}), f32[8,64,256]{2,1,0:T(8,128)S(1)}, u32[]{:S(2)}, u32[]{:S(2)}) async-start(f32[8,64,256]{2,1,0:T(8,128)} %bitcast.67), calls=%async_computation.5 | async-start | bytes 1048576 | tf_op jit(solution)/shard_map/all_to_all | solution.py:151
  166.3 6.5 %all-to-all-done.5 = f32[8,64,256]{2,1,0:T(8,128)S(1)} async-done(((f32[8,64,256]{2,1,0:T(8,128)}), f32[8,64,256]{2,1,0:T(8,128)S(1)}, u32[]{:S(2)}, u32[]{:S(2)}) %all-to-all-start.5) | async-done | bytes 524320 | tf_op jit(solution)/shard_map/all_to_all | solution.py:151
  172.8 5.7 %all-to-all-start.4 = ((f32[16,48,256]{2,1,0:T(8,128)}), f32[16,48,256]{2,1,0:T(8,128)S(1)}, u32[]{:S(2)}, u32[]{:S(2)}) async-start(f32[16,48,256]{2,1,0:T(8,128)} %pad_maximum_fusion.8), calls=%async_computation.4 | async-start | bytes 1572864 | tf_op jit(solution)/shard_map/all_to_all | solution.py:151
  181.7 11.1 %all-to-all-done.4 = f32[16,48,256]{2,1,0:T(8,128)S(1)} async-done(((f32[16,48,256]{2,1,0:T(8,128)}), f32[16,48,256]{2,1,0:T(8,128)S(1)}, u32[]{:S(2)}, u32[]{:S(2)}) %all-to-all-start.4) | async-done | bytes 786464 | tf_op jit(solution)/shard_map/all_to_all | solution.py:151
  (101 shorter events, 28.6 us)
Async XLA Ops:
  2.7 22.6 %all-to-all-start = ((f32[16,48,256]{2,1,0:T(8,128)}), f32[16,48,256]{2,1,0:T(8,128)S(1)}, u32[]{:S(2)}, u32[]{:S(2)}) async-start(f32[16,48,256]{2,1,0:T(8,128)} %pad_maximum_fusion.6), calls=%async_computation | async-start | bytes 1572864 | tf_op jit(solution)/shard_map/all_to_all | solution.py:151
  26.7 16.4 %all-to-all-start.1 = ((f32[16,32,256]{2,1,0:T(8,128)}), f32[16,32,256]{2,1,0:T(8,128)S(1)}, u32[]{:S(2)}, u32[]{:S(2)}) async-start(f32[16,32,256]{2,1,0:T(8,128)} %bitcast.36), calls=%async_computation.1 | async-start | bytes 1048576 | tf_op jit(solution)/shard_map/all_to_all | solution.py:151
  34.5 1.6 collective-permute-start
  43.2 13.5 %collective-permute-start.1 = (f32[256,512]{1,0:T(8,128)S(1)}, f32[256,512]{1,0:T(8,128)S(1)}, u32[]{:S(2)}, u32[]{:S(2)}) collective-permute-start(f32[256,512]{1,0:T(8,128)S(1)} %copy-done), channel_id=1, source_target_pairs={{0,16},{16,32},{32,48},{48,0},{1,17},{17,33},{33,49},{49,1},{2,18}... | collective-permute-start | bytes 1572872 | tf_op jit(solution)/shard_map/ppermute | solution.py:164
  43.2 26.2 %collective-permute-start.4 = (f32[2,17,16,256]{3,2,1,0:T(8,128)S(1)}, f32[2,17,16,256]{3,2,1,0:T(8,128)S(1)}, u32[]{:S(2)}, u32[]{:S(2)}) collective-permute-start(f32[2,17,16,256]{3,2,1,0:T(8,128)S(1)} %pad_maximum_fusion.9.refs_11_), channel_id=1, source_target_pairs={{0,4},{4,8},{8,12},{12,0},{1,5},{5,9},{9,13},{13,1},{2,6},{6,10},{... | collective-permute-start | bytes 1671176 | tf_op jit(solution)/shard_map/ppermute | solution.py:164
  43.3 26.1 %collective-permute-start.5 = (f32[2,17,16,256]{3,2,1,0:T(8,128)S(1)}, f32[2,17,16,256]{3,2,1,0:T(8,128)S(1)}, u32[]{:S(2)}, u32[]{:S(2)}) collective-permute-start(f32[2,17,16,256]{3,2,1,0:T(8,128)S(1)} %pad_maximum_fusion.9.refs_11_), channel_id=1, source_target_pairs={{0,12},{4,0},{8,4},{12,8},{1,13},{5,1},{9,5},{13,9},{2,14},{6,2},{... | collective-permute-start | bytes 1671176 | tf_op jit(solution)/shard_map/ppermute | solution.py:164
  46.0 23.4 %collective-permute-start.6 = (f32[2,17,16,256]{3,2,1,0:T(8,128)S(1)}, f32[2,17,16,256]{3,2,1,0:T(8,128)S(1)}, u32[]{:S(2)}, u32[]{:S(2)}) collective-permute-start(f32[2,17,16,256]{3,2,1,0:T(8,128)S(1)} %pad_maximum_fusion.9.refs_11_), channel_id=1, source_target_pairs={{0,2},{2,0},{1,3},{3,1},{4,6},{6,4},{5,7},{7,5},{8,10},{10,8},{9,1... | collective-permute-start | bytes 1671176 | tf_op jit(solution)/shard_map/ppermute | solution.py:159
  46.7 12.5 %collective-permute-start.2 = (f32[256,512]{1,0:T(8,128)S(1)}, f32[256,512]{1,0:T(8,128)S(1)}, u32[]{:S(2)}, u32[]{:S(2)}) collective-permute-start(f32[256,512]{1,0:T(8,128)S(1)} %copy-done), channel_id=1, source_target_pairs={{0,48},{16,0},{32,16},{48,32},{1,49},{17,1},{33,17},{49,33},{2,50}... | collective-permute-start | bytes 1572872 | tf_op jit(solution)/shard_map/ppermute | solution.py:164
  56.7 12.7 %collective-permute-start.3 = (f32[256,512]{1,0:T(8,128)S(1)}, f32[256,512]{1,0:T(8,128)S(1)}, u32[]{:S(2)}, u32[]{:S(2)}) collective-permute-start(f32[256,512]{1,0:T(8,128)S(1)} %copy-done), channel_id=1, source_target_pairs={{0,64},{64,0},{1,65},{65,1},{2,66},{66,2},{3,67},{67,3},{4,68},{68... | collective-permute-start | bytes 1572872 | tf_op jit(solution)/shard_map/ppermute | solution.py:159
  69.7 19.5 %collective-permute-start.10 = (f32[3,17,16,256]{3,2,1,0:T(8,128)S(1)}, f32[3,17,16,256]{3,2,1,0:T(8,128)S(1)}, u32[]{:S(2)}, u32[]{:S(2)}) collective-permute-start(f32[3,17,16,256]{3,2,1,0:T(8,128)S(1)} %get-tuple-element.54), channel_id=1, source_target_pairs={{0,12},{4,0},{8,4},{12,8},{1,13},{5,1},{9,5},{13,9},{2,14},{6,2},{... | collective-permute-start | bytes 2506760 | tf_op jit(solution)/shard_map/ppermute | solution.py:164
  69.8 19.4 %collective-permute-start.9 = (f32[3,17,16,256]{3,2,1,0:T(8,128)S(1)}, f32[3,17,16,256]{3,2,1,0:T(8,128)S(1)}, u32[]{:S(2)}, u32[]{:S(2)}) collective-permute-start(f32[3,17,16,256]{3,2,1,0:T(8,128)S(1)} %get-tuple-element.55), channel_id=1, source_target_pairs={{0,4},{4,8},{8,12},{12,0},{1,5},{5,9},{9,13},{13,1},{2,6},{6,10},{... | collective-permute-start | bytes 2506760 | tf_op jit(solution)/shard_map/ppermute | solution.py:164
  71.5 17.7 %collective-permute-start.7 = (f32[384,512]{1,0:T(8,128)S(1)}, f32[384,512]{1,0:T(8,128)S(1)}, u32[]{:S(2)}, u32[]{:S(2)}) collective-permute-start(f32[384,512]{1,0:T(8,128)S(1)} %get-tuple-element.57), channel_id=1, source_target_pairs={{0,16},{16,32},{32,48},{48,0},{1,17},{17,33},{33,49},{49,1},{2,18}... | collective-permute-start | bytes 2359304 | tf_op jit(solution)/shard_map/ppermute | solution.py:164
  72.7 16.5 %collective-permute-start.8 = (f32[384,512]{1,0:T(8,128)S(1)}, f32[384,512]{1,0:T(8,128)S(1)}, u32[]{:S(2)}, u32[]{:S(2)}) collective-permute-start(f32[384,512]{1,0:T(8,128)S(1)} %get-tuple-element.56), channel_id=1, source_target_pairs={{0,48},{16,0},{32,16},{48,32},{1,49},{17,1},{33,17},{49,33},{2,50}... | collective-permute-start | bytes 2359304 | tf_op jit(solution)/shard_map/ppermute | solution.py:164
  76.5 27.2 %collective-permute-start.13 = (f32[4,256,256]{2,1,0:T(8,128)S(1)}, f32[4,256,256]{2,1,0:T(8,128)S(1)}, u32[]{:S(2)}, u32[]{:S(2)}) collective-permute-start(f32[4,256,256]{2,1,0:T(8,128)S(1)} %pad_maximum_fusion.1), channel_id=1, source_target_pairs={{0,1},{1,0},{2,3},{3,2},{4,5},{5,4},{6,7},{7,6},{8,9},{9,8},{10,11... | collective-permute-start | bytes 3145736 | tf_op jit(solution)/shard_map/ppermute | solution.py:159
  89.2 9.4 %collective-permute-start.11 = (f32[128,512]{1,0:T(8,128)S(1)}, f32[128,512]{1,0:T(8,128)S(1)}, u32[]{:S(2)}, u32[]{:S(2)}) collective-permute-start(f32[128,512]{1,0:T(8,128)S(1)} %get-tuple-element.53), channel_id=1, source_target_pairs={{0,16},{16,32},{32,48},{48,0},{1,17},{17,33},{33,49},{49,1},{2,18}... | collective-permute-start | bytes 786440 | tf_op jit(solution)/shard_map/ppermute | solution.py:164
  90.5 10.9 %collective-permute-start.12 = (f32[128,512]{1,0:T(8,128)S(1)}, f32[128,512]{1,0:T(8,128)S(1)}, u32[]{:S(2)}, u32[]{:S(2)}) collective-permute-start(f32[128,512]{1,0:T(8,128)S(1)} %get-tuple-element.51), channel_id=1, source_target_pairs={{0,48},{16,0},{32,16},{48,32},{1,49},{17,1},{33,17},{49,33},{2,50}... | collective-permute-start | bytes 786440 | tf_op jit(solution)/shard_map/ppermute | solution.py:164
  95.1 13.0 %collective-permute-start.14 = (f32[3,256,256]{2,1,0:T(8,128)S(1)}, f32[3,256,256]{2,1,0:T(8,128)S(1)}, u32[]{:S(2)}, u32[]{:S(2)}) collective-permute-start(f32[3,256,256]{2,1,0:T(8,128)S(1)} %pad_maximum_fusion.7), channel_id=1, source_target_pairs={{0,1},{1,0},{2,3},{3,2},{4,5},{5,4},{6,7},{7,6},{8,9},{9,8},{10,11... | collective-permute-start | bytes 2359304 | tf_op jit(solution)/shard_map/ppermute | solution.py:159
  98.5 9.6 %collective-permute-start.16 = (f32[1,17,16,256]{3,2,1,0:T(8,128)S(1)}, f32[1,17,16,256]{3,2,1,0:T(8,128)S(1)}, u32[]{:S(2)}, u32[]{:S(2)}) collective-permute-start(f32[1,17,16,256]{3,2,1,0:T(8,128)S(1)} %slice.158), channel_id=1, source_target_pairs={{0,4},{4,8},{8,12},{12,0},{1,5},{5,9},{9,13},{13,1},{2,6},{6,10},{... | collective-permute-start | bytes 835592 | tf_op jit(solution)/shard_map/ppermute | solution.py:164
  98.6 9.4 %collective-permute-start.17 = (f32[1,17,16,256]{3,2,1,0:T(8,128)S(1)}, f32[1,17,16,256]{3,2,1,0:T(8,128)S(1)}, u32[]{:S(2)}, u32[]{:S(2)}) collective-permute-start(f32[1,17,16,256]{3,2,1,0:T(8,128)S(1)} %slice.159), channel_id=1, source_target_pairs={{0,12},{4,0},{8,4},{12,8},{1,13},{5,1},{9,5},{13,9},{2,14},{6,2},{... | collective-permute-start | bytes 835592 | tf_op jit(solution)/shard_map/ppermute | solution.py:164
  102.1 6.0 %collective-permute-start.15 = (f32[1,256,256]{2,1,0:T(8,128)S(1)}, f32[1,256,256]{2,1,0:T(8,128)S(1)}, u32[]{:S(2)}, u32[]{:S(2)}) collective-permute-start(f32[1,256,256]{2,1,0:T(8,128)S(1)} %fusion.3), channel_id=1, source_target_pairs={{0,1},{1,0},{2,3},{3,2},{4,5},{5,4},{6,7},{7,6},{8,9},{9,8},{10,11... | collective-permute-start | bytes 786440 | tf_op jit(solution)/shard_map/ppermute | solution.py:159
  134.0 25.7 %all-to-all-start.3 = ((f32[16,80,256]{2,1,0:T(8,128)}), f32[16,80,256]{2,1,0:T(8,128)S(1)}, u32[]{:S(2)}, u32[]{:S(2)}) async-start(f32[16,80,256]{2,1,0:T(8,128)} %bitcast.91), calls=%async_computation.3 | async-start | bytes 2621440 | tf_op jit(solution)/shard_map/all_to_all | solution.py:151
  161.1 11.7 %all-to-all-start.5 = ((f32[8,64,256]{2,1,0:T(8,128)}), f32[8,64,256]{2,1,0:T(8,128)S(1)}, u32[]{:S(2)}, u32[]{:S(2)}) async-start(f32[8,64,256]{2,1,0:T(8,128)} %bitcast.67), calls=%async_computation.5 | async-start | bytes 1048576 | tf_op jit(solution)/shard_map/all_to_all | solution.py:151
  172.8 19.9 %all-to-all-start.4 = ((f32[16,48,256]{2,1,0:T(8,128)}), f32[16,48,256]{2,1,0:T(8,128)S(1)}, u32[]{:S(2)}, u32[]{:S(2)}) async-start(f32[16,48,256]{2,1,0:T(8,128)} %pad_maximum_fusion.8), calls=%async_computation.4 | async-start | bytes 1572864 | tf_op jit(solution)/shard_map/all_to_all | solution.py:151
  178.5 1.5 collective-permute-start.18
  (5 other events, 53.0 us)

commit v5 on v4

--- a/solution.py
+++ b/solution.py
@@ -30,13 +30,16 @@
     ((0, 0, 0), (0, 0, 1)),
     ((-1, 0, 0), (-1, 0, 1)),
     ((1, 0, 0), (1, 0, 1)),
+    ((2, 0, 0),),
+    ((2, 0, 1),),
     ((0, 1, 0), (0, 1, 1)),
-    ((-1, 1, 0), (-1, 1, 1), (2, 0, 0)),
-    ((1, 1, 0), (1, 1, 1), (2, 0, 1)),
+    ((-1, 1, 0), (-1, 1, 1)),
+    ((1, 1, 0), (1, 1, 1)),
     ((2, 1, 0),),
     ((2, 1, 1),),
 )
-PLACES = ((0, 0), (-1, 0), (1, 0), (0, 1), (-1, 1), (1, 1), (2, 0), (2, 1))
+PLACES = ((0, 0), (-1, 0), (1, 0), (2, 0), (0, 1), (-1, 1), (1, 1), (2, 1))
+GROUPS = (0, 5, 7)
 
 
 def kernel(info, *refs):
@@ -62,8 +65,8 @@
             target = left.at[t, pl.ds(part * parts_of, parts_of)]
             left_copies[t].append(pltpu.make_async_copy(source, target, left_done.at[t, part]))
     for t in range(slots):
-        group = 0 if t < 4 else 1 if t < 7 else 2
-        source = given[group].at[t - (0, 4, 7)[group]]
+        group = sum(t >= first for first in GROUPS) - 1
+        source = given[group].at[t - GROUPS[group]]
         left_copies[t].append(pltpu.make_async_copy(source, left.at[t, pl.ds(width, width)], left_done.at[t, 2]))
     for copy in low_copies:
         copy.start()
@@ -166,23 +169,26 @@
 
 def go_round(*ways):
     hold = lax.optimization_barrier
-    owns = hold(tuple(own for own, _, _ in ways))
-    near = []
-    for own, (_, line, neighbour) in zip(owns, ways):
-        near.append((shift(own, line, 1), shift(own, line, -1), swap(own, neighbour)))
-    near = hold(near)
-    far = []
-    for (below, above, beside), (_, line, _) in zip(near, ways):
-        half = below.shape[0] // 2
-        up = shift(jnp.concatenate([beside, below[:half]]), line, 1)
-        down = shift(jnp.concatenate([beside, above[half:]]), line, -1)
-        far.append((up, down))
-    far = hold(far)
-    ends = []
-    for (up, down), (own, line, _) in zip(far, ways):
-        half = own.shape[0] // 2
-        ends.append((shift(up[:half], line, 1), shift(down[half : 2 * half], line, -1)))
-    return [(own, *n, *f, *e) for own, n, f, e in zip(owns, near, far, ends)]
+    owns = hold([own for own, _, _ in ways])
+    lines = [line for _, line, _ in ways]
+
+    def both_ways(arrays):
+        return [(shift(x, line, 1), shift(x, line, -1)) for x, line in zip(arrays, lines)]
+
+    def onward(pairs):
+        half = pairs[0][0].shape[0] // 2, pairs[1][0].shape[0] // 2
+        return [
+            (shift(low[:n], line, 1), shift(high[n:], line, -1))
+            for (low, high), line, n in zip(pairs, lines, half)
+        ]
+
+    beside = [swap(own, neighbour) for own, (_, _, neighbour) in zip(owns, ways)]
+    near = hold(both_ways(owns))
+    across = onward(near)
+    beside, across = hold((beside, across))
+    far = hold(both_ways(beside))
+    last = onward(far)
+    return [(o, *n, *a, b, *f, *e) for o, n, a, b, f, e in zip(owns, near, across, beside, far, last)]
 
 
 def body(anc, pattern, parents, low_one, pivot_one, low_two, factor, pivot_two):
@@ -228,10 +234,10 @@
         picked = [jnp.where(picks[first + n], x[:, width:], x[:, :width]) for n, x in enumerate(blocks)]
         return swap(jnp.stack(picked))
 
-    own, below, above, beside, up, down, low_far, high_far = inverse
+    own, below, above, low_across, high_across, beside, up, down, low_far, high_far = inverse
     given = (
-        handed(0, own, below, above, beside),
-        handed(4, up[:width], down[:width], jnp.concatenate([up[width:], down[width:]])),
+        handed(0, own, below, above, jnp.concatenate([low_across, high_across]), beside),
+        handed(5, up, down),
         handed(7, jnp.concatenate([low_far, high_far])),
     )
     keep, give, second, parts = level_blocks(info, inverse, given, lows, pivot_one)

time: 195 us -> 191 us (0.979)
  waiting for transfers between devices: 88.5 us -> 82.1 us
  starting transfers between devices: 58.3 us -> 62.2 us
    ppermute x12 -> x16, starting transfers between devices: 16.4 us -> 21.3 us  [shift(): return lax.ppermute(x, axis, [(i, (i + by) % n) for i in range(n)])]
    ppermute x12 -> x16, waiting for transfers between devices: 21.2 us -> 16.4 us  [shift(): return lax.ppermute(x, axis, [(i, (i + by) % n) for i in range(n)])]
    another operation x10 -> x5, other arithmetic: 5.43 us -> 2.75 us  [handed(): return swap(jnp.stack(picked))]
    unnamed x0 -> x4, other arithmetic: none -> 2.58 us
  transfers between devices with their start and end apart: 24 -> 28, of which waited for: 10 -> 10; matrix products, arithmetic and copies ran while one was open for 7% -> 7% of each run, Pallas kernels for 0% -> 0%
where the time goes in v5:
time: 191 us; the launch traced here: 190 us
  waiting for transfers between devices  82.1 us (43%)
  starting transfers between devices  62.2 us (33%)
  blocking collectives  16.6 us (9%)
  other arithmetic  12.3 us (6%)
  local copies, waits for them, and re-layouts  8.36 us (4%)
  Pallas kernels  6.76 us (4%)
    all_to_all x5, waiting for transfers between devices, exchange(): return lax.all_to_all(x, axis, split_axis=0, concat_axis=0, tiled=True)  55.8 us
    all_to_all x5, starting transfers between devices, exchange(): return lax.all_to_all(x, axis, split_axis=0, concat_axis=0, tiled=True)  30.7 us
    ppermute x16, starting transfers between devices, shift(): return lax.ppermute(x, axis, [(i, (i + by) % n) for i in range(n)])  21.3 us
    all_to_all x1, blocking collectives, exchange(): return lax.all_to_all(x, axis, split_axis=0, concat_axis=0, tiled=True)  16.6 us
    ppermute x16, waiting for transfers between devices, shift(): return lax.ppermute(x, axis, [(i, (i + by) % n) for i in range(n)])  16.4 us
    ppermute x7, starting transfers between devices, swap(): return lax.ppermute(x, axis, [(0, 1), (1, 0)])  10.3 us
    ppermute x7, waiting for transfers between devices, swap(): return lax.ppermute(x, axis, [(0, 1), (1, 0)])  9.9 us
    pallas_call x1, Pallas kernels, level_blocks(): pl.pallas_call(kernel, grid_spec=grid_spec, out_shape=[jax.ShapeDtypeStru...  6.76 us
  transfers between devices with their start and end apart: 28, of which 10 were waited for; matrix products, arithmetic and copies ran while one was open for 7% of the time, Pallas kernels for 0%

profile of v5, /device:TPU:1, one launch (start us, length us, event | category | flops | bytes accessed | tf_op | source)
XLA Modules:
  0.0 190.2 jit_solution(16773483146294178775)
XLA Ops:
  2.7 8.4 %all-to-all-start = ((f32[16,48,256]{2,1,0:T(8,128)}), f32[16,48,256]{2,1,0:T(8,128)S(1)}, u32[]{:S(2)}, u32[]{:S(2)}) async-start(f32[16,48,256]{2,1,0:T(8,128)} %pad_maximum_fusion.1), calls=%async_computation | async-start | bytes 1572864 | tf_op jit(solution)/shard_map/all_to_all | solution.py:154
  12.6 12.7 %all-to-all-done = f32[16,48,256]{2,1,0:T(8,128)S(1)} async-done(((f32[16,48,256]{2,1,0:T(8,128)}), f32[16,48,256]{2,1,0:T(8,128)S(1)}, u32[]{:S(2)}, u32[]{:S(2)}) %all-to-all-start) | async-done | bytes 786464 | tf_op jit(solution)/shard_map/all_to_all | solution.py:154
  26.7 6.6 %all-to-all-start.1 = ((f32[16,32,256]{2,1,0:T(8,128)}), f32[16,32,256]{2,1,0:T(8,128)S(1)}, u32[]{:S(2)}, u32[]{:S(2)}) async-start(f32[16,32,256]{2,1,0:T(8,128)} %bitcast.36), calls=%async_computation.1 | async-start | bytes 1048576 | tf_op jit(solution)/shard_map/all_to_all | solution.py:154
  36.2 6.9 %all-to-all-done.1 = f32[16,32,256]{2,1,0:T(8,128)S(1)} async-done(((f32[16,32,256]{2,1,0:T(8,128)}), f32[16,32,256]{2,1,0:T(8,128)S(1)}, u32[]{:S(2)}, u32[]{:S(2)}) %all-to-all-start.1) | async-done | bytes 524320 | tf_op jit(solution)/shard_map/all_to_all | solution.py:154
  43.3 2.7 %collective-permute-start.4 = (f32[2,17,16,256]{3,2,1,0:T(8,128)S(1)}, f32[2,17,16,256]{3,2,1,0:T(8,128)S(1)}, u32[]{:S(2)}, u32[]{:S(2)}) collective-permute-start(f32[2,17,16,256]{3,2,1,0:T(8,128)S(1)} %pad_maximum_fusion.3.refs_13_), channel_id=1, source_target_pairs={{0,12},{4,0},{8,4},{12,8},{1,13},{5,1},{9,5},{13,9},{2,14},{6,2},{... | collective-permute-start | bytes 1671176 | tf_op jit(solution)/shard_map/ppermute | solution.py:167
  46.0 2.6 %collective-permute-start.2 = (f32[256,512]{1,0:T(8,128)S(1)}, f32[256,512]{1,0:T(8,128)S(1)}, u32[]{:S(2)}, u32[]{:S(2)}) collective-permute-start(f32[256,512]{1,0:T(8,128)S(1)} %copy-done), channel_id=1, source_target_pairs={{0,48},{16,0},{32,16},{48,32},{1,49},{17,1},{33,17},{49,33},{2,50}... | collective-permute-start | bytes 1572872 | tf_op jit(solution)/shard_map/ppermute | solution.py:167
  50.0 6.7 %collective-permute-done.1.refs_1_ = f32[256,512]{1,0:T(8,128)S(1)} collective-permute-done((f32[256,512]{1,0:T(8,128)S(1)}, f32[256,512]{1,0:T(8,128)S(1)}, u32[]{:S(2)}, u32[]{:S(2)}) %collective-permute-start.1) | collective-permute-done | bytes 524320 | tf_op jit(solution)/shard_map/ppermute | solution.py:167
  64.4 8.6 %collective-permute-done.6.refs_18_ = f32[2,17,16,256]{3,2,1,0:T(8,128)S(1)} collective-permute-done((f32[2,17,16,256]{3,2,1,0:T(8,128)S(1)}, f32[2,17,16,256]{3,2,1,0:T(8,128)S(1)}, u32[]{:S(2)}, u32[]{:S(2)}) %collective-permute-start.6) | collective-permute-done | bytes 557088 | tf_op jit(solution)/shard_map/ppermute | solution.py:162
  73.0 2.7 %collective-permute-start.14 = (f32[2,17,16,256]{3,2,1,0:T(8,128)S(1)}, f32[2,17,16,256]{3,2,1,0:T(8,128)S(1)}, u32[]{:S(2)}, u32[]{:S(2)}) collective-permute-start(f32[2,17,16,256]{3,2,1,0:T(8,128)S(1)} %collective-permute-done.6.refs_18_), channel_id=1, source_target_pairs={{0,12},{4,0},{8,4},{12,8},{1,13},{5,1},{9,5},{13,9},{2,14},{6,2},{... | collective-permute-start | bytes 1671176 | tf_op jit(solution)/shard_map/ppermute | solution.py:167
  75.7 2.7 %collective-permute-start.12 = (f32[256,512]{1,0:T(8,128)S(1)}, f32[256,512]{1,0:T(8,128)S(1)}, u32[]{:S(2)}, u32[]{:S(2)}) collective-permute-start(f32[256,512]{1,0:T(8,128)S(1)} %collective-permute-done.5.refs_5_), channel_id=1, source_target_pairs={{0,48},{16,0},{32,16},{48,32},{1,49},{17,1},{33,17},{49,33},{2,50}... | collective-permute-start | bytes 1572872 | tf_op jit(solution)/shard_map/ppermute | solution.py:167
  79.8 3.2 %collective-permute-start.17 = (f32[5,256,256]{2,1,0:T(8,128)S(1)}, f32[5,256,256]{2,1,0:T(8,128)S(1)}, u32[]{:S(2)}, u32[]{:S(2)}) collective-permute-start(f32[5,256,256]{2,1,0:T(8,128)S(1)} %bitcast_dynamic-update-slice_fusion), channel_id=1, source_target_pairs={{0,1},{1,0},{2,3},{3,2},{4,5},{5,4},{6,7},{7,6},{8,9},{9,8},{10,11... | collective-permute-start | bytes 3932168 | tf_op jit(solution)/shard_map/ppermute | solution.py:162
  83.0 4.8 %collective-permute-done.11.refs_6_ = f32[256,512]{1,0:T(8,128)S(1)} collective-permute-done((f32[256,512]{1,0:T(8,128)S(1)}, f32[256,512]{1,0:T(8,128)S(1)}, u32[]{:S(2)}, u32[]{:S(2)}) %collective-permute-start.11) | collective-permute-done | bytes 524320 | tf_op jit(solution)/shard_map/ppermute | solution.py:167
  88.0 2.6 %collective-permute-start.16 = (f32[128,512]{1,0:T(8,128)S(1)}, f32[128,512]{1,0:T(8,128)S(1)}, u32[]{:S(2)}, u32[]{:S(2)}) collective-permute-start(f32[128,512]{1,0:T(8,128)S(1)} %slice.119), channel_id=1, source_target_pairs={{0,48},{16,0},{32,16},{48,32},{1,49},{17,1},{33,17},{49,33},{2,50}... | collective-permute-start | bytes 786440 | tf_op jit(solution)/shard_map/ppermute | solution.py:167
  92.1 4.1 %collective-permute-start.18 = (f32[2,256,256]{2,1,0:T(8,128)S(1)}, f32[2,256,256]{2,1,0:T(8,128)S(1)}, u32[]{:S(2)}, u32[]{:S(2)}) collective-permute-start(f32[2,256,256]{2,1,0:T(8,128)S(1)} %pad_maximum_fusion.4), channel_id=1, source_target_pairs={{0,1},{1,0},{2,3},{3,2},{4,5},{5,4},{6,7},{7,6},{8,9},{9,8},{10,11... | collective-permute-start | bytes 1572872 | tf_op jit(solution)/shard_map/ppermute | solution.py:162
  96.3 2.7 %collective-permute-start.21 = (f32[1,17,16,256]{3,2,1,0:T(8,128)S(1)}, f32[1,17,16,256]{3,2,1,0:T(8,128)S(1)}, u32[]{:S(2)}, u32[]{:S(2)}) collective-permute-start(f32[1,17,16,256]{3,2,1,0:T(8,128)S(1)} %slice.145), channel_id=1, source_target_pairs={{0,12},{4,0},{8,4},{12,8},{1,13},{5,1},{9,5},{13,9},{2,14},{6,2},{... | collective-permute-start | bytes 835592 | tf_op jit(solution)/shard_map/ppermute | solution.py:167
  100.9 4.9 %collective-permute-done.20.refs_21_ = f32[1,17,16,256]{3,2,1,0:T(8,128)S(1)} collective-permute-done((f32[1,17,16,256]{3,2,1,0:T(8,128)S(1)}, f32[1,17,16,256]{3,2,1,0:T(8,128)S(1)}, u32[]{:S(2)}, u32[]{:S(2)}) %collective-permute-start.20) | collective-permute-done | bytes 278560 | tf_op jit(solution)/shard_map/ppermute | solution.py:167
  105.8 6.8 %shard_map.119 = (f32[1,256,256]{2,1,0:T(8,128)S(1)}, f32[1,256,256]{2,1,0:T(8,128)S(1)}, f32[8,2,32,256]{3,2,1,0:T(8,128)S(1)}, f32[8,96,256]{2,1,0:T(8,128)S(1)}) custom-call(s32[28]{0:T(128)S(1)} %concatenate.63.info, f32[256,512]{1,0:T(8,128)S(1)} %copy-done, f32[256,512]{1,0:T(8,128)S(1)} %collective-permute-done.1.refs_1_, ...), custom_call_target="tpu_custom_call" | custom-call | flops 10000000000 | bytes 12000000 | tf_op jit(solution)/shard_map/pallas_call | solution.py:139
  112.5 16.6 %all_to_all.30 = f32[8,96,256]{2,1,0:T(8,128)S(1)} all-to-all(f32[8,96,256]{2,1,0:T(8,128)S(1)} %get-tuple-element.51), channel_id=1, replica_groups=mesh['next'=2,'ring'=4,'x'=4,'across'=2,'core'=2] {'x','across'}, dimensions={0} | all-to-all | bytes 1572864 | tf_op jit(solution)/shard_map/all_to_all | solution.py:154
  130.5 6.3 %all-to-all-start.3 = ((f32[16,80,256]{2,1,0:T(8,128)}), f32[16,80,256]{2,1,0:T(8,128)S(1)}, u32[]{:S(2)}, u32[]{:S(2)}) async-start(f32[16,80,256]{2,1,0:T(8,128)} %bitcast.93), calls=%async_computation.3 | async-start | bytes 2621440 | tf_op jit(solution)/shard_map/all_to_all | solution.py:154
  136.8 18.7 %all-to-all-done.3 = f32[16,80,256]{2,1,0:T(8,128)S(1)} async-done(((f32[16,80,256]{2,1,0:T(8,128)}), f32[16,80,256]{2,1,0:T(8,128)S(1)}, u32[]{:S(2)}, u32[]{:S(2)}) %all-to-all-start.3) | async-done | bytes 1310752 | tf_op jit(solution)/shard_map/all_to_all | solution.py:154
  156.9 3.6 %all-to-all-start.5 = ((f32[8,64,256]{2,1,0:T(8,128)}), f32[8,64,256]{2,1,0:T(8,128)S(1)}, u32[]{:S(2)}, u32[]{:S(2)}) async-start(f32[8,64,256]{2,1,0:T(8,128)} %bitcast.67), calls=%async_computation.5 | async-start | bytes 1048576 | tf_op jit(solution)/shard_map/all_to_all | solution.py:154
  162.1 6.5 %all-to-all-done.5 = f32[8,64,256]{2,1,0:T(8,128)S(1)} async-done(((f32[8,64,256]{2,1,0:T(8,128)}), f32[8,64,256]{2,1,0:T(8,128)S(1)}, u32[]{:S(2)}, u32[]{:S(2)}) %all-to-all-start.5) | async-done | bytes 524320 | tf_op jit(solution)/shard_map/all_to_all | solution.py:154
  168.6 5.8 %all-to-all-start.4 = ((f32[16,48,256]{2,1,0:T(8,128)}), f32[16,48,256]{2,1,0:T(8,128)S(1)}, u32[]{:S(2)}, u32[]{:S(2)}) async-start(f32[16,48,256]{2,1,0:T(8,128)} %pad_maximum_fusion.2), calls=%async_computation.4 | async-start | bytes 1572864 | tf_op jit(solution)/shard_map/all_to_all | solution.py:154
  177.6 11.0 %all-to-all-done.4 = f32[16,48,256]{2,1,0:T(8,128)S(1)} async-done(((f32[16,48,256]{2,1,0:T(8,128)}), f32[16,48,256]{2,1,0:T(8,128)S(1)}, u32[]{:S(2)}, u32[]{:S(2)}) %all-to-all-start.4) | async-done | bytes 786464 | tf_op jit(solution)/shard_map/all_to_all | solution.py:154
  (108 shorter events, 30.4 us)
Async XLA Ops:
  2.7 22.6 %all-to-all-start = ((f32[16,48,256]{2,1,0:T(8,128)}), f32[16,48,256]{2,1,0:T(8,128)S(1)}, u32[]{:S(2)}, u32[]{:S(2)}) async-start(f32[16,48,256]{2,1,0:T(8,128)} %pad_maximum_fusion.1), calls=%async_computation | async-start | bytes 1572864 | tf_op jit(solution)/shard_map/all_to_all | solution.py:154
  26.7 16.4 %all-to-all-start.1 = ((f32[16,32,256]{2,1,0:T(8,128)}), f32[16,32,256]{2,1,0:T(8,128)S(1)}, u32[]{:S(2)}, u32[]{:S(2)}) async-start(f32[16,32,256]{2,1,0:T(8,128)} %bitcast.36), calls=%async_computation.1 | async-start | bytes 1048576 | tf_op jit(solution)/shard_map/all_to_all | solution.py:154
  43.2 13.5 %collective-permute-start.1 = (f32[256,512]{1,0:T(8,128)S(1)}, f32[256,512]{1,0:T(8,128)S(1)}, u32[]{:S(2)}, u32[]{:S(2)}) collective-permute-start(f32[256,512]{1,0:T(8,128)S(1)} %copy-done), channel_id=1, source_target_pairs={{0,16},{16,32},{32,48},{48,0},{1,17},{17,33},{33,49},{49,1},{2,18}... | collective-permute-start | bytes 1572872 | tf_op jit(solution)/shard_map/ppermute | solution.py:167
  43.2 14.9 %collective-permute-start.3 = (f32[2,17,16,256]{3,2,1,0:T(8,128)S(1)}, f32[2,17,16,256]{3,2,1,0:T(8,128)S(1)}, u32[]{:S(2)}, u32[]{:S(2)}) collective-permute-start(f32[2,17,16,256]{3,2,1,0:T(8,128)S(1)} %pad_maximum_fusion.3.refs_13_), channel_id=1, source_target_pairs={{0,4},{4,8},{8,12},{12,0},{1,5},{5,9},{9,13},{13,1},{2,6},{6,10},{... | collective-permute-start | bytes 1671176 | tf_op jit(solution)/shard_map/ppermute | solution.py:167
  43.3 14.8 %collective-permute-start.4 = (f32[2,17,16,256]{3,2,1,0:T(8,128)S(1)}, f32[2,17,16,256]{3,2,1,0:T(8,128)S(1)}, u32[]{:S(2)}, u32[]{:S(2)}) collective-permute-start(f32[2,17,16,256]{3,2,1,0:T(8,128)S(1)} %pad_maximum_fusion.3.refs_13_), channel_id=1, source_target_pairs={{0,12},{4,0},{8,4},{12,8},{1,13},{5,1},{9,5},{13,9},{2,14},{6,2},{... | collective-permute-start | bytes 1671176 | tf_op jit(solution)/shard_map/ppermute | solution.py:167
  46.0 12.1 %collective-permute-start.2 = (f32[256,512]{1,0:T(8,128)S(1)}, f32[256,512]{1,0:T(8,128)S(1)}, u32[]{:S(2)}, u32[]{:S(2)}) collective-permute-start(f32[256,512]{1,0:T(8,128)S(1)} %copy-done), channel_id=1, source_target_pairs={{0,48},{16,0},{32,16},{48,32},{1,49},{17,1},{33,17},{49,33},{2,50}... | collective-permute-start | bytes 1572872 | tf_op jit(solution)/shard_map/ppermute | solution.py:167
  48.6 13.3 %collective-permute-start.5 = (f32[256,512]{1,0:T(8,128)S(1)}, f32[256,512]{1,0:T(8,128)S(1)}, u32[]{:S(2)}, u32[]{:S(2)}) collective-permute-start(f32[256,512]{1,0:T(8,128)S(1)} %copy-done), channel_id=1, source_target_pairs={{0,64},{64,0},{1,65},{65,1},{2,66},{66,2},{3,67},{67,3},{4,68},{68... | collective-permute-start | bytes 1572872 | tf_op jit(solution)/shard_map/ppermute | solution.py:162
  56.7 16.2 %collective-permute-start.6 = (f32[2,17,16,256]{3,2,1,0:T(8,128)S(1)}, f32[2,17,16,256]{3,2,1,0:T(8,128)S(1)}, u32[]{:S(2)}, u32[]{:S(2)}) collective-permute-start(f32[2,17,16,256]{3,2,1,0:T(8,128)S(1)} %pad_maximum_fusion.3.refs_13_), channel_id=1, source_target_pairs={{0,2},{2,0},{1,3},{3,1},{4,6},{6,4},{5,7},{7,5},{8,10},{10,8},{9,1... | collective-permute-start | bytes 1671176 | tf_op jit(solution)/shard_map/ppermute | solution.py:162
  58.1 14.8 %collective-permute-start.10 = (f32[1,17,16,256]{3,2,1,0:T(8,128)S(1)}, f32[1,17,16,256]{3,2,1,0:T(8,128)S(1)}, u32[]{:S(2)}, u32[]{:S(2)}) collective-permute-start(f32[1,17,16,256]{3,2,1,0:T(8,128)S(1)} %slice.117), channel_id=1, source_target_pairs={{0,12},{4,0},{8,4},{12,8},{1,13},{5,1},{9,5},{13,9},{2,14},{6,2},{... | collective-permute-start | bytes 835592 | tf_op jit(solution)/shard_map/ppermute | solution.py:167
  60.0 12.9 %collective-permute-start.9 = (f32[1,17,16,256]{3,2,1,0:T(8,128)S(1)}, f32[1,17,16,256]{3,2,1,0:T(8,128)S(1)}, u32[]{:S(2)}, u32[]{:S(2)}) collective-permute-start(f32[1,17,16,256]{3,2,1,0:T(8,128)S(1)} %slice.116), channel_id=1, source_target_pairs={{0,4},{4,8},{8,12},{12,0},{1,5},{5,9},{9,13},{13,1},{2,6},{6,10},{... | collective-permute-start | bytes 835592 | tf_op jit(solution)/shard_map/ppermute | solution.py:167
  60.1 12.8 %collective-permute-start.7 = (f32[128,512]{1,0:T(8,128)S(1)}, f32[128,512]{1,0:T(8,128)S(1)}, u32[]{:S(2)}, u32[]{:S(2)}) collective-permute-start(f32[128,512]{1,0:T(8,128)S(1)} %slice.114), channel_id=1, source_target_pairs={{0,16},{16,32},{32,48},{48,0},{1,17},{17,33},{33,49},{49,1},{2,18}... | collective-permute-start | bytes 786440 | tf_op jit(solution)/shard_map/ppermute | solution.py:167
  61.8 11.1 %collective-permute-start.8 = (f32[128,512]{1,0:T(8,128)S(1)}, f32[128,512]{1,0:T(8,128)S(1)}, u32[]{:S(2)}, u32[]{:S(2)}) collective-permute-start(f32[128,512]{1,0:T(8,128)S(1)} %slice.115), channel_id=1, source_target_pairs={{0,48},{16,0},{32,16},{48,32},{1,49},{17,1},{33,17},{49,33},{2,50}... | collective-permute-start | bytes 786440 | tf_op jit(solution)/shard_map/ppermute | solution.py:167
  72.9 14.8 %collective-permute-start.13 = (f32[2,17,16,256]{3,2,1,0:T(8,128)S(1)}, f32[2,17,16,256]{3,2,1,0:T(8,128)S(1)}, u32[]{:S(2)}, u32[]{:S(2)}) collective-permute-start(f32[2,17,16,256]{3,2,1,0:T(8,128)S(1)} %collective-permute-done.6.refs_18_), channel_id=1, source_target_pairs={{0,4},{4,8},{8,12},{12,0},{1,5},{5,9},{9,13},{13,1},{2,6},{6,10},{... | collective-permute-start | bytes 1671176 | tf_op jit(solution)/shard_map/ppermute | solution.py:167
  73.0 14.8 %collective-permute-start.14 = (f32[2,17,16,256]{3,2,1,0:T(8,128)S(1)}, f32[2,17,16,256]{3,2,1,0:T(8,128)S(1)}, u32[]{:S(2)}, u32[]{:S(2)}) collective-permute-start(f32[2,17,16,256]{3,2,1,0:T(8,128)S(1)} %collective-permute-done.6.refs_18_), channel_id=1, source_target_pairs={{0,12},{4,0},{8,4},{12,8},{1,13},{5,1},{9,5},{13,9},{2,14},{6,2},{... | collective-permute-start | bytes 1671176 | tf_op jit(solution)/shard_map/ppermute | solution.py:167
  75.7 12.1 %collective-permute-start.11 = (f32[256,512]{1,0:T(8,128)S(1)}, f32[256,512]{1,0:T(8,128)S(1)}, u32[]{:S(2)}, u32[]{:S(2)}) collective-permute-start(f32[256,512]{1,0:T(8,128)S(1)} %collective-permute-done.5.refs_5_), channel_id=1, source_target_pairs={{0,16},{16,32},{32,48},{48,0},{1,17},{17,33},{33,49},{49,1},{2,18}... | collective-permute-start | bytes 1572872 | tf_op jit(solution)/shard_map/ppermute | solution.py:167
  75.7 12.1 %collective-permute-start.12 = (f32[256,512]{1,0:T(8,128)S(1)}, f32[256,512]{1,0:T(8,128)S(1)}, u32[]{:S(2)}, u32[]{:S(2)}) collective-permute-start(f32[256,512]{1,0:T(8,128)S(1)} %collective-permute-done.5.refs_5_), channel_id=1, source_target_pairs={{0,48},{16,0},{32,16},{48,32},{1,49},{17,1},{33,17},{49,33},{2,50}... | collective-permute-start | bytes 1572872 | tf_op jit(solution)/shard_map/ppermute | solution.py:167
  79.8 26.0 %collective-permute-start.17 = (f32[5,256,256]{2,1,0:T(8,128)S(1)}, f32[5,256,256]{2,1,0:T(8,128)S(1)}, u32[]{:S(2)}, u32[]{:S(2)}) collective-permute-start(f32[5,256,256]{2,1,0:T(8,128)S(1)} %bitcast_dynamic-update-slice_fusion), channel_id=1, source_target_pairs={{0,1},{1,0},{2,3},{3,2},{4,5},{5,4},{6,7},{7,6},{8,9},{9,8},{10,11... | collective-permute-start | bytes 3932168 | tf_op jit(solution)/shard_map/ppermute | solution.py:162
  88.0 11.0 %collective-permute-start.16 = (f32[128,512]{1,0:T(8,128)S(1)}, f32[128,512]{1,0:T(8,128)S(1)}, u32[]{:S(2)}, u32[]{:S(2)}) collective-permute-start(f32[128,512]{1,0:T(8,128)S(1)} %slice.119), channel_id=1, source_target_pairs={{0,48},{16,0},{32,16},{48,32},{1,49},{17,1},{33,17},{49,33},{2,50}... | collective-permute-start | bytes 786440 | tf_op jit(solution)/shard_map/ppermute | solution.py:167
  92.1 13.7 %collective-permute-start.18 = (f32[2,256,256]{2,1,0:T(8,128)S(1)}, f32[2,256,256]{2,1,0:T(8,128)S(1)}, u32[]{:S(2)}, u32[]{:S(2)}) collective-permute-start(f32[2,256,256]{2,1,0:T(8,128)S(1)} %pad_maximum_fusion.4), channel_id=1, source_target_pairs={{0,1},{1,0},{2,3},{3,2},{4,5},{5,4},{6,7},{7,6},{8,9},{9,8},{10,11... | collective-permute-start | bytes 1572872 | tf_op jit(solution)/shard_map/ppermute | solution.py:162
  96.2 9.6 %collective-permute-start.20 = (f32[1,17,16,256]{3,2,1,0:T(8,128)S(1)}, f32[1,17,16,256]{3,2,1,0:T(8,128)S(1)}, u32[]{:S(2)}, u32[]{:S(2)}) collective-permute-start(f32[1,17,16,256]{3,2,1,0:T(8,128)S(1)} %slice.144), channel_id=1, source_target_pairs={{0,4},{4,8},{8,12},{12,0},{1,5},{5,9},{9,13},{13,1},{2,6},{6,10},{... | collective-permute-start | bytes 835592 | tf_op jit(solution)/shard_map/ppermute | solution.py:167
  96.3 9.4 %collective-permute-start.21 = (f32[1,17,16,256]{3,2,1,0:T(8,128)S(1)}, f32[1,17,16,256]{3,2,1,0:T(8,128)S(1)}, u32[]{:S(2)}, u32[]{:S(2)}) collective-permute-start(f32[1,17,16,256]{3,2,1,0:T(8,128)S(1)} %slice.145), channel_id=1, source_target_pairs={{0,12},{4,0},{8,4},{12,8},{1,13},{5,1},{9,5},{13,9},{2,14},{6,2},{... | collective-permute-start | bytes 835592 | tf_op jit(solution)/shard_map/ppermute | solution.py:167
  130.5 25.1 %all-to-all-start.3 = ((f32[16,80,256]{2,1,0:T(8,128)}), f32[16,80,256]{2,1,0:T(8,128)S(1)}, u32[]{:S(2)}, u32[]{:S(2)}) async-start(f32[16,80,256]{2,1,0:T(8,128)} %bitcast.93), calls=%async_computation.3 | async-start | bytes 2621440 | tf_op jit(solution)/shard_map/all_to_all | solution.py:154
  156.9 11.7 %all-to-all-start.5 = ((f32[8,64,256]{2,1,0:T(8,128)}), f32[8,64,256]{2,1,0:T(8,128)S(1)}, u32[]{:S(2)}, u32[]{:S(2)}) async-start(f32[8,64,256]{2,1,0:T(8,128)} %bitcast.67), calls=%async_computation.5 | async-start | bytes 1048576 | tf_op jit(solution)/shard_map/all_to_all | solution.py:154
  168.6 19.9 %all-to-all-start.4 = ((f32[16,48,256]{2,1,0:T(8,128)}), f32[16,48,256]{2,1,0:T(8,128)S(1)}, u32[]{:S(2)}, u32[]{:S(2)}) async-start(f32[16,48,256]{2,1,0:T(8,128)} %pad_maximum_fusion.2), calls=%async_computation.4 | async-start | bytes 1572864 | tf_op jit(solution)/shard_map/all_to_all | solution.py:154
  (9 other events, 70.5 us)

commit v6 on v5

--- a/solution.py
+++ b/solution.py
@@ -169,7 +169,8 @@
 
 def go_round(*ways):
     hold = lax.optimization_barrier
-    owns = hold([own for own, _, _ in ways])
+    first = swap(ways[0][0], ways[0][2])
+    owns, first = hold(([own for own, _, _ in ways], first))
     lines = [line for _, line, _ in ways]
 
     def both_ways(arrays):
@@ -182,7 +183,7 @@
             for (low, high), line, n in zip(pairs, lines, half)
         ]
 
-    beside = [swap(own, neighbour) for own, (_, _, neighbour) in zip(owns, ways)]
+    beside = [first, swap(owns[1], ways[1][2])]
     near = hold(both_ways(owns))
     across = onward(near)
     beside, across = hold((beside, across))
@@ -226,7 +227,7 @@
     away = pick(here, chip) != col
     flags = jnp.stack([away.astype(jnp.int32), (chip == row).astype(jnp.int32), chip, core])
     info = jnp.concatenate([pick(here, slot) % 2, flags, slot, places])
-    info, picks, anc, both = lax.optimization_barrier((info, picks, anc, both))
+    info, picks, both = lax.optimization_barrier((info, picks, both))
 
     inverse, lows = go_round((anc, RING, NEXT), (both, LINE, ACROSS))
 

time: 191 us -> 186 us (0.974)
  waiting for transfers between devices: 82.1 us -> 73.5 us
  starting transfers between devices: 62.2 us -> 68.2 us
  blocking collectives: 16.6 us -> 14.6 us
    ppermute x7, waiting for transfers between devices: 9.9 us -> 1.25 us  [swap(): return lax.ppermute(x, axis, [(0, 1), (1, 0)])]
    ppermute x7, starting transfers between devices: 10.3 us -> 15.7 us  [swap(): return lax.ppermute(x, axis, [(0, 1), (1, 0)])]
    all_to_all x1, blocking collectives: 16.6 us -> 14.6 us  [exchange(): return lax.all_to_all(x, axis, split_axis=0, concat_axis=0, tiled=True)]
  transfers between devices with their start and end apart: 28 -> 28, of which waited for: 10 -> 11; matrix products, arithmetic and copies ran while one was open for 7% -> 8% of each run, Pallas kernels for 0% -> 0%
where the time goes in v6:
time: 186 us
  waiting for transfers between devices  73.5 us (40%)
  starting transfers between devices  68.2 us (37%)
  blocking collectives  14.6 us (8%)
  other arithmetic  12.4 us (7%)
  local copies, waits for them, and re-layouts  8.37 us (4%)
  Pallas kernels  6.76 us (4%)
    all_to_all x5, waiting for transfers between devices, exchange(): return lax.all_to_all(x, axis, split_axis=0, concat_axis=0, tiled=True)  55.4 us
    all_to_all x5, starting transfers between devices, exchange(): return lax.all_to_all(x, axis, split_axis=0, concat_axis=0, tiled=True)  31.7 us
    ppermute x16, starting transfers between devices, shift(): return lax.ppermute(x, axis, [(i, (i + by) % n) for i in range(n)])  20.9 us
    ppermute x16, waiting for transfers between devices, shift(): return lax.ppermute(x, axis, [(i, (i + by) % n) for i in range(n)])  16.8 us
    ppermute x7, starting transfers between devices, swap(): return lax.ppermute(x, axis, [(0, 1), (1, 0)])  15.7 us
    all_to_all x1, blocking collectives, exchange(): return lax.all_to_all(x, axis, split_axis=0, concat_axis=0, tiled=True)  14.6 us
    pallas_call x1, Pallas kernels, level_blocks(): pl.pallas_call(kernel, grid_spec=grid_spec, out_shape=[jax.ShapeDtypeStru...  6.76 us
    gather x6, local copies, waits for them, and re-layouts, pick(): return x.at[index].get(mode='promise_in_bounds')  5.18 us
  transfers between devices with their start and end apart: 28, of which 11 were waited for; matrix products, arithmetic and copies ran while one was open for 8% of the time, Pallas kernels for 0%

profile of v6, /device:TPU:1, one launch (start us, length us, event | category | flops | bytes accessed | tf_op | source)
XLA Modules:
  0.0 185.6 jit_solution(7074273611327574630)
XLA Ops:
  0.7 2.1 %pad_maximum_fusion.1 = f32[16,48,256]{2,1,0:T(8,128)} fusion(f32[16,16,256]{2,1,0:T(8,128)} %bitcast.104, f32[16,16,256]{2,1,0:T(8,128)} %bitcast.105, f32[16,16,256]{2,1,0:T(8,128)} %bitcast.106), kind=kLoop, calls=%fused_computation.7 | loop fusion | flops 393216 | bytes 1572864 | tf_op jit(solution)/shard_map/concatenate | solution.py:209
  2.8 8.4 %all-to-all-start = ((f32[16,48,256]{2,1,0:T(8,128)}), f32[16,48,256]{2,1,0:T(8,128)S(1)}, u32[]{:S(2)}, u32[]{:S(2)}) async-start(f32[16,48,256]{2,1,0:T(8,128)} %pad_maximum_fusion.1), calls=%async_computation | async-start | bytes 1572864 | tf_op jit(solution)/shard_map/all_to_all | solution.py:154
  13.2 12.2 %all-to-all-done = f32[16,48,256]{2,1,0:T(8,128)S(1)} async-done(((f32[16,48,256]{2,1,0:T(8,128)}), f32[16,48,256]{2,1,0:T(8,128)S(1)}, u32[]{:S(2)}, u32[]{:S(2)}) %all-to-all-start) | async-done | bytes 786464 | tf_op jit(solution)/shard_map/all_to_all | solution.py:154
  26.8 6.6 %all-to-all-start.1 = ((f32[16,32,256]{2,1,0:T(8,128)}), f32[16,32,256]{2,1,0:T(8,128)S(1)}, u32[]{:S(2)}, u32[]{:S(2)}) async-start(f32[16,32,256]{2,1,0:T(8,128)} %bitcast.36), calls=%async_computation.1 | async-start | bytes 1048576 | tf_op jit(solution)/shard_map/all_to_all | solution.py:154
  36.3 6.9 %all-to-all-done.1 = f32[16,32,256]{2,1,0:T(8,128)S(1)} async-done(((f32[16,32,256]{2,1,0:T(8,128)}), f32[16,32,256]{2,1,0:T(8,128)S(1)}, u32[]{:S(2)}, u32[]{:S(2)}) %all-to-all-start.1) | async-done | bytes 524320 | tf_op jit(solution)/shard_map/all_to_all | solution.py:154
  43.3 2.7 %collective-permute-start.5 = (f32[2,17,16,256]{3,2,1,0:T(8,128)S(1)}, f32[2,17,16,256]{3,2,1,0:T(8,128)S(1)}, u32[]{:S(2)}, u32[]{:S(2)}) collective-permute-start(f32[2,17,16,256]{3,2,1,0:T(8,128)S(1)} %pad_maximum_fusion.3.refs_13_), channel_id=1, source_target_pairs={{0,12},{4,0},{8,4},{12,8},{1,13},{5,1},{9,5},{13,9},{2,14},{6,2},{... | collective-permute-start | bytes 1671176 | tf_op jit(solution)/shard_map/ppermute | solution.py:167
  46.0 2.7 %collective-permute-start.3 = (f32[256,512]{1,0:T(8,128)S(1)}, f32[256,512]{1,0:T(8,128)S(1)}, u32[]{:S(2)}, u32[]{:S(2)}) collective-permute-start(f32[256,512]{1,0:T(8,128)S(1)} %copy-done), channel_id=1, source_target_pairs={{0,48},{16,0},{32,16},{48,32},{1,49},{17,1},{33,17},{49,33},{2,50}... | collective-permute-start | bytes 1572872 | tf_op jit(solution)/shard_map/ppermute | solution.py:167
  51.9 7.0 %collective-permute-done.2.refs_1_ = f32[256,512]{1,0:T(8,128)S(1)} collective-permute-done((f32[256,512]{1,0:T(8,128)S(1)}, f32[256,512]{1,0:T(8,128)S(1)}, u32[]{:S(2)}, u32[]{:S(2)}) %collective-permute-start.2) | collective-permute-done | bytes 524320 | tf_op jit(solution)/shard_map/ppermute | solution.py:167
  61.5 1.9 %collective-permute-start.8 = (f32[128,512]{1,0:T(8,128)S(1)}, f32[128,512]{1,0:T(8,128)S(1)}, u32[]{:S(2)}, u32[]{:S(2)}) collective-permute-start(f32[128,512]{1,0:T(8,128)S(1)} %slice.115), channel_id=1, source_target_pairs={{0,48},{16,0},{32,16},{48,32},{1,49},{17,1},{33,17},{49,33},{2,50}... | collective-permute-start | bytes 786440 | tf_op jit(solution)/shard_map/ppermute | solution.py:167
  64.7 2.7 %collective-permute-done.7.refs_3_ = f32[128,512]{1,0:T(8,128)S(1)} collective-permute-done((f32[128,512]{1,0:T(8,128)S(1)}, f32[128,512]{1,0:T(8,128)S(1)}, u32[]{:S(2)}, u32[]{:S(2)}) %collective-permute-start.7) | collective-permute-done | bytes 262176 | tf_op jit(solution)/shard_map/ppermute | solution.py:167
  67.5 2.7 %collective-permute-start.14 = (f32[2,17,16,256]{3,2,1,0:T(8,128)S(1)}, f32[2,17,16,256]{3,2,1,0:T(8,128)S(1)}, u32[]{:S(2)}, u32[]{:S(2)}) collective-permute-start(f32[2,17,16,256]{3,2,1,0:T(8,128)S(1)} %collective-permute-done.6.refs_18_), channel_id=1, source_target_pairs={{0,12},{4,0},{8,4},{12,8},{1,13},{5,1},{9,5},{13,9},{2,14},{6,2},{... | collective-permute-start | bytes 1671176 | tf_op jit(solution)/shard_map/ppermute | solution.py:167
  74.3 5.3 %collective-permute-start.17 = (f32[5,256,256]{2,1,0:T(8,128)S(1)}, f32[5,256,256]{2,1,0:T(8,128)S(1)}, u32[]{:S(2)}, u32[]{:S(2)}) collective-permute-start(f32[5,256,256]{2,1,0:T(8,128)S(1)} %bitcast_dynamic-update-slice_fusion), channel_id=1, source_target_pairs={{0,1},{1,0},{2,3},{3,2},{4,5},{5,4},{6,7},{7,6},{8,9},{9,8},{10,11... | collective-permute-start | bytes 3932168 | tf_op jit(solution)/shard_map/ppermute | solution.py:162
  82.0 2.5 %collective-permute-start.16 = (f32[128,512]{1,0:T(8,128)S(1)}, f32[128,512]{1,0:T(8,128)S(1)}, u32[]{:S(2)}, u32[]{:S(2)}) collective-permute-start(f32[128,512]{1,0:T(8,128)S(1)} %slice.119), channel_id=1, source_target_pairs={{0,48},{16,0},{32,16},{48,32},{1,49},{17,1},{33,17},{49,33},{2,50}... | collective-permute-start | bytes 786440 | tf_op jit(solution)/shard_map/ppermute | solution.py:167
  85.9 6.6 %collective-permute-start.18 = (f32[2,256,256]{2,1,0:T(8,128)S(1)}, f32[2,256,256]{2,1,0:T(8,128)S(1)}, u32[]{:S(2)}, u32[]{:S(2)}) collective-permute-start(f32[2,256,256]{2,1,0:T(8,128)S(1)} %pad_maximum_fusion.4), channel_id=1, source_target_pairs={{0,1},{1,0},{2,3},{3,2},{4,5},{5,4},{6,7},{7,6},{8,9},{9,8},{10,11... | collective-permute-start | bytes 1572872 | tf_op jit(solution)/shard_map/ppermute | solution.py:162
  92.6 2.7 %collective-permute-start.21 = (f32[1,17,16,256]{3,2,1,0:T(8,128)S(1)}, f32[1,17,16,256]{3,2,1,0:T(8,128)S(1)}, u32[]{:S(2)}, u32[]{:S(2)}) collective-permute-start(f32[1,17,16,256]{3,2,1,0:T(8,128)S(1)} %slice.145), channel_id=1, source_target_pairs={{0,12},{4,0},{8,4},{12,8},{1,13},{5,1},{9,5},{13,9},{2,14},{6,2},{... | collective-permute-start | bytes 835592 | tf_op jit(solution)/shard_map/ppermute | solution.py:167
  97.0 5.1 %collective-permute-done.20.refs_21_ = f32[1,17,16,256]{3,2,1,0:T(8,128)S(1)} collective-permute-done((f32[1,17,16,256]{3,2,1,0:T(8,128)S(1)}, f32[1,17,16,256]{3,2,1,0:T(8,128)S(1)}, u32[]{:S(2)}, u32[]{:S(2)}) %collective-permute-start.20) | collective-permute-done | bytes 278560 | tf_op jit(solution)/shard_map/ppermute | solution.py:167
  102.1 6.8 %shard_map.119 = (f32[1,256,256]{2,1,0:T(8,128)S(1)}, f32[1,256,256]{2,1,0:T(8,128)S(1)}, f32[8,2,32,256]{3,2,1,0:T(8,128)S(1)}, f32[8,96,256]{2,1,0:T(8,128)S(1)}) custom-call(s32[28]{0:T(128)S(1)} %concatenate.63.info, f32[256,512]{1,0:T(8,128)S(1)} %copy-done, f32[256,512]{1,0:T(8,128)S(1)} %collective-permute-done.2.refs_1_, ...), custom_call_target="tpu_custom_call" | custom-call | flops 10000000000 | bytes 12000000 | tf_op jit(solution)/shard_map/pallas_call | solution.py:139
  108.8 14.6 %all_to_all.30 = f32[8,96,256]{2,1,0:T(8,128)S(1)} all-to-all(f32[8,96,256]{2,1,0:T(8,128)S(1)} %get-tuple-element.51), channel_id=1, replica_groups=mesh['next'=2,'ring'=4,'x'=4,'across'=2,'core'=2] {'x','across'}, dimensions={0} | all-to-all | bytes 1572864 | tf_op jit(solution)/shard_map/all_to_all | solution.py:154
  124.8 7.4 %all-to-all-start.3 = ((f32[16,80,256]{2,1,0:T(8,128)}), f32[16,80,256]{2,1,0:T(8,128)S(1)}, u32[]{:S(2)}, u32[]{:S(2)}) async-start(f32[16,80,256]{2,1,0:T(8,128)} %bitcast.61), calls=%async_computation.3 | async-start | bytes 2621440 | tf_op jit(solution)/shard_map/all_to_all | solution.py:154
  132.2 18.7 %all-to-all-done.3 = f32[16,80,256]{2,1,0:T(8,128)S(1)} async-done(((f32[16,80,256]{2,1,0:T(8,128)}), f32[16,80,256]{2,1,0:T(8,128)S(1)}, u32[]{:S(2)}, u32[]{:S(2)}) %all-to-all-start.3) | async-done | bytes 1310752 | tf_op jit(solution)/shard_map/all_to_all | solution.py:154
  152.4 3.6 %all-to-all-start.5 = ((f32[8,64,256]{2,1,0:T(8,128)}), f32[8,64,256]{2,1,0:T(8,128)S(1)}, u32[]{:S(2)}, u32[]{:S(2)}) async-start(f32[8,64,256]{2,1,0:T(8,128)} %bitcast.67), calls=%async_computation.5 | async-start | bytes 1048576 | tf_op jit(solution)/shard_map/all_to_all | solution.py:154
  157.6 6.5 %all-to-all-done.5 = f32[8,64,256]{2,1,0:T(8,128)S(1)} async-done(((f32[8,64,256]{2,1,0:T(8,128)}), f32[8,64,256]{2,1,0:T(8,128)S(1)}, u32[]{:S(2)}, u32[]{:S(2)}) %all-to-all-start.5) | async-done | bytes 524320 | tf_op jit(solution)/shard_map/all_to_all | solution.py:154
  164.1 5.7 %all-to-all-start.4 = ((f32[16,48,256]{2,1,0:T(8,128)}), f32[16,48,256]{2,1,0:T(8,128)S(1)}, u32[]{:S(2)}, u32[]{:S(2)}) async-start(f32[16,48,256]{2,1,0:T(8,128)} %pad_maximum_fusion.2), calls=%async_computation.4 | async-start | bytes 1572864 | tf_op jit(solution)/shard_map/all_to_all | solution.py:154
  172.9 11.1 %all-to-all-done.4 = f32[16,48,256]{2,1,0:T(8,128)S(1)} async-done(((f32[16,48,256]{2,1,0:T(8,128)}), f32[16,48,256]{2,1,0:T(8,128)S(1)}, u32[]{:S(2)}, u32[]{:S(2)}) %all-to-all-start.4) | async-done | bytes 786464 | tf_op jit(solution)/shard_map/all_to_all | solution.py:154
  (108 shorter events, 31.6 us)
Async XLA Ops:
  2.8 22.6 %all-to-all-start = ((f32[16,48,256]{2,1,0:T(8,128)}), f32[16,48,256]{2,1,0:T(8,128)S(1)}, u32[]{:S(2)}, u32[]{:S(2)}) async-start(f32[16,48,256]{2,1,0:T(8,128)} %pad_maximum_fusion.1), calls=%async_computation | async-start | bytes 1572864 | tf_op jit(solution)/shard_map/all_to_all | solution.py:154
  11.2 32.0 %collective-permute-start.1 = (f32[256,512]{1,0:T(8,128)S(1)}, f32[256,512]{1,0:T(8,128)S(1)}, u32[]{:S(2)}, u32[]{:S(2)}) collective-permute-start(f32[256,512]{1,0:T(8,128)S(1)} %copy-done), channel_id=1, source_target_pairs={{0,64},{64,0},{1,65},{65,1},{2,66},{66,2},{3,67},{67,3},{4,68},{68... | collective-permute-start | bytes 1572872 | tf_op jit(solution)/shard_map/ppermute | solution.py:162
  26.8 16.4 %all-to-all-start.1 = ((f32[16,32,256]{2,1,0:T(8,128)}), f32[16,32,256]{2,1,0:T(8,128)S(1)}, u32[]{:S(2)}, u32[]{:S(2)}) async-start(f32[16,32,256]{2,1,0:T(8,128)} %bitcast.36), calls=%async_computation.1 | async-start | bytes 1048576 | tf_op jit(solution)/shard_map/all_to_all | solution.py:154
  43.2 15.7 %collective-permute-start.4 = (f32[2,17,16,256]{3,2,1,0:T(8,128)S(1)}, f32[2,17,16,256]{3,2,1,0:T(8,128)S(1)}, u32[]{:S(2)}, u32[]{:S(2)}) collective-permute-start(f32[2,17,16,256]{3,2,1,0:T(8,128)S(1)} %pad_maximum_fusion.3.refs_13_), channel_id=1, source_target_pairs={{0,4},{4,8},{8,12},{12,0},{1,5},{5,9},{9,13},{13,1},{2,6},{6,10},{... | collective-permute-start | bytes 1671176 | tf_op jit(solution)/shard_map/ppermute | solution.py:167
  43.3 15.6 %collective-permute-start.5 = (f32[2,17,16,256]{3,2,1,0:T(8,128)S(1)}, f32[2,17,16,256]{3,2,1,0:T(8,128)S(1)}, u32[]{:S(2)}, u32[]{:S(2)}) collective-permute-start(f32[2,17,16,256]{3,2,1,0:T(8,128)S(1)} %pad_maximum_fusion.3.refs_13_), channel_id=1, source_target_pairs={{0,12},{4,0},{8,4},{12,8},{1,13},{5,1},{9,5},{13,9},{2,14},{6,2},{... | collective-permute-start | bytes 1671176 | tf_op jit(solution)/shard_map/ppermute | solution.py:167
  46.0 12.9 %collective-permute-start.2 = (f32[256,512]{1,0:T(8,128)S(1)}, f32[256,512]{1,0:T(8,128)S(1)}, u32[]{:S(2)}, u32[]{:S(2)}) collective-permute-start(f32[256,512]{1,0:T(8,128)S(1)} %copy-done), channel_id=1, source_target_pairs={{0,16},{16,32},{32,48},{48,0},{1,17},{17,33},{33,49},{49,1},{2,18}... | collective-permute-start | bytes 1572872 | tf_op jit(solution)/shard_map/ppermute | solution.py:167
  46.0 12.9 %collective-permute-start.3 = (f32[256,512]{1,0:T(8,128)S(1)}, f32[256,512]{1,0:T(8,128)S(1)}, u32[]{:S(2)}, u32[]{:S(2)}) collective-permute-start(f32[256,512]{1,0:T(8,128)S(1)} %copy-done), channel_id=1, source_target_pairs={{0,48},{16,0},{32,16},{48,32},{1,49},{17,1},{33,17},{49,33},{2,50}... | collective-permute-start | bytes 1572872 | tf_op jit(solution)/shard_map/ppermute | solution.py:167
  48.7 16.0 %collective-permute-start.6 = (f32[2,17,16,256]{3,2,1,0:T(8,128)S(1)}, f32[2,17,16,256]{3,2,1,0:T(8,128)S(1)}, u32[]{:S(2)}, u32[]{:S(2)}) collective-permute-start(f32[2,17,16,256]{3,2,1,0:T(8,128)S(1)} %pad_maximum_fusion.3.refs_13_), channel_id=1, source_target_pairs={{0,2},{2,0},{1,3},{3,1},{4,6},{6,4},{5,7},{7,5},{8,10},{10,8},{9,1... | collective-permute-start | bytes 1671176 | tf_op jit(solution)/shard_map/ppermute | solution.py:162
  58.9 8.5 %collective-permute-start.10 = (f32[1,17,16,256]{3,2,1,0:T(8,128)S(1)}, f32[1,17,16,256]{3,2,1,0:T(8,128)S(1)}, u32[]{:S(2)}, u32[]{:S(2)}) collective-permute-start(f32[1,17,16,256]{3,2,1,0:T(8,128)S(1)} %slice.117), channel_id=1, source_target_pairs={{0,12},{4,0},{8,4},{12,8},{1,13},{5,1},{9,5},{13,9},{2,14},{6,2},{... | collective-permute-start | bytes 835592 | tf_op jit(solution)/shard_map/ppermute | solution.py:167
  60.0 7.4 %collective-permute-start.9 = (f32[1,17,16,256]{3,2,1,0:T(8,128)S(1)}, f32[1,17,16,256]{3,2,1,0:T(8,128)S(1)}, u32[]{:S(2)}, u32[]{:S(2)}) collective-permute-start(f32[1,17,16,256]{3,2,1,0:T(8,128)S(1)} %slice.116), channel_id=1, source_target_pairs={{0,4},{4,8},{8,12},{12,0},{1,5},{5,9},{9,13},{13,1},{2,6},{6,10},{... | collective-permute-start | bytes 835592 | tf_op jit(solution)/shard_map/ppermute | solution.py:167
  60.6 6.8 %collective-permute-start.7 = (f32[128,512]{1,0:T(8,128)S(1)}, f32[128,512]{1,0:T(8,128)S(1)}, u32[]{:S(2)}, u32[]{:S(2)}) collective-permute-start(f32[128,512]{1,0:T(8,128)S(1)} %slice.114), channel_id=1, source_target_pairs={{0,16},{16,32},{32,48},{48,0},{1,17},{17,33},{33,49},{49,1},{2,18}... | collective-permute-start | bytes 786440 | tf_op jit(solution)/shard_map/ppermute | solution.py:167
  67.4 14.2 %collective-permute-start.13 = (f32[2,17,16,256]{3,2,1,0:T(8,128)S(1)}, f32[2,17,16,256]{3,2,1,0:T(8,128)S(1)}, u32[]{:S(2)}, u32[]{:S(2)}) collective-permute-start(f32[2,17,16,256]{3,2,1,0:T(8,128)S(1)} %collective-permute-done.6.refs_18_), channel_id=1, source_target_pairs={{0,4},{4,8},{8,12},{12,0},{1,5},{5,9},{9,13},{13,1},{2,6},{6,10},{... | collective-permute-start | bytes 1671176 | tf_op jit(solution)/shard_map/ppermute | solution.py:167
  67.5 14.1 %collective-permute-start.14 = (f32[2,17,16,256]{3,2,1,0:T(8,128)S(1)}, f32[2,17,16,256]{3,2,1,0:T(8,128)S(1)}, u32[]{:S(2)}, u32[]{:S(2)}) collective-permute-start(f32[2,17,16,256]{3,2,1,0:T(8,128)S(1)} %collective-permute-done.6.refs_18_), channel_id=1, source_target_pairs={{0,12},{4,0},{8,4},{12,8},{1,13},{5,1},{9,5},{13,9},{2,14},{6,2},{... | collective-permute-start | bytes 1671176 | tf_op jit(solution)/shard_map/ppermute | solution.py:167
  70.1 10.0 %collective-permute-start.11 = (f32[256,512]{1,0:T(8,128)S(1)}, f32[256,512]{1,0:T(8,128)S(1)}, u32[]{:S(2)}, u32[]{:S(2)}) collective-permute-start(f32[256,512]{1,0:T(8,128)S(1)} %collective-permute-done.1.refs_5_), channel_id=1, source_target_pairs={{0,16},{16,32},{32,48},{48,0},{1,17},{17,33},{33,49},{49,1},{2,18}... | collective-permute-start | bytes 1572872 | tf_op jit(solution)/shard_map/ppermute | solution.py:167
  72.0 9.5 %collective-permute-start.12 = (f32[256,512]{1,0:T(8,128)S(1)}, f32[256,512]{1,0:T(8,128)S(1)}, u32[]{:S(2)}, u32[]{:S(2)}) collective-permute-start(f32[256,512]{1,0:T(8,128)S(1)} %collective-permute-done.1.refs_5_), channel_id=1, source_target_pairs={{0,48},{16,0},{32,16},{48,32},{1,49},{17,1},{33,17},{49,33},{2,50}... | collective-permute-start | bytes 1572872 | tf_op jit(solution)/shard_map/ppermute | solution.py:167
  74.3 27.8 %collective-permute-start.17 = (f32[5,256,256]{2,1,0:T(8,128)S(1)}, f32[5,256,256]{2,1,0:T(8,128)S(1)}, u32[]{:S(2)}, u32[]{:S(2)}) collective-permute-start(f32[5,256,256]{2,1,0:T(8,128)S(1)} %bitcast_dynamic-update-slice_fusion), channel_id=1, source_target_pairs={{0,1},{1,0},{2,3},{3,2},{4,5},{5,4},{6,7},{7,6},{8,9},{9,8},{10,11... | collective-permute-start | bytes 3932168 | tf_op jit(solution)/shard_map/ppermute | solution.py:162
  81.6 11.0 %collective-permute-start.15 = (f32[128,512]{1,0:T(8,128)S(1)}, f32[128,512]{1,0:T(8,128)S(1)}, u32[]{:S(2)}, u32[]{:S(2)}) collective-permute-start(f32[128,512]{1,0:T(8,128)S(1)} %slice.118), channel_id=1, source_target_pairs={{0,16},{16,32},{32,48},{48,0},{1,17},{17,33},{33,49},{49,1},{2,18}... | collective-permute-start | bytes 786440 | tf_op jit(solution)/shard_map/ppermute | solution.py:167
  82.0 13.4 %collective-permute-start.16 = (f32[128,512]{1,0:T(8,128)S(1)}, f32[128,512]{1,0:T(8,128)S(1)}, u32[]{:S(2)}, u32[]{:S(2)}) collective-permute-start(f32[128,512]{1,0:T(8,128)S(1)} %slice.119), channel_id=1, source_target_pairs={{0,48},{16,0},{32,16},{48,32},{1,49},{17,1},{33,17},{49,33},{2,50}... | collective-permute-start | bytes 786440 | tf_op jit(solution)/shard_map/ppermute | solution.py:167
  85.9 16.2 %collective-permute-start.18 = (f32[2,256,256]{2,1,0:T(8,128)S(1)}, f32[2,256,256]{2,1,0:T(8,128)S(1)}, u32[]{:S(2)}, u32[]{:S(2)}) collective-permute-start(f32[2,256,256]{2,1,0:T(8,128)S(1)} %pad_maximum_fusion.4), channel_id=1, source_target_pairs={{0,1},{1,0},{2,3},{3,2},{4,5},{5,4},{6,7},{7,6},{8,9},{9,8},{10,11... | collective-permute-start | bytes 1572872 | tf_op jit(solution)/shard_map/ppermute | solution.py:162
  92.5 9.6 %collective-permute-start.20 = (f32[1,17,16,256]{3,2,1,0:T(8,128)S(1)}, f32[1,17,16,256]{3,2,1,0:T(8,128)S(1)}, u32[]{:S(2)}, u32[]{:S(2)}) collective-permute-start(f32[1,17,16,256]{3,2,1,0:T(8,128)S(1)} %slice.144), channel_id=1, source_target_pairs={{0,4},{4,8},{8,12},{12,0},{1,5},{5,9},{9,13},{13,1},{2,6},{6,10},{... | collective-permute-start | bytes 835592 | tf_op jit(solution)/shard_map/ppermute | solution.py:167
  92.6 9.4 %collective-permute-start.21 = (f32[1,17,16,256]{3,2,1,0:T(8,128)S(1)}, f32[1,17,16,256]{3,2,1,0:T(8,128)S(1)}, u32[]{:S(2)}, u32[]{:S(2)}) collective-permute-start(f32[1,17,16,256]{3,2,1,0:T(8,128)S(1)} %slice.145), channel_id=1, source_target_pairs={{0,12},{4,0},{8,4},{12,8},{1,13},{5,1},{9,5},{13,9},{2,14},{6,2},{... | collective-permute-start | bytes 835592 | tf_op jit(solution)/shard_map/ppermute | solution.py:167
  124.8 26.2 %all-to-all-start.3 = ((f32[16,80,256]{2,1,0:T(8,128)}), f32[16,80,256]{2,1,0:T(8,128)S(1)}, u32[]{:S(2)}, u32[]{:S(2)}) async-start(f32[16,80,256]{2,1,0:T(8,128)} %bitcast.61), calls=%async_computation.3 | async-start | bytes 2621440 | tf_op jit(solution)/shard_map/all_to_all | solution.py:154
  152.4 11.7 %all-to-all-start.5 = ((f32[8,64,256]{2,1,0:T(8,128)}), f32[8,64,256]{2,1,0:T(8,128)S(1)}, u32[]{:S(2)}, u32[]{:S(2)}) async-start(f32[8,64,256]{2,1,0:T(8,128)} %bitcast.67), calls=%async_computation.5 | async-start | bytes 1048576 | tf_op jit(solution)/shard_map/all_to_all | solution.py:154
  164.1 19.9 %all-to-all-start.4 = ((f32[16,48,256]{2,1,0:T(8,128)}), f32[16,48,256]{2,1,0:T(8,128)S(1)}, u32[]{:S(2)}, u32[]{:S(2)}) async-start(f32[16,48,256]{2,1,0:T(8,128)} %pad_maximum_fusion.2), calls=%async_computation.4 | async-start | bytes 1572864 | tf_op jit(solution)/shard_map/all_to_all | solution.py:154
  (9 other events, 70.5 us)
